TPU v7x, 128 devices: a whole 4x4x4 slice. The times are simulated.
128 devices in a mesh: tile: 32 (over y, z, core), batch: 4 (over x).
Axes of the slice: x: 4, y: 4, z: 4, core: 2. Of those that a mesh axis runs over, the one named last changes fastest.
Arguments:
- states: bfloat16 [4, 256, 16, 16, 256], P('batch', 'tile'), may hold values from -6 to 6
- cotangent: bfloat16 [4, 256, 16, 16, 256], P('batch', 'tile'), may hold values from -6 to 6
- beside_slot: int32 [256, 8], replicated, may hold values from 0 to 255, as said below
- beside_code: int32 [256, 8], replicated, may hold values from 0 to 7
- mixers: bfloat16 [2, 256, 256], replicated, may hold values from -0.375 to 0.375
- stencils: float32 [2, 9, 256], replicated, may hold values from -2 to 2
- shifts: float32 [2, 256], replicated, may hold values from -3 to 3
Outputs:
- outcome: bfloat16 [4, 256, 16, 16, 256], P('batch', 'tile')
- state_grad: bfloat16 [4, 256, 16, 16, 256], P('batch', 'tile')
- mixer_grads: float32 [2, 256, 256], replicated
- stencil_grads: float32 [2, 9, 256], replicated
- shift_grads: float32 [2, 256], replicated
Inputs may be any that keep to these rules, and one draw needn't show every extreme that they name: `beside_slot`: tiles are numbered by slot; the tiles of one aligned block of 8 slots have 8 * 8 entries, of which at most 2 name slots of any one other block, and in every block exactly 2 entries name one other block; how many entries of a block name other blocks varies from block to block.
All inputs are finite; a program needn't handle non-finite values.
Results may differ from a plain program's by a relative error of at most 0.009.
Values may be sent and summed in bfloat16 or wider, within the bound.
No kernel may reach another device: no remote copies, remote signals or barrier semaphores. Data moves between devices by JAX's collectives and lax.ppermute only.
A program may use at most 128 MiB of HBM per device.

v0:
```python
import math

import jax
import jax.numpy as jnp
from jax import lax
from jax.sharding import Mesh
from jax.sharding import PartitionSpec as P

CAP = 2
TILE = ("tile_0", "tile_1", "tile_2")


SQRT_HALF = 0.7071067811865476
INV_ROOT_TAU = 0.3989422804014327


def filled_up(lines, count):
    spare = -len(lines) % count
    return jnp.pad(lines, [(0, spare)] + [(0, 0)] * (lines.ndim - 1))


def copy_for_each(array, axis):
    copies = jnp.broadcast_to(array, (lax.axis_size(axis), *array.shape))
    return lax.all_to_all(copies, axis, split_axis=0, concat_axis=0, tiled=True)


def laid_out(parts, dim):
    dims = list(parts.shape[1:])
    dims[dim] *= parts.shape[0]
    return jnp.moveaxis(parts, 0, dim).reshape(dims)


def gathered_by_axis(array, axes, dim):
    far, near = axes
    parts = copy_for_each(copy_for_each(array, far), near)
    return laid_out(parts.swapaxes(0, 1).reshape(-1, *array.shape), dim)


def cut_along(array, dim, count):
    before, after = (array.shape[:dim], array.shape[dim + 1 :])
    return jnp.moveaxis(array.reshape(*before, count, -1, *after), dim, 0)


def sent_and_summed(array, axis, dim):
    parts = cut_along(array, dim, lax.axis_size(axis))
    arrived = lax.all_to_all(parts, axis, split_axis=0, concat_axis=0, tiled=True)
    return arrived.sum(axis=0)


def sum_by_axis(array, axes, dim):
    far, near = axes
    own = sent_and_summed(cut_along(array, dim, lax.axis_size(far)), near, dim + 1)
    return jnp.sum(lax.all_to_all(own, far, 0, 0, tiled=True), axis=0)


def nested_sum(array, axes):
    padded = filled_up(array, lax.axis_size(axes[0]) * lax.axis_size(axes[1]))
    whole = gathered_by_axis(sum_by_axis(padded, axes, 0), axes, 0)
    return lax.slice_in_dim(whole, 0, len(array)).reshape(array.shape)


def in_one(arrays, axis):
    flat, at, gathered = (jnp.concatenate([a.reshape(-1) for a in arrays]), 0, [])
    running = nested_sum(flat, axis)
    for a in arrays:
        gathered.append(running[at : at + a.size].reshape(a.shape))
        at += a.size
    return tuple(gathered)


def gelu_exact(value):
    return 0.5 * value * (1.0 + lax.erf(value * SQRT_HALF))


def gelu_slope(value):
    return (
        0.5 * (1.0 + lax.erf(value * SQRT_HALF))
        + value * jnp.exp(-0.5 * value * value) * INV_ROOT_TAU
    )


def rim_rows(field):
    return jnp.stack(
        [field[:, :, 0], field[:, :, :, -1], field[:, :, -1], field[:, :, :, 0]], axis=2
    )


def assemble(field, panels, flip_bits):
    turned = jnp.where(flip_bits[None, :, :, None, None] == 1, panels[:, :, :, ::-1], panels)
    corners = turned[:, :, 4:, 0]
    top_row = jnp.concatenate([corners[:, :, 3:4], turned[:, :, 0], corners[:, :, 0:1]], axis=2)
    bottom = jnp.concatenate([corners[:, :, 2:3], turned[:, :, 2], corners[:, :, 1:2]], axis=2)
    middle = jnp.concatenate(
        [turned[:, :, 3][:, :, :, None], field, turned[:, :, 1][:, :, :, None]], axis=3
    )
    return jnp.concatenate([top_row[:, :, None], middle, bottom[:, :, None]], axis=2)


def stencil_apply(padded, kernel):
    side_len = padded.shape[2] - 2
    running = jnp.zeros(padded.shape[:2] + (side_len, side_len, padded.shape[4]), jnp.float32)
    for row_at in range(3):
        for col_at in range(3):
            window = padded[:, :, row_at : row_at + side_len, col_at : col_at + side_len]
            running = running + kernel[3 * row_at + col_at] * window.astype(jnp.float32)
    return running


def stencil_back(grad, kernel):
    widened = grad.astype(jnp.float32)
    running = jnp.zeros(
        grad.shape[:2] + (grad.shape[2] + 2, grad.shape[3] + 2, grad.shape[4]), jnp.float32
    )
    for row_at in range(3):
        for col_at in range(3):
            running = running + jnp.pad(
                kernel[3 * row_at + col_at] * widened,
                ((0, 0), (0, 0), (row_at, 2 - row_at), (col_at, 2 - col_at), (0, 0)),
            )
    return running


def stencil_grad(grad, padded):
    side_len = grad.shape[2]
    widened = grad.astype(jnp.float32)
    terms = []
    for row_at in range(3):
        for col_at in range(3):
            window = padded[:, :, row_at : row_at + side_len, col_at : col_at + side_len].astype(
                jnp.float32
            )
            terms.append(jnp.sum(widened * window, axis=(0, 1, 2, 3)))
    return jnp.stack(terms)


def halo_parts(padded_grad, flip_bits):
    side_len = padded_grad.shape[2] - 2
    side_parts = jnp.stack(
        [
            padded_grad[:, :, 0, 1:-1],
            padded_grad[:, :, 1:-1, -1],
            padded_grad[:, :, -1, 1:-1],
            padded_grad[:, :, 1:-1, 0],
        ],
        axis=2,
    )
    corner_vals = jnp.stack(
        [
            padded_grad[:, :, 0, -1],
            padded_grad[:, :, -1, -1],
            padded_grad[:, :, -1, 0],
            padded_grad[:, :, 0, 0],
        ],
        axis=2,
    )
    flip_wide = flip_bits[None, :, :, None, None]
    side_parts = jnp.where(flip_wide[:, :, :4] == 1, side_parts[:, :, :, ::-1], side_parts)
    positions = jnp.arange(side_len)
    first_spot = (positions == 0).astype(jnp.float32)[:, None]
    last_spot = (positions == side_len - 1).astype(jnp.float32)[:, None]
    corner_spot = jnp.where(flip_wide[:, :, 4:] == 1, last_spot, first_spot)
    return jnp.concatenate([side_parts, corner_spot * corner_vals[:, :, :, None]], axis=2)


def add_rims(inner, rim_grad):
    inner = inner.at[:, :, 0].add(rim_grad[:, :, 0])
    inner = inner.at[:, :, :, -1].add(rim_grad[:, :, 1])
    inner = inner.at[:, :, -1].add(rim_grad[:, :, 2])
    inner = inner.at[:, :, :, 0].add(rim_grad[:, :, 3])
    return inner


def block_pass(
    states, cotangent, panel_fetch, send_back, flip_bits, mixers, stencils, shifts, early
):
    shape = states.shape
    channels = shape[4]
    padded_in = assemble(states, panel_fetch(states), flip_bits)
    conv_first = stencil_apply(padded_in, stencils[0]).astype(jnp.bfloat16)
    flat_first = conv_first.reshape(-1, channels)
    hidden = jnp.dot(flat_first, mixers[0], preferred_element_type=jnp.float32) + shifts[0]
    active = gelu_exact(hidden).astype(jnp.bfloat16).reshape(shape)
    padded_mid = assemble(active, panel_fetch(active), flip_bits)
    conv_second = stencil_apply(padded_mid, stencils[1]).astype(jnp.bfloat16)
    flat_second = conv_second.reshape(-1, channels)
    outcome = (
        states.reshape(-1, channels).astype(jnp.float32)
        + jnp.dot(flat_second, mixers[1], preferred_element_type=jnp.float32)
        + shifts[1]
    ).astype(jnp.bfloat16)
    upstream = cotangent.reshape(-1, channels)
    mixer_second = lax.dot_general(
        flat_second, upstream, (((0,), (0,)), ((), ())), preferred_element_type=jnp.float32
    )
    shift_second = jnp.sum(upstream.astype(jnp.float32), axis=0)
    grad_second = (
        lax.dot_general(
            upstream, mixers[1], (((1,), (1,)), ((), ())), preferred_element_type=jnp.float32
        )
        .astype(jnp.bfloat16)
        .reshape(shape)
    )
    stencil_second = stencil_grad(grad_second, padded_mid)
    later = early((mixer_second, stencil_second, shift_second))
    grad_active = send_back(stencil_back(grad_second, stencils[1]))
    grad_hidden = (grad_active.reshape(-1, channels) * gelu_slope(hidden)).astype(jnp.bfloat16)
    mixer_first = lax.dot_general(
        flat_first, grad_hidden, (((0,), (0,)), ((), ())), preferred_element_type=jnp.float32
    )
    shift_first = jnp.sum(grad_hidden.astype(jnp.float32), axis=0)
    grad_conv = (
        lax.dot_general(
            grad_hidden, mixers[0], (((1,), (1,)), ((), ())), preferred_element_type=jnp.float32
        )
        .astype(jnp.bfloat16)
        .reshape(shape)
    )
    stencil_first = stencil_grad(grad_conv, padded_in)
    state_grad = (
        cotangent.astype(jnp.float32) + send_back(stencil_back(grad_conv, stencils[0]))
    ).astype(jnp.bfloat16)
    return (outcome.reshape(shape), state_grad, (mixer_first, stencil_first, shift_first), later)


def shards(states, cotangent, beside_slot, beside_code, mixers, stencils, shifts):
    samples = states.shape[0]
    tile_count = states.shape[1]
    side_len = states.shape[2]
    channels = states.shape[4]
    groups = lax.axis_size(TILE)
    own_index = lax.axis_index(TILE)
    entries = tile_count * 8
    owner_all = (beside_slot // tile_count).reshape(groups, entries)
    source_all = (beside_slot % tile_count * 4 + beside_code // 2).reshape(groups, entries)
    peer_ids = jnp.arange(groups, dtype=jnp.int32)
    entry_ids = jnp.arange(entries, dtype=jnp.int32)
    remote_all = owner_all != peer_ids[:, None]
    earlier = (owner_all[:, :, None] == owner_all[:, None, :]) & (
        entry_ids[None, None, :] < entry_ids[None, :, None]
    )
    place_all = jnp.sum(earlier.astype(jnp.int32), axis=2)
    wanted = remote_all & (owner_all == own_index)
    slot_ids = jnp.arange(CAP, dtype=jnp.int32)
    chosen = wanted[:, None, :] & (place_all[:, None, :] == slot_ids[None, :, None])
    send_rim = jnp.sum(jnp.where(chosen, source_all[:, None, :], 0), axis=2).reshape(-1)
    send_live = jnp.any(chosen, axis=2).reshape(-1)
    own_owner = lax.dynamic_index_in_dim(owner_all, own_index, 0, keepdims=False)
    own_place = lax.dynamic_index_in_dim(place_all, own_index, 0, keepdims=False)
    own_source = lax.dynamic_index_in_dim(source_all, own_index, 0, keepdims=False)
    own_remote = own_owner != own_index
    from_peer = jnp.where(own_remote, own_owner * CAP + own_place, 0)
    flip_bits = lax.dynamic_slice_in_dim(beside_code % 2, own_index * tile_count, tile_count, 0)
    mail_ids = jnp.arange(groups * CAP, dtype=jnp.int32)
    mail_match = own_remote[None, :] & (from_peer[None, :] == mail_ids[:, None])
    mail_entry = jnp.sum(jnp.where(mail_match, entry_ids[None, :], 0), axis=1)
    mail_live = jnp.any(mail_match, axis=1)

    def panel_fetch(field):
        rims = rim_rows(field).reshape(samples, tile_count * 4, side_len, channels)
        outgoing = jnp.where(
            send_live[None, :, None, None],
            jnp.take(rims, send_rim, axis=1),
            jnp.zeros((), jnp.bfloat16),
        )
        incoming = lax.all_to_all(
            outgoing.reshape(samples, groups, CAP, side_len, channels),
            TILE,
            split_axis=1,
            concat_axis=1,
            tiled=True,
        )
        incoming = incoming.reshape(samples, groups * CAP, side_len, channels)
        panels = jnp.where(
            own_remote[None, :, None, None],
            jnp.take(incoming, from_peer, axis=1),
            jnp.take(rims, own_source, axis=1),
        )
        return panels.reshape(samples, tile_count, 8, side_len, channels)

    def send_back(padded_grad):
        parts = halo_parts(padded_grad, flip_bits).reshape(samples, entries, side_len, channels)
        outgoing = jnp.where(
            mail_live[None, :, None, None],
            jnp.take(parts, mail_entry, axis=1),
            jnp.zeros((), jnp.float32),
        )
        incoming = lax.all_to_all(
            outgoing.reshape(samples, groups, CAP, side_len, channels),
            TILE,
            split_axis=1,
            concat_axis=1,
            tiled=True,
        )
        incoming = incoming.reshape(samples, groups * CAP, side_len, channels)
        kept_parts = jnp.where(own_remote[None, :, None, None], jnp.zeros((), jnp.float32), parts)
        returned = jnp.where(send_live[None, :, None, None], incoming, jnp.zeros((), jnp.float32))
        rim_grad = jnp.zeros((samples, tile_count * 4, side_len, channels), jnp.float32)
        rim_grad = rim_grad.at[:, own_source].add(kept_parts)
        rim_grad = rim_grad.at[:, send_rim].add(returned)
        return add_rims(
            padded_grad[:, :, 1:-1, 1:-1],
            rim_grad.reshape(samples, tile_count, 4, side_len, channels),
        )

    def early(group):
        return group

    outcome, state_grad, first, second = block_pass(
        states, cotangent, panel_fetch, send_back, flip_bits, mixers, stencils, shifts, early
    )
    summed = in_one(
        (first[0], first[1], first[2], second[0], second[1], second[2]),
        (("tile_0", "tile_1"), ("tile_2", "batch")),
    )
    first = summed[:3]
    second = summed[3:]
    scale = 1.0 / math.sqrt(
        samples * tile_count * side_len * side_len * groups * lax.axis_size("batch")
    )
    mixer_grads = jnp.stack([first[0], second[0]]) * scale
    stencil_grads = jnp.stack([first[1], second[1]]) * scale
    shift_grads = jnp.stack([first[2], second[2]]) * scale
    return (outcome, state_grad, mixer_grads, stencil_grads, shift_grads)


def solution(mesh):
    torus = Mesh(
        mesh.devices.reshape(4, 4, 2, mesh.shape["batch"]), ("tile_0", "tile_1", "tile_2", "batch")
    )
    in_specs = (
        P("batch", TILE, None, None, None),
        P("batch", TILE, None, None, None),
        P(),
        P(),
        P(),
        P(),
        P(),
    )
    out_specs = (
        P("batch", TILE, None, None, None),
        P("batch", TILE, None, None, None),
        P(),
        P(),
        P(),
    )
    return jax.shard_map(
        shards, mesh=torus, in_specs=in_specs, out_specs=out_specs, check_vma=False
    )
```

profile of v0, /device:TPU:1, one launch (start us, length us, event | category | flops | bytes accessed | tf_op | source)
XLA Modules:
  0.0 396.2 jit_solution(10766597976360307351)
XLA Ops:
  9.2 9.9 %all-to-all-start = ((bf16[1,32,2,16,256]{4,3,2,0,1:T(8,128)(2,1)}), bf16[1,32,2,16,256]{4,3,2,0,1:T(8,128)(2,1)S(1)}, u32[]{:S(2)}, u32[]{:S(2)}) async-start(bf16[1,32,2,16,256]{4,3,2,0,1:T(8,128)(2,1)} %bitcast.10), calls=%async_computation | async-start | bytes 1048576 | tf_op jit(solution)/shard_map/all_to_all | solution.py:265
  24.4 6.2 %all-to-all-done = bf16[1,32,2,16,256]{4,3,2,0,1:T(8,128)(2,1)S(1)} async-done(((bf16[1,32,2,16,256]{4,3,2,0,1:T(8,128)(2,1)}), bf16[1,32,2,16,256]{4,3,2,0,1:T(8,128)(2,1)S(1)}, u32[]{:S(2)}, u32[]{:S(2)}) %all-to-all-start) | async-done | bytes 524320 | tf_op jit(solution)/shard_map/all_to_all | solution.py:265
  32.8 8.4 %constant_dynamic-update-slice_fusion.1 = (bf16[1,8,16,18,256]{4,0,3,2,1:T(2,128)(2,1)S(1)}, f32[1,8,16,16,256]{4,0,3,2,1:T(1,128)}, bf16[1,8,16,16,256]{4,0,3,2,1:T(2,128)(2,1)S(1)}) fusion(bf16[1,8,16,18,256]{4,0,3,2,1:T(2,128)(2,1)S(1)} %get-tuple-element.232, bf16[1,8,16,16,256]{4,3,2,1,0:T(8,128)(2,1)S(1)} %copy-done.25), kind=kLoop, calls=%fused_computation.229 | loop fusion | flops 524288 | bytes 7340032
  42.0 19.6 %add_convert_fusion.1 = bf16[1,8,16,16,256]{4,0,3,2,1:T(2,128)(2,1)S(1)} fusion(f32[256]{0:T(256)S(1)} %bitcast.338, f32[256]{0:T(256)S(1)} %bitcast.340, f32[256]{0:T(256)S(1)} %bitcast.342, f32[256]{0:T(256)S(1)} %bitcast.344, f32[256]{0:T(256)S(1)} %bitcast.346, f32[256]{0:T(256)S(1)} %bitcast.336, f32[256]{0:T(256)S(1)} %bitcast.348, ...), kind=kLoop, calls=%fused_computation.85 | loop fusion | flops 18350080 | bytes 3564544 | tf_op jit(solution)/shard_map/convert_element_type | solution.py:179
  70.2 4.8 %all-to-all-start.1 = ((bf16[1,32,2,16,256]{4,3,2,0,1:T(8,128)(2,1)}), bf16[1,32,2,16,256]{4,3,2,0,1:T(8,128)(2,1)}, u32[]{:S(2)}, u32[]{:S(2)}) async-start(bf16[1,32,2,16,256]{4,3,2,0,1:T(8,128)(2,1)} %bitcast.324), calls=%async_computation.1 | async-start | bytes 1048576 | tf_op jit(solution)/shard_map/all_to_all | solution.py:265
  75.0 17.3 %broadcast_multiply_fusion.17 = (f32[1,8,16,16,256]{4,0,3,2,1:T(1,128)}, f32[1,8,16,16,256]{4,0,3,2,1:T(1,128)}, f32[1,8,16,16,256]{4,0,3,2,1:T(1,128)}, f32[1,8...) fusion(f32[256]{0:T(256)} %bitcast.354, ...), kind=kLoop, calls=%fused_computation.118 | loop fusion | flops 3670016 | bytes 16784384 | tf_op jit(solution)/shard_map/mul | solution.py:117
  106.3 24.1 %multiply_reduce_fusion = (f32[256]{0:T(256)}, f32[256]{0:T(256)}, f32[256]{0:T(256)}, f32[256]{0:T(256)}, f32[256]{0:T(256)}, /*index=5*/f32[256]{0:T(256)}, f3...) fusion(bf16[1,8,1,18,256]{4,0,3,2,1:T(2,128)(2,1)S(1)} %copy.390, ...), kind=kLoop, calls=%fused_computation.63 | loop fusion | flops 17823744 | bytes 8808448 | tf_op jit(solution)/shard_map/reduce_sum | solution.py:132
  130.5 14.9 %pad_add_fusion.1 = f32[1,8,18,18,256]{4,0,3,2,1:T(1,128)S(1)} fusion(f32[1,8,16,16,256]{4,0,3,2,1:T(1,128)S(1)} %get-tuple-element.176, f32[1,8,16,16,256]{4,0,3,2,1:T(1,128)S(1)} %copy-done.22, f32[1,8,16,16,256]{4,0,3,2,1:T(1,128)S(1)} %copy-done.21, f32[1,8,16,16,256]{4,0,3,2,1:T(1,128)S(1)} %copy-done.20, f32[1,8,16,16,256]{4,0,3,2,1:T(1,128)S(1)} %copy-done.19, ...), kind=kLoop, calls=%fused_computation.17 | loop fusion | flops 5308416 | bytes 21528576 | tf_op jit(solution)/shard_map/add | solution.py:116
  155.0 7.3 %all-to-all-start.2 = ((f32[1,32,2,16,256]{4,3,2,0,1:T(8,128)}), f32[1,32,2,16,256]{4,3,2,0,1:T(8,128)}, u32[]{:S(2)}, u32[]{:S(2)}) async-start(f32[1,32,2,16,256]{4,3,2,0,1:T(8,128)} %bitcast.320), calls=%async_computation.2 | async-start | bytes 2097152 | tf_op jit(solution)/shard_map/all_to_all | solution.py:287
  162.4 22.4 %add_convert_fusion = bf16[1,8,16,16,256]{4,0,3,2,1:T(2,128)(2,1)S(1)} fusion(bf16[1,8,16,16,256]{4,0,3,2,1:T(2,128)(2,1)} %copy-done.3, f32[256]{0:T(256)S(1)} %bitcast.371, f32[256]{0:T(256)S(1)} %bitcast.367, f32[256]{0:T(256)S(1)} %bitcast.357, f32[256]{0:T(256)S(1)} %bitcast.359, f32[256]{0:T(256)S(1)} %bitcast.361, f32[256]{0:T(256)S(1)} %bitcast.369, ...), kind=kLoop, calls=%fused_computation.82 | loop fusion | flops 18350080 | bytes 3564544 | tf_op jit(solution)/shard_map/convert_element_type | solution.py:184
  194.9 6.1 %scatter_fusion = f32[32,16,256]{2,1,0:T(8,128)S(1)} fusion(f32[32,16,256]{2,1,0:T(8,128)S(1)} %broadcast.631.clone, s32[64]{0:T(128)S(1)} %copy-done.90, f32[64,16,256]{2,1,0:T(8,128)} %select_bitcast_fusion.3), kind=kCustom, calls=%fused_computation.8 | custom fusion | flops 262144 | bytes 3145984 | tf_op jit(solution)/shard_map/scatter-add | solution.py:298
  203.4 6.2 %scatter_fusion.1 = f32[32,16,256]{2,1,0:T(8,128)S(1)} fusion(f32[32,16,256]{2,1,0:T(8,128)S(1)} %scatter_fusion, s32[64]{0:T(128)S(1)} %copy-done.88, f32[64,16,256]{2,1,0:T(8,128)} %select_bitcast_fusion.2), kind=kCustom, calls=%fused_computation.9 | custom fusion | flops 262144 | bytes 3145984 | tf_op jit(solution)/shard_map/scatter-add | solution.py:299
  221.6 13.0 %broadcast_multiply_fusion.16 = (f32[1,8,16,16,256]{4,0,3,2,1:T(1,128)S(1)}, f32[1,8,16,16,256]{4,0,3,2,1:T(1,128)S(1)}, f32[1,8,16,16,256]{4,0,3,2,1:T(1,128)S(...) fusion(f32[256]{0:T(256)S(1)} %bitcast.353, ...), kind=kLoop, calls=%fused_computation.116 | loop fusion | flops 4194304 | bytes 18882560 | tf_op jit(solution)/shard_map/mul | solution.py:117
  234.7 25.6 %multiply_reduce_fusion.9 = (f32[256]{0:T(256)S(1)}, f32[256]{0:T(256)S(1)}, f32[256]{0:T(256)S(1)}, f32[256]{0:T(256)S(1)}, f32[256]{0:T(256)S(1)}, /*index=5*/...) fusion(bf16[1,8,1,18,256]{4,0,3,2,1:T(2,128)(2,1)S(1)} %copy-done.28, ...), kind=kLoop, calls=%fused_computation.73 | loop fusion | flops 18872064 | bytes 7759872 | tf_op jit(solution)/shard_map/reduce_sum | solution.py:132
  260.3 14.8 %pad_add_fusion = f32[1,8,18,18,256]{4,0,3,2,1:T(1,128)S(1)} fusion(f32[1,8,16,16,256]{4,0,3,2,1:T(1,128)S(1)} %get-tuple-element.184, f32[1,8,16,16,256]{4,0,3,2,1:T(1,128)S(1)} %get-tuple-element.183, f32[1,8,16,16,256]{4,0,3,2,1:T(1,128)S(1)} %get-tuple-element.182, f32[1,8,16,16,256]{4,0,3,2,1:T(1,128)S(1)} %get-tuple-element.181, ...), kind=kLoop, calls=%fused_computation.16 | loop fusion | flops 5308416 | bytes 21528576 | tf_op jit(solution)/shard_map/add | solution.py:116
  275.1 3.7 slice.823
  291.0 8.0 %all-to-all-start.3 = ((f32[1,32,2,16,256]{4,3,2,0,1:T(8,128)}), f32[1,32,2,16,256]{4,3,2,0,1:T(8,128)}, u32[]{:S(2)}, u32[]{:S(2)}) async-start(f32[1,32,2,16,256]{4,3,2,0,1:T(8,128)} %bitcast.321), calls=%async_computation.3 | async-start | bytes 2097152 | tf_op jit(solution)/shard_map/all_to_all | solution.py:287
  300.0 6.1 %scatter_fusion.2 = f32[32,16,256]{2,1,0:T(8,128)S(1)} fusion(f32[32,16,256]{2,1,0:T(8,128)S(1)} %broadcast.631, s32[64]{0:T(128)S(1)} %copy-done.91, f32[64,16,256]{2,1,0:T(8,128)} %select_bitcast_fusion.1), kind=kCustom, calls=%fused_computation.10 | custom fusion | flops 262144 | bytes 3145984 | tf_op jit(solution)/shard_map/scatter-add | solution.py:298
  318.1 6.2 %scatter_fusion.3 = f32[32,16,256]{2,1,0:T(8,128)S(1)} fusion(f32[32,16,256]{2,1,0:T(8,128)S(1)} %scatter_fusion.2, s32[64]{0:T(128)S(1)} %copy-done.89, f32[64,16,256]{2,1,0:T(8,128)} %select_bitcast_fusion), kind=kCustom, calls=%fused_computation.11 | custom fusion | flops 262144 | bytes 3145984 | tf_op jit(solution)/shard_map/scatter-add | solution.py:299
  340.0 14.7 %all_to_all.49 = f32[8,16,1064]{2,1,0:T(8,128)S(1)} all-to-all(f32[8,16,1064]{2,1,0:T(8,128)S(1)} %copy.435), channel_id=1, replica_groups=mesh['tile_0'=4,'tile_1'=4,'tile_2'=2,'batch'=4] {'tile_2','batch'}, dimensions={0} | all-to-all | bytes 1089536 | tf_op jit(solution)/shard_map/all_to_all | solution.py:46
  354.8 10.9 %all_to_all.50 = f32[16,1,1064]{2,1,0:T(1,128)S(1)} all-to-all(f32[16,1,1064]{2,1,0:T(1,128)S(1)} %all_to_all.35), channel_id=1, replica_groups=mesh['tile_0'=4,'tile_1'=4,'tile_2'=2,'batch'=4] {'tile_0','tile_1'}, dimensions={0} | all-to-all | bytes 136192 | tf_op jit(solution)/shard_map/all_to_all | solution.py:53
  365.8 9.8 %all_to_all.48 = f32[16,1,1064]{2,1,0:T(1,128)S(1)} all-to-all(f32[16,1,1064]{2,1,0:T(1,128)S(1)} %broadcast_in_dim.249), channel_id=1, replica_groups=mesh['tile_0'=4,'tile_1'=4,'tile_2'=2,'batch'=4] {'tile_0','tile_1'}, dimensions={0} | all-to-all | bytes 136192 | tf_op jit(solution)/shard_map/all_to_all | solution.py:24
  376.5 6.4 %all-to-all-start.7 = ((f32[8,16,1064]{2,1,0:T(8,128)}), f32[8,16,1064]{2,1,0:T(8,128)S(1)}, u32[]{:S(2)}, u32[]{:S(2)}) async-start(f32[8,16,1064]{2,1,0:T(8,128)} %broadcast_in_dim.250), calls=%async_computation.7 | async-start | bytes 1179648 | tf_op jit(solution)/shard_map/all_to_all | solution.py:24
  385.6 7.4 %all-to-all-done.7 = f32[8,16,1064]{2,1,0:T(8,128)S(1)} async-done(((f32[8,16,1064]{2,1,0:T(8,128)}), f32[8,16,1064]{2,1,0:T(8,128)S(1)}, u32[]{:S(2)}, u32[]{:S(2)}) %all-to-all-start.7) | async-done | bytes 544800 | tf_op jit(solution)/shard_map/all_to_all | solution.py:24
  (371 shorter events, 119.6 us)
Async XLA Ops:
  5.9 25.3 %copy-start.47 = (pred[64]{0:T(512)(128)(4,1)}, pred[64]{0:T(512)(128)(4,1)S(1)}, u32[]{:S(2)}) copy-start(pred[64]{0:T(512)(128)(4,1)S(1)} %get-tuple-element.159) | copy-start | bytes 196
  5.9 25.3 %copy-start.85 = (pred[64]{0:T(512)(128)(4,1)}, pred[64]{0:T(512)(128)(4,1)S(1)}, u32[]{:S(2)}) copy-start(pred[64]{0:T(512)(128)(4,1)S(1)} %get-tuple-element.157) | copy-start | bytes 196
  9.2 21.4 %all-to-all-start = ((bf16[1,32,2,16,256]{4,3,2,0,1:T(8,128)(2,1)}), bf16[1,32,2,16,256]{4,3,2,0,1:T(8,128)(2,1)S(1)}, u32[]{:S(2)}, u32[]{:S(2)}) async-start(bf16[1,32,2,16,256]{4,3,2,0,1:T(8,128)(2,1)} %bitcast.10), calls=%async_computation | async-start | bytes 1048576 | tf_op jit(solution)/shard_map/all_to_all | solution.py:265
  41.6 20.1 %copy-start.27 = (bf16[1,8,1,18,256]{4,0,3,2,1:T(2,128)(2,1)}, bf16[1,8,1,18,256]{4,0,3,2,1:T(2,128)(2,1)S(1)}, u32[]{:S(2)}) copy-start(bf16[1,8,1,18,256]{4,0,3,2,1:T(2,128)(2,1)S(1)} %copy.373) | copy-start | bytes 221188
  41.9 19.8 %copy-start.6 = (bf16[1,8,16,18,256]{4,0,3,2,1:T(2,128)(2,1)}, bf16[1,8,16,18,256]{4,0,3,2,1:T(2,128)(2,1)S(1)}, u32[]{:S(2)}) copy-start(bf16[1,8,16,18,256]{4,0,3,2,1:T(2,128)(2,1)S(1)} %get-tuple-element.230) | copy-start | bytes 3538948
  41.9 19.8 %copy-start.32 = (bf16[1,8,16,1,256]{4,0,3,2,1:T(2,128)(2,1)}, bf16[1,8,16,1,256]{4,0,3,2,1:T(2,128)(2,1)S(1)}, u32[]{:S(2)}) copy-start(bf16[1,8,16,1,256]{4,0,3,2,1:T(2,128)(2,1)S(1)} %get-tuple-element.231) | copy-start | bytes 196612
  70.2 23.6 %all-to-all-start.1 = ((bf16[1,32,2,16,256]{4,3,2,0,1:T(8,128)(2,1)}), bf16[1,32,2,16,256]{4,3,2,0,1:T(8,128)(2,1)}, u32[]{:S(2)}, u32[]{:S(2)}) async-start(bf16[1,32,2,16,256]{4,3,2,0,1:T(8,128)(2,1)} %bitcast.324), calls=%async_computation.1 | async-start | bytes 1048576 | tf_op jit(solution)/shard_map/all_to_all | solution.py:265
  102.1 28.3 %copy-start.24 = (f32[1,8,16,16,256]{4,0,3,2,1:T(1,128)S(1)}, f32[1,8,16,16,256]{4,0,3,2,1:T(1,128)}, u32[]{:S(2)}) copy-start(f32[1,8,16,16,256]{4,0,3,2,1:T(1,128)} %get-tuple-element.193) | copy-start | bytes 6291460
  105.4 24.9 %copy-start.3 = (bf16[1,8,16,16,256]{4,0,3,2,1:T(2,128)(2,1)}, bf16[1,8,16,16,256]{4,0,3,2,1:T(2,128)(2,1)S(1)}, u32[]{:S(2)}) copy-start(bf16[1,8,16,16,256]{4,0,3,2,1:T(2,128)(2,1)S(1)} %get-tuple-element.197) | copy-start | bytes 3145732
  105.5 24.9 %copy-start.23 = (f32[1,8,16,16,256]{4,0,3,2,1:T(1,128)S(1)}, f32[1,8,16,16,256]{4,0,3,2,1:T(1,128)}, u32[]{:S(2)}) copy-start(f32[1,8,16,16,256]{4,0,3,2,1:T(1,128)} %get-tuple-element.192) | copy-start | bytes 6291460
  105.9 24.5 %copy-start.29 = (bf16[1,8,1,18,256]{4,0,3,2,1:T(2,128)(2,1)}, bf16[1,8,1,18,256]{4,0,3,2,1:T(2,128)(2,1)S(1)}, u32[]{:S(2)}) copy-start(bf16[1,8,1,18,256]{4,0,3,2,1:T(2,128)(2,1)S(1)} %copy.390) | copy-start | bytes 221188
  106.2 24.2 %copy-start.8 = (bf16[1,8,16,18,256]{4,0,3,2,1:T(2,128)(2,1)}, bf16[1,8,16,18,256]{4,0,3,2,1:T(2,128)(2,1)S(1)}, u32[]{:S(2)}) copy-start(bf16[1,8,16,18,256]{4,0,3,2,1:T(2,128)(2,1)S(1)} %get-tuple-element.226) | copy-start | bytes 3538948
  106.2 24.2 %copy-start.35 = (bf16[1,8,16,1,256]{4,0,3,2,1:T(2,128)(2,1)}, bf16[1,8,16,1,256]{4,0,3,2,1:T(2,128)(2,1)S(1)}, u32[]{:S(2)}) copy-start(bf16[1,8,16,1,256]{4,0,3,2,1:T(2,128)(2,1)S(1)} %get-tuple-element.227) | copy-start | bytes 196612
  106.2 24.2 %copy-start.18 = (f32[1,8,16,16,256]{4,0,3,2,1:T(1,128)S(1)}, f32[1,8,16,16,256]{4,0,3,2,1:T(1,128)}, u32[]{:S(2)}) copy-start(f32[1,8,16,16,256]{4,0,3,2,1:T(1,128)} %get-tuple-element.187) | copy-start | bytes 6291460
  106.2 24.2 %copy-start.19 = (f32[1,8,16,16,256]{4,0,3,2,1:T(1,128)S(1)}, f32[1,8,16,16,256]{4,0,3,2,1:T(1,128)}, u32[]{:S(2)}) copy-start(f32[1,8,16,16,256]{4,0,3,2,1:T(1,128)} %get-tuple-element.188) | copy-start | bytes 6291460
  106.3 24.2 %copy-start.20 = (f32[1,8,16,16,256]{4,0,3,2,1:T(1,128)S(1)}, f32[1,8,16,16,256]{4,0,3,2,1:T(1,128)}, u32[]{:S(2)}) copy-start(f32[1,8,16,16,256]{4,0,3,2,1:T(1,128)} %get-tuple-element.189) | copy-start | bytes 6291460
  106.3 24.2 %copy-start.21 = (f32[1,8,16,16,256]{4,0,3,2,1:T(1,128)S(1)}, f32[1,8,16,16,256]{4,0,3,2,1:T(1,128)}, u32[]{:S(2)}) copy-start(f32[1,8,16,16,256]{4,0,3,2,1:T(1,128)} %get-tuple-element.190) | copy-start | bytes 6291460
  106.3 24.2 %copy-start.22 = (f32[1,8,16,16,256]{4,0,3,2,1:T(1,128)S(1)}, f32[1,8,16,16,256]{4,0,3,2,1:T(1,128)}, u32[]{:S(2)}) copy-start(f32[1,8,16,16,256]{4,0,3,2,1:T(1,128)} %get-tuple-element.191) | copy-start | bytes 6291460
  130.5 16.7 %copy-start.40 = (f32[8,4,16]{2,1,0:T(4,128)S(1)}, f32[8,4,16]{2,1,0:T(4,128)}, u32[]{:S(2)}) copy-start(f32[8,4,16]{2,1,0:T(4,128)} %broadcast_select_fusion.4) | copy-start | bytes 6148
  155.0 46.0 %all-to-all-start.2 = ((f32[1,32,2,16,256]{4,3,2,0,1:T(8,128)}), f32[1,32,2,16,256]{4,3,2,0,1:T(8,128)}, u32[]{:S(2)}, u32[]{:S(2)}) async-start(f32[1,32,2,16,256]{4,3,2,0,1:T(8,128)} %bitcast.320), calls=%async_computation.2 | async-start | bytes 2097152 | tf_op jit(solution)/shard_map/all_to_all | solution.py:287
  162.4 22.4 %copy-start.5 = (f32[1,8,18,18,256]{4,0,3,2,1:T(1,128)S(1)}, f32[1,8,18,18,256]{4,0,3,2,1:T(1,128)}, u32[]{:S(2)}) copy-start(f32[1,8,18,18,256]{4,0,3,2,1:T(1,128)} %copy-done.4) | copy-start | bytes 7962628
  291.0 24.8 %all-to-all-start.3 = ((f32[1,32,2,16,256]{4,3,2,0,1:T(8,128)}), f32[1,32,2,16,256]{4,3,2,0,1:T(8,128)}, u32[]{:S(2)}, u32[]{:S(2)}) async-start(f32[1,32,2,16,256]{4,3,2,0,1:T(8,128)} %bitcast.321), calls=%async_computation.3 | async-start | bytes 2097152 | tf_op jit(solution)/shard_map/all_to_all | solution.py:287
  340.0 42.9 %copy-start.17 = (f32[1,8,16,16,256]{4,0,3,2,1:T(1,128)S(1)}, f32[1,8,16,16,256]{4,0,3,2,1:T(1,128)}, u32[]{:S(2)}) copy-start(f32[1,8,16,16,256]{4,0,3,2,1:T(1,128)} %get-tuple-element.203) | copy-start | bytes 6291460
  376.5 16.5 %all-to-all-start.7 = ((f32[8,16,1064]{2,1,0:T(8,128)}), f32[8,16,1064]{2,1,0:T(8,128)S(1)}, u32[]{:S(2)}, u32[]{:S(2)}) async-start(f32[8,16,1064]{2,1,0:T(8,128)} %broadcast_in_dim.250), calls=%async_computation.7 | async-start | bytes 1179648 | tf_op jit(solution)/shard_map/all_to_all | solution.py:24
  (81 other events, 529.9 us)
where the time goes:
time: 401 us; the launch traced here: 396 us
  other arithmetic  234 us (58%)
  local copies, waits for them, and re-layouts  65.3 us (16%)
  starting transfers between devices  36.4 us (9%)
  blocking collectives  35.4 us (9%)
  waiting for transfers between devices  15.9 us (4%)
  matrix products  5.87 us (1%)
    reduce_sum x2, other arithmetic, stencil_grad(): terms.append(jnp.sum(widened * window, axis=(0, 1, 2, 3)))  49.7 us
    mul x2, other arithmetic, stencil_back(): kernel[3 * row_at + col_at] * widened  30.2 us
    add x2, other arithmetic, stencil_back(): running + jnp.pad(kernel[3 * row_at + col_at] * widened, ((0, 0), (0, 0),...  29.7 us
    unnamed x228, local copies, waits for them, and re-layouts  25.5 us
    convert_element_type x1, other arithmetic, block_pass(): conv_second = stencil_apply(padded_mid, stencils[1]).astype(jnp.bfloat16)  22.4 us
    convert_element_type x1, other arithmetic, block_pass(): conv_first = stencil_apply(padded_in, stencils[0]).astype(jnp.bfloat16)  19.6 us
    all_to_all x2, starting transfers between devices, send_back(): lax.all_to_all(outgoing.reshape(samples, groups, CAP, side_len, channels)...  15.3 us
    all_to_all x1, blocking collectives, sent_and_summed(): lax.all_to_all(parts, axis, split_axis=0, concat_axis=0, tiled=True)  14.7 us
  transfers between devices with their start and end apart: 5, of which 3 were waited for; matrix products, arithmetic and copies ran while one was open for 20% of the time, Pallas kernels for 0%

commit v1 on v0

v1 whole, which is shorter than its diff:
```python
import math

import jax
import jax.numpy as jnp
import numpy as np
from jax import lax
from jax.experimental import pallas as pl
from jax.experimental.pallas import tpu as pltpu
from jax.sharding import Mesh
from jax.sharding import PartitionSpec as P


TILE = ("tile_0", "tile_1", "tile_2")
SQRT_HALF = 0.7071067811865476
INV_ROOT_TAU = 0.3989422804014327

F32 = jnp.float32
BF16 = jnp.bfloat16
I32 = jnp.int32

S = 16
T = 8
CELLS = S * S
SIDE_TAPS = {0: (0, 1, 2), 1: (2, 5, 8), 2: (6, 7, 8), 3: (0, 3, 6)}
CORNER_TAP = {4: 2, 5: 8, 6: 6, 7: 0}
VMEM_LIMIT = 60 * 1024 * 1024


def line_cell(d, i):
    if d == 0:
        return i
    if d == 1:
        return S * i + S - 1
    if d == 2:
        return S * (S - 1) + i
    if d == 3:
        return S * i
    if i != 0:
        return None
    return {4: S - 1, 5: CELLS - 1, 6: S * (S - 1), 7: 0}[d]


def selection():
    sel = np.zeros((256, CELLS), np.float32)
    for d in range(8):
        for f in range(2):
            for i in range(S):
                cell = line_cell(d, S - 1 - i if f else i)
                if cell is not None:
                    sel[(2 * d + f) * S + i, cell] = 1.0
    return sel


def spreading():
    out = np.zeros((CELLS, 128), np.float32)
    for d in range(4):
        for i in range(S):
            out[line_cell(d, i), d * S + i] = 1.0
            out[line_cell(d, i), 64 + d * S + i] = 1.0
    return out


def shifting():
    out = np.zeros((512, CELLS), np.float32)
    for i in range(S):
        for j in range(S):
            if j > 0:
                out[S * i + j, S * i + j - 1] = 1.0
            if j < S - 1:
                out[256 + S * i + j, S * i + j + 1] = 1.0
    return out


def dot(a, b):
    return jnp.dot(a, b, preferred_element_type=F32)


def dot_t(a, b):
    return lax.dot_general(a, b, (((1,), (1,)), ((), ())), preferred_element_type=F32)


def t_dot(a, b):
    return lax.dot_general(a, b, (((0,), (0,)), ((), ())), preferred_element_type=F32)


def iota(shape, axis):
    return lax.broadcasted_iota(I32, shape, axis)


def neighbours(x):
    place = iota(x.shape, 0)
    before = jnp.where(place == 0, 0.0, pltpu.roll(x, 1, 0))
    after = jnp.where(place == S - 1, 0.0, pltpu.roll(x, S - 1, 0))
    return before, after


def down(x):
    return jnp.concatenate([jnp.zeros((S, x.shape[1]), x.dtype), x[: CELLS - S]], axis=0)


def up(x):
    return jnp.concatenate([x[S:], jnp.zeros((S, x.shape[1]), x.dtype)], axis=0)


def conv_inner(left, centre, right, w):
    rows = [w[3 * a] * left + w[3 * a + 1] * centre + w[3 * a + 2] * right for a in range(3)]
    return rows[1] + down(rows[0]) + up(rows[2])


def back_inner(left, centre, right, w):
    rows = [w[3 * a] * right + w[3 * a + 1] * centre + w[3 * a + 2] * left for a in range(3)]
    return rows[1] + up(rows[0]) + down(rows[2])


def tap_rows(ref, layer):
    return [ref[layer, k : k + 1, :] for k in range(9)]


def fill_tap_sets(taps_ref, stencil_ref, layer):
    w = tap_rows(stencil_ref, layer)
    zero = jnp.zeros_like(w[0])
    for d in range(8):
        if d < 4:
            three = [w[k] for k in SIDE_TAPS[d]]
        else:
            three = [zero, w[CORNER_TAP[d]], zero]
        for f in range(2):
            for m, row in enumerate(three[::-1] if f else three):
                taps_ref[2 * d + f, m : m + 1, :] = row


def tile_of(ref, t):
    return ref[pl.ds(pl.multiple_of(t * CELLS, CELLS), CELLS), :]


def put_tile(ref, t, value):
    ref[pl.ds(pl.multiple_of(t * CELLS, CELLS), CELLS), :] = value


def split_store(ref, t, first, value):
    high = value.astype(BF16)
    ref[t, pl.ds(first, value.shape[0]), :] = high
    ref[t, pl.ds(64 + first, value.shape[0]), :] = (value - high.astype(F32)).astype(BF16)


def forward_lines(split_ref, buf_ref, tab_ref, w):
    place = None

    def one(t, carry):
        corner = {}
        for d in range(4, 8):
            row = buf_ref[tab_ref[0, t * 8 + d]][:8, :].astype(F32)[:1, :]
            corner[d] = w[CORNER_TAP[d]] * row
        for d in range(4):
            x = buf_ref[tab_ref[0, t * 8 + d]].astype(F32)
            before, after = neighbours(x)
            a, b, c = SIDE_TAPS[d]
            line = w[a] * before + w[b] * x + w[c] * after
            at = iota(line.shape, 0)
            if d == 0:
                line = line + jnp.where(at == 0, corner[7], 0.0)
                line = line + jnp.where(at == S - 1, corner[4], 0.0)
            if d == 2:
                line = line + jnp.where(at == 0, corner[6], 0.0)
                line = line + jnp.where(at == S - 1, corner[5], 0.0)
            split_store(split_ref, t, d * S, line)
        return carry

    del place
    lax.fori_loop(0, T, one, 0)


def rim_gradients(split_ref, rim_ref, lines_ref, tab_ref, taps_ref):
    rim_ref[...] = jnp.zeros_like(rim_ref)

    def one(i, carry):
        x = lines_ref[i].astype(F32)
        before, after = neighbours(x)
        u = taps_ref[tab_ref[3, i]]
        rim = tab_ref[2, i] >> 1
        rim_ref[rim] += u[0:1] * after + u[1:2] * x + u[2:3] * before
        return carry

    lax.fori_loop(0, 128, one, 0, unroll=8)

    def split(t, carry):
        for e in range(4):
            split_store(split_ref, t, e * S, rim_ref[t * 4 + e])
        return carry

    lax.fori_loop(0, T, split, 0)


def live_lines(dst_ref, own_ref, in_ref, tab_ref):
    def own(i, carry):
        dst_ref[i] = jnp.where(tab_ref[4, i] > 0, own_ref[i], jnp.zeros((S, 256), BF16))
        j = i + 64
        dst_ref[j] = jnp.where(tab_ref[4, j] > 0, in_ref[i, S : 2 * S], jnp.zeros((S, 256), BF16))
        return carry

    lax.fori_loop(0, 64, own, 0, unroll=8)


def gather_out(out_ref, own_ref, rims_ref, lines_ref, tab_ref):
    def one(s, carry):
        out_ref[s, 0:S] = rims_ref[tab_ref[2, 64 + s]]
        out_ref[s, S : 2 * S] = lines_ref[tab_ref[1, s]]
        own_ref[s] = lines_ref[tab_ref[5, s]]
        return carry

    lax.fori_loop(0, 64, one, 0, unroll=8)


def banks(rims_ref, lines_ref, rim_field, line_field, sel_ref):
    def one(t, carry):
        rims = dot(sel_ref[0:128, :], tile_of(rim_field, t)).astype(BF16)
        rims_ref[pl.ds(t * 8, 8)] = rims.reshape(8, S, 256)
        lines = dot(sel_ref[...], tile_of(line_field, t)).astype(BF16)
        lines_ref[pl.ds(t * 16, 16)] = lines.reshape(16, S, 256)
        return carry

    lax.fori_loop(0, T, one, 0)


def own_position():
    a, b, c = (lax.axis_index(name) for name in TILE)
    return (a * lax.axis_size(TILE[1]) + b) * lax.axis_size(TILE[2]) + c


def first_kernel(
    comb_ref, states_ref, cot_ref, sel_ref, tab_ref, out_ref, rims_ref, own_ref, lines_ref, smem, sem
):
    me = own_position()
    comb = comb_ref[...]
    groups = comb.shape[0]
    lane = iota(comb.shape, 1)
    home = iota(comb.shape, 0)
    slot = comb >> 3
    wanted = (lane < 64) & ((slot >> 3) == me) & (home != me)
    wanted_f = wanted.astype(F32)
    before = (iota((128, 128), 0) < iota((128, 128), 1)).astype(F32).astype(BF16)
    place = dot(wanted_f.astype(BF16), before)
    code = comb & 7
    rim_code = (slot & 7) * 8 + code
    tap_set = (lane & 7) * 2 + (code & 1)
    packed = (rim_code * 16 + tap_set + 1024).astype(F32)
    asked = jnp.zeros((1, 128), F32)
    for k in range(2):
        value = jnp.sum(
            jnp.where(wanted & (place == k), packed, 0.0), axis=1, keepdims=True
        )
        at = (lane >= 64) & (((lane - 64) >> 1) == home) & ((lane & 1) == k)
        asked = asked + jnp.sum(jnp.where(at, value, 0.0), axis=0, keepdims=True)
    asked = asked.astype(I32)

    own = comb_ref[pl.ds(me, 1), :]
    sub2 = iota((128, 128), 0)
    lane2 = iota((128, 128), 1)
    own_wide = jnp.broadcast_to(own, (128, 128))
    own_col = jnp.sum(
        jnp.where(sub2 == lane2, own_wide, 0).astype(F32), axis=1, keepdims=True
    ).astype(I32)
    owner_col = own_col >> 6
    owner_row = own >> 6
    same = (owner_col == owner_row) & (sub2 < 64) & (lane2 < 64)
    place_col = jnp.sum((same & (lane2 < sub2)).astype(F32), axis=1, keepdims=True).astype(I32)
    place_row = jnp.sum((same & (sub2 < lane2)).astype(F32), axis=0, keepdims=True).astype(I32)
    lane1 = iota((1, 128), 1)
    sub1 = iota((128, 1), 0)
    remote_row = owner_row != me
    slot_col = jnp.where((owner_col != me) & (sub1 < 64), owner_col * 2 + place_col, -1)
    line_col = (sub1 * 2 + (own_col & 1)).astype(F32)
    sent = jnp.sum(jnp.where(slot_col == lane2, line_col, 0.0), axis=0, keepdims=True).astype(I32)
    own_rim = (own & 511)
    own_rim = ((own_rim >> 3) & 7) * 8 + (own_rim & 7)
    in_own = lane1 < 64
    panel = jnp.where(remote_row, 64 + owner_row * 2 + place_row, own_rim)
    tab_ref[...] = jnp.zeros_like(tab_ref)
    tab_ref[0:1, :] = jnp.where(in_own, panel, 0)
    tab_ref[1:2, :] = jnp.where(in_own, sent, 0)
    tab_ref[2:3, :] = jnp.where(in_own, own_rim, (asked & 1023) >> 4)
    tab_ref[3:4, :] = jnp.where(in_own, (lane1 & 7) * 2 + (own & 1), asked & 15)
    tab_ref[4:5, :] = jnp.where(in_own, (~remote_row).astype(I32), asked >> 10)
    tab_ref[5:6, :] = jnp.where(in_own, lane1 * 2 + (own & 1), 0)
    del groups
    copy = pltpu.make_async_copy(tab_ref, smem, sem)
    copy.start()
    banks(rims_ref, lines_ref, states_ref, cot_ref, sel_ref)
    copy.wait()
    gather_out(out_ref, own_ref, rims_ref, lines_ref, smem)


def inner_kernel(states_ref, cot_ref, mixers_ref, stencils_ref, shift_ref, conv_ref, back_ref, g_ref):
    w0 = tap_rows(stencils_ref, 0)
    w1 = tap_rows(stencils_ref, 1)

    def one(t, carry):
        x = tile_of(states_ref, t)
        moved = dot(shift_ref[...], x)
        put_tile(conv_ref, t, conv_inner(moved[:CELLS], x.astype(F32), moved[CELLS:], w0))
        g = dot_t(tile_of(cot_ref, t), mixers_ref[1]).astype(BF16)
        put_tile(g_ref, t, g)
        moved = dot(shift_ref[...], g)
        put_tile(back_ref, t, back_inner(moved[:CELLS], g.astype(F32), moved[CELLS:], w1))
        return carry

    lax.fori_loop(0, T, one, 0)


def middle_kernel(
    tab_ref, in_ref, rims_in_ref, own_in_ref, conv_ref, back_ref, mixers_ref, stencils_ref,
    shifts_ref, sel_ref, spread_ref,
    active_ref, first_ref, gh_ref, gc_ref, rims_ref, lines_ref, out_ref, own_ref, c_ref, g_ref,
    buf_ref, split_ref, split2_ref, rim_ref, taps_ref,
):
    w0 = tap_rows(stencils_ref, 0)
    buf_ref[0:64] = rims_in_ref[...]
    buf_ref[64:128] = in_ref[:, 0:S, :]
    forward_lines(split_ref, buf_ref, tab_ref, w0)
    fill_tap_sets(taps_ref, stencils_ref, 1)
    live_lines(c_ref, own_in_ref, in_ref, tab_ref)

    def line_grads(b, carry):
        part = c_ref[pl.ds(b * 16, 16)].reshape(256, 256)
        g_ref[pl.ds(b * 16, 16)] = dot_t(part, mixers_ref[1]).astype(BF16).reshape(16, S, 256)
        return carry

    lax.fori_loop(0, 8, line_grads, 0)
    rim_gradients(split2_ref, rim_ref, g_ref, tab_ref, taps_ref)

    def one(t, carry):
        first = (tile_of(conv_ref, t) + dot(spread_ref[...], split_ref[t])).astype(BF16)
        put_tile(first_ref, t, first)
        hidden = dot(first, mixers_ref[0]) + shifts_ref[0:1, :]
        cdf = 0.5 * (1.0 + lax.erf(hidden * SQRT_HALF))
        active = (hidden * cdf).astype(BF16)
        put_tile(active_ref, t, active)
        slope = cdf + hidden * jnp.exp(-0.5 * hidden * hidden) * INV_ROOT_TAU
        grad = tile_of(back_ref, t) + dot(spread_ref[...], split2_ref[t])
        gh = (grad * slope).astype(BF16)
        put_tile(gh_ref, t, gh)
        put_tile(gc_ref, t, dot_t(gh, mixers_ref[0]).astype(BF16))
        return carry

    lax.fori_loop(0, T, one, 0)
    banks(rims_ref, lines_ref, active_ref, gc_ref, sel_ref)
    gather_out(out_ref, own_ref, rims_ref, lines_ref, tab_ref)


def weight_kernel(
    tab_ref, states_ref, cot_ref, active_ref, first_ref, gh_ref, gc_ref, g2_ref, rims_ref, lines_ref,
    rims_in_ref, in_ref, c_ref, g_ref, stencils_ref, shift_ref,
    pack_ref, conv_ref, back_ref,
    second_ref, h_ref, taps_ref, acc1_ref, acc2_ref, accl_ref, sums_ref, buf_ref,
):
    w0 = tap_rows(stencils_ref, 0)
    w1 = tap_rows(stencils_ref, 1)
    acc1_ref[...] = jnp.zeros_like(acc1_ref)
    acc2_ref[...] = jnp.zeros_like(acc2_ref)
    accl_ref[...] = jnp.zeros_like(accl_ref)
    sums_ref[...] = jnp.zeros_like(sums_ref)
    buf_ref[0:64] = rims_in_ref[...]
    buf_ref[64:128] = in_ref[:, 0:S, :]
    fill_tap_sets(taps_ref, stencils_ref, 1)

    def folded(x):
        return jnp.sum(x.reshape(-1, 8, 256), axis=0)

    def taps_of(acc_ref, g, left, centre, right):
        for b, x in enumerate((left, centre, right)):
            acc_ref[b] += folded(g[S:] * x[: CELLS - S])
            acc_ref[3 + b] += folded(g * x)
            acc_ref[6 + b] += folded(g[: CELLS - S] * x[S:])

    def one(t, carry):
        gc = tile_of(gc_ref, t)
        moved = dot(shift_ref[...], gc)
        gcf = gc.astype(F32)
        put_tile(back_ref, t, back_inner(moved[:CELLS], gcf, moved[CELLS:], w0))
        x = tile_of(states_ref, t)
        moved = dot(shift_ref[...], x)
        taps_of(acc1_ref, gcf, moved[:CELLS], x.astype(F32), moved[CELLS:])
        x = tile_of(active_ref, t)
        moved = dot(shift_ref[...], x)
        xf = x.astype(F32)
        second = conv_inner(moved[:CELLS], xf, moved[CELLS:], w1)
        put_tile(conv_ref, t, second)
        put_tile(second_ref, t, second.astype(BF16))
        taps_of(acc2_ref, tile_of(g2_ref, t).astype(F32), moved[:CELLS], xf, moved[CELLS:])
        sums_ref[0] += folded(tile_of(gh_ref, t).astype(F32))
        sums_ref[1] += folded(tile_of(cot_ref, t).astype(F32))
        return carry

    lax.fori_loop(0, T, one, 0)

    def halves(x):
        return x[0:8] + x[8:16]

    def first_halo(t, carry):
        for d in range(8):
            x = buf_ref[tab_ref[0, t * 8 + d]].astype(F32)
            g = lines_ref[(t * 8 + d) * 2].astype(F32)
            if d < 4:
                before, after = neighbours(x)
                for k, y in zip(SIDE_TAPS[d], (before, x, after)):
                    acc1_ref[k] += halves(g * y)
            else:
                acc1_ref[CORNER_TAP[d]] += halves(g * x)
        return carry

    lax.fori_loop(0, T, first_halo, 0)

    def second_halo(i, carry):
        x = rims_ref[(tab_ref[2, i] >> 1) * 2].astype(F32)
        g = g_ref[i].astype(F32)
        before, after = neighbours(x)
        kind = tab_ref[3, i]
        u = taps_ref[kind]
        h_ref[i] = (u[0:1] * before + u[1:2] * x + u[2:3] * after).astype(BF16)
        for m, y in enumerate((before, x, after)):
            accl_ref[kind, m] += halves(g * y)
        return carry

    lax.fori_loop(0, 128, second_halo, 0, unroll=8)
    for d in range(8):
        for f in range(2):
            if d < 4:
                taps = SIDE_TAPS[d][::-1] if f else SIDE_TAPS[d]
                for m, k in enumerate(taps):
                    acc2_ref[k] += accl_ref[2 * d + f, m]
            else:
                acc2_ref[CORNER_TAP[d]] += accl_ref[2 * d + f, 1]

    mixer_first = t_dot(first_ref[...], gh_ref[...])
    mixer_second = t_dot(second_ref[...], cot_ref[...]) + t_dot(
        h_ref[...].reshape(2048, 256), c_ref[...].reshape(2048, 256)
    )
    half = pack_ref.shape[0] // 2
    for r in range(half):
        pack_ref[r, 0:16] = mixer_first[16 * r : 16 * r + 16].astype(BF16)
        pack_ref[half + r, 0:16] = mixer_second[16 * r : 16 * r + 16].astype(BF16)
    rows = [jnp.sum(acc1_ref[k], axis=0, keepdims=True) for k in range(9)]
    rows += [jnp.sum(acc2_ref[k], axis=0, keepdims=True) for k in range(9)]
    rows += [jnp.sum(sums_ref[k], axis=0, keepdims=True) for k in range(2)]
    rows += [jnp.zeros_like(rows[0])] * 4
    for r in range(3):
        pack_ref[r, 16:24] = jnp.concatenate(rows[8 * r : 8 * r + 8], axis=0).astype(BF16)
    for r in range(3, pack_ref.shape[0]):
        pack_ref[r, 16:24] = jnp.zeros((8, 256), BF16)


def last_kernel(
    tab_ref, in_ref, rims_in_ref, own_in_ref, conv_ref, back_ref, states_ref, cot_ref, mixers_ref,
    stencils_ref, shifts_ref, spread_ref,
    outcome_ref, grad_ref,
    buf_ref, split_ref, split2_ref, rim_ref, taps_ref, lines_ref,
):
    w1 = tap_rows(stencils_ref, 1)
    buf_ref[0:64] = rims_in_ref[...]
    buf_ref[64:128] = in_ref[:, 0:S, :]
    forward_lines(split_ref, buf_ref, tab_ref, w1)
    fill_tap_sets(taps_ref, stencils_ref, 0)
    live_lines(lines_ref, own_in_ref, in_ref, tab_ref)
    rim_gradients(split2_ref, rim_ref, lines_ref, tab_ref, taps_ref)

    def one(t, carry):
        second = (tile_of(conv_ref, t) + dot(spread_ref[...], split_ref[t])).astype(BF16)
        out = tile_of(states_ref, t).astype(F32) + dot(second, mixers_ref[1]) + shifts_ref[1:2, :]
        put_tile(outcome_ref, t, out.astype(BF16))
        grad = tile_of(back_ref, t) + dot(spread_ref[...], split2_ref[t])
        put_tile(grad_ref, t, (tile_of(cot_ref, t).astype(F32) + grad).astype(BF16))
        return carry

    lax.fori_loop(0, T, one, 0)


def sum_kernel(in_ref, out_ref):
    total = in_ref[0].astype(F32)
    for r in range(1, in_ref.shape[0]):
        total = total + in_ref[r].astype(F32)
    out_ref[...] = total


def spread_kernel(a_ref, b_ref, out_ref):
    value = (a_ref[...] + b_ref[...]).astype(BF16)
    for r in range(out_ref.shape[0]):
        out_ref[r] = value


def unpack_kernel(scale, in_ref, mixer_ref, stencil_ref, shift_ref):
    half = in_ref.shape[0] // 2
    for r in range(half):
        for k in range(2):
            mixer_ref[k, 16 * r : 16 * r + 16, :] = in_ref[k * half + r, 0:16].astype(F32) * scale
    rows = [in_ref[r, 16:24].astype(F32) * scale for r in range(3)]
    rows = [row for block in rows for row in jnp.split(block, 8, axis=0)]
    for k in range(2):
        for j in range(9):
            stencil_ref[k, j : j + 1, :] = rows[9 * k + j]
        shift_ref[k : k + 1, :] = rows[18 + k]


def shape_of(*dims, dtype=BF16):
    return jax.ShapeDtypeStruct(dims, dtype)


def call(body, outs, scratch=(), smem_first=False, count=0):
    vmem = pl.BlockSpec(memory_space=pltpu.VMEM)
    specs = [vmem] * count
    if smem_first:
        specs[0] = pl.BlockSpec(memory_space=pltpu.SMEM)
    many = isinstance(outs, (list, tuple))
    return pl.pallas_call(
        body,
        out_shape=outs,
        in_specs=specs,
        out_specs=[vmem] * len(outs) if many else vmem,
        scratch_shapes=list(scratch),
        compiler_params=pltpu.CompilerParams(vmem_limit_bytes=VMEM_LIMIT),
    )


def exchange(array):
    return lax.all_to_all(array, TILE, split_axis=0, concat_axis=0, tiled=True)


def whole_block(states, cotangent, beside_slot, beside_code, mixers, stencils, shifts):
    groups = lax.axis_size(TILE)
    batch = lax.axis_size("batch")
    shape = states.shape
    x = states.reshape(T * CELLS, 256)
    cot = cotangent.reshape(T * CELLS, 256)
    comb = (beside_slot * 8 + beside_code).astype(I32).reshape(groups, 64)
    comb = jnp.pad(comb, ((0, 0), (0, 64)))
    sel = jnp.asarray(selection(), BF16)
    spread = jnp.asarray(spreading(), BF16)
    shift = jnp.asarray(shifting(), BF16)
    lines16 = shape_of(128, S, 256)
    rims16 = shape_of(64, S, 256)
    field = shape_of(T * CELLS, 256)
    wide = shape_of(T * CELLS, 256, dtype=F32)
    tab, out1, rims1, own1 = call(
        first_kernel,
        [shape_of(8, 128, dtype=I32), shape_of(64, 2 * S, 256), rims16, rims16],
        [pltpu.VMEM((128, S, 256), BF16), pltpu.SMEM((8, 128), I32), pltpu.SemaphoreType.DMA],
        count=4,
    )(comb, x, cot, sel)
    in1 = exchange(out1.reshape(groups, 4 * S, 256)).reshape(64, 2 * S, 256)
    conv1, back2, g2 = call(inner_kernel, [wide, wide, field], count=5)(
        x, cot, mixers, stencils, shift
    )
    line_scratch = [
        pltpu.VMEM((128, S, 256), BF16),
        pltpu.VMEM((T, 128, 256), BF16),
        pltpu.VMEM((T, 128, 256), BF16),
        pltpu.VMEM((32, S, 256), F32),
        pltpu.VMEM((16, 3, 256), F32),
    ]
    active, first, gh, gc, rims2, lines2, out2, own2, c_lines, g_lines = call(
        middle_kernel,
        [field, field, field, field, rims16, lines16, shape_of(64, 2 * S, 256), rims16, lines16, lines16],
        line_scratch,
        smem_first=True,
        count=11,
    )(tab, in1, rims1, own1, conv1, back2, mixers, stencils, shifts, sel, spread)
    in2 = exchange(out2.reshape(groups, 4 * S, 256)).reshape(64, 2 * S, 256)
    pack, conv2, back1 = call(
        weight_kernel,
        [shape_of(groups, 24, 256), wide, wide],
        [
            pltpu.VMEM((T * CELLS, 256), BF16),
            pltpu.VMEM((128, S, 256), BF16),
            pltpu.VMEM((16, 3, 256), F32),
            pltpu.VMEM((9, 8, 256), F32),
            pltpu.VMEM((9, 8, 256), F32),
            pltpu.VMEM((16, 3, 8, 256), F32),
            pltpu.VMEM((2, 8, 256), F32),
            pltpu.VMEM((128, S, 256), BF16),
        ],
        smem_first=True,
        count=16,
    )(
        tab, x, cot, active, first, gh, gc, g2, rims2, lines2, rims1, in1, c_lines, g_lines,
        stencils, shift,
    )
    parts = exchange(pack)
    outcome, state_grad = call(
        last_kernel,
        [field, field],
        line_scratch + [pltpu.VMEM((128, S, 256), BF16)],
        smem_first=True,
        count=12,
    )(tab, in2, rims2, own2, conv2, back1, x, cot, mixers, stencils, shifts, spread)
    part = call(sum_kernel, shape_of(24, 256, dtype=F32), count=1)(parts)
    step = 1
    while 2 * step < batch:
        part = part + lax.ppermute(part, "batch", [(i, i ^ step) for i in range(batch)])
        step *= 2
    other = lax.ppermute(part, "batch", [(i, i ^ step) for i in range(batch)])
    spread_out = call(spread_kernel, shape_of(groups, 24, 256), count=2)(part, other)
    whole = exchange(spread_out)
    scale = 1.0 / math.sqrt(T * CELLS * groups * batch)

    def unpack(*refs):
        unpack_kernel(scale, *refs)

    mixer_grads, stencil_grads, shift_grads = call(
        unpack,
        [shape_of(2, 256, 256, dtype=F32), shape_of(2, 9, 256, dtype=F32), shape_of(2, 256, dtype=F32)],
        count=1,
    )(whole)
    return (
        outcome.reshape(shape),
        state_grad.reshape(shape),
        mixer_grads,
        stencil_grads,
        shift_grads,
    )


def solution(mesh):
    torus = Mesh(
        mesh.devices.reshape(4, 4, 2, mesh.shape["batch"]), ("tile_0", "tile_1", "tile_2", "batch")
    )
    in_specs = (
        P("batch", TILE, None, None, None),
        P("batch", TILE, None, None, None),
        P(),
        P(),
        P(),
        P(),
        P(),
    )
    out_specs = (
        P("batch", TILE, None, None, None),
        P("batch", TILE, None, None, None),
        P(),
        P(),
        P(),
    )
    return jax.shard_map(
        whole_block, mesh=torus, in_specs=in_specs, out_specs=out_specs, check_vma=False
    )
```

time: 401 us -> 141 us (0.35)
  other arithmetic: 234 us -> 1.46 us
  local copies, waits for them, and re-layouts: 65.3 us -> 5.4 us
  Pallas kernels: 0 us -> 59.1 us
  starting transfers between devices: 36.4 us -> 17.3 us
  waiting for transfers between devices: 15.9 us -> 24.7 us
  matrix products: 5.87 us -> 0 us
    pallas_call x0 -> x8, Pallas kernels: none -> 59.1 us  [the longest x1 16.5 us: whole_block(): call(middle_kernel, [field, field, field, field, rims16, lines16, shape_o...]
    reduce_sum x9 -> x0, other arithmetic: 54.2 us -> none  [the longest x2 49.7 us: stencil_grad(): terms.append(jnp.sum(widened * window, axis=(0, 1, 2, 3)))]
    convert_element_type x3 -> x0, other arithmetic: 42 us -> none  [the longest x1 22.4 us: block_pass(): conv_second = stencil_apply(padded_mid, stencils[1]).astype(jnp.bfloat16)]
    scatter-add x11 -> x0, other arithmetic: 36.7 us -> none  [the longest x2 12.4 us: send_back(): rim_grad = rim_grad.at[:, send_rim].add(returned)]
    mul x7 -> x0, other arithmetic: 33.1 us -> none  [the longest x2 30.2 us: stencil_back(): kernel[3 * row_at + col_at] * widened]
    add x3 -> x2, other arithmetic: 30.8 us -> 1.46 us  [the longest x1 0.74 us: whole_block(): part + lax.ppermute(part, 'batch', [(i, i ^ step) for i in range(batch)])]
    all_to_all x5 -> x2, starting transfers between devices: 36.4 us -> 13.3 us  [exchange(): return lax.all_to_all(array, TILE, split_axis=0, concat_axis=0, tiled=True)]
    select_n x17 -> x0, other arithmetic: 22 us -> none  [the longest x2 4.89 us: send_back(): jnp.where(mail_live[None, :, None, None], jnp.take(parts, mail_entry, axi...]
  transfers between devices with their start and end apart: 5 -> 4, of which waited for: 3 -> 4; matrix products, arithmetic and copies ran while one was open for 20% -> 1% of each run, Pallas kernels for 0% -> 7%
where the time goes in v1:
time: 141 us; the launch traced here: 140 us
  Pallas kernels  59.1 us (42%)
  blocking collectives  31.6 us (22%)
  waiting for transfers between devices  24.7 us (18%)
  starting transfers between devices  17.3 us (12%)
  local copies, waits for them, and re-layouts  5.4 us (4%)
  other arithmetic  1.46 us (1%)
    all_to_all x2, blocking collectives, exchange(): return lax.all_to_all(array, TILE, split_axis=0, concat_axis=0, tiled=True)  31.6 us
    all_to_all x2, waiting for transfers between devices, exchange(): return lax.all_to_all(array, TILE, split_axis=0, concat_axis=0, tiled=True)  21.5 us
    pallas_call x1, Pallas kernels, whole_block(): call(middle_kernel, [field, field, field, field, rims16, lines16, shape_o...  16.5 us
    pallas_call x1, Pallas kernels, whole_block(): call(weight_kernel, [shape_of(groups, 24, 256), wide, wide], [pltpu.VMEM(...  14.6 us
    all_to_all x2, starting transfers between devices, exchange(): return lax.all_to_all(array, TILE, split_axis=0, concat_axis=0, tiled=True)  13.3 us
    pallas_call x1, Pallas kernels, whole_block(): call(last_kernel, [field, field], line_scratch + [pltpu.VMEM((128, S, 256...  9.32 us
    pallas_call x1, Pallas kernels, whole_block(): call(inner_kernel, [wide, wide, field], count=5)  8.31 us
    pallas_call x1, Pallas kernels, whole_block(): call(first_kernel, [shape_of(8, 128, dtype=I32), shape_of(64, 2 * S, 256)...  5.3 us
  transfers between devices with their start and end apart: 4, of which 4 were waited for; matrix products, arithmetic and copies ran while one was open for 1% of the time, Pallas kernels for 7%

profile of v1, /device:TPU:1, one launch (start us, length us, event | category | flops | bytes accessed | tf_op | source)
XLA Modules:
  0.0 140.1 jit_solution(11884827642065168069)
XLA Ops:
  0.6 0.7 multiply_add_fusion
  2.2 5.3 %shard_map.137 = (s32[8,128]{1,0:T(8,128)}, bf16[64,32,256]{2,1,0:T(8,128)(2,1)}, bf16[64,16,256]{2,1,0:T(8,128)(2,1)}, bf16[64,16,256]{2,1,0:T(8,128)(2,1)}) custom-call(s32[32,128]{1,0:T(8,128)} %pad.4.comb_ref, bf16[2048,256]{1,0:T(8,128)(2,1)} %bitcast.8, bf16[2048,256]{1,0:T(8,128)(2,1)} %bitcast.12, bf16[256,256]{1,0:T(8,128)(2,1)} %constant.10.clone.sel_ref), custom_call_target="tpu_custom_call" | custom-call | tf_op jit(solution)/shard_map/pallas_call | solution.py:542
  7.5 9.6 %all-to-all-start = ((bf16[32,64,256]{2,1,0:T(8,128)(2,1)}), bf16[32,64,256]{2,1,0:T(8,128)(2,1)S(1)}, u32[]{:S(2)}, u32[]{:S(2)}) async-start(bf16[32,64,256]{2,1,0:T(8,128)(2,1)} %bitcast.19), calls=%async_computation | async-start | bytes 2097152 | tf_op jit(solution)/shard_map/all_to_all | solution.py:524
  17.1 0.6 copy.22.stencils_ref
  17.8 8.3 %shard_map.138 = (f32[2048,256]{1,0:T(8,128)}, f32[2048,256]{1,0:T(8,128)}, bf16[2048,256]{1,0:T(8,128)(2,1)}) custom-call(bf16[2048,256]{1,0:T(8,128)(2,1)} %bitcast.9, bf16[2048,256]{1,0:T(8,128)(2,1)} %bitcast.13, bf16[2,256,256]{2,1,0:T(8,128)(2,1)} %mixers_ref.5, f32[2,9,256]{2,1,0:T(8,128)} %copy.22.stencils_ref, bf16[512,256]{1,0:T(8,128)(2,1)} %constant.12.clone.shift_ref), custom_call_target="tpu_custom_call" | custom-call | tf_op jit(solution)/shard_map/pallas_call | solution.py:549
  26.1 8.0 %all-to-all-done = bf16[32,64,256]{2,1,0:T(8,128)(2,1)S(1)} async-done(((bf16[32,64,256]{2,1,0:T(8,128)(2,1)}), bf16[32,64,256]{2,1,0:T(8,128)(2,1)S(1)}, u32[]{:S(2)}, u32[]{:S(2)}) %all-to-all-start) | async-done | bytes 1048608 | tf_op jit(solution)/shard_map/all_to_all | solution.py:524
  34.0 1.0 copy-done
  35.0 16.5 %shard_map.139 = (bf16[2048,256]{1,0:T(8,128)(2,1)}, bf16[2048,256]{1,0:T(8,128)(2,1)}, bf16[2048,256]{1,0:T(8,128)(2,1)}, bf16[2048,256]{1,0:T(8,128)(2,1)}, bf...) custom-call(s32[8,128]{1,0:T(8,128)} %get-tuple-element.30.tab_ref, ...), custom_call_target="tpu_custom_call" | custom-call | tf_op jit(solution)/shard_map/pallas_call | solution.py:559
  51.5 14.6 %shard_map.140 = (bf16[32,24,256]{2,1,0:T(8,128)(2,1)}, f32[2048,256]{1,0:T(8,128)}, f32[2048,256]{1,0:T(8,128)}) custom-call(s32[8,128]{1,0:T(8,128)} %get-tuple-element.30.tab_ref, bf16[2048,256]{1,0:T(8,128)(2,1)} %bitcast.10, bf16[2048,256]{1,0:T(8,128)(2,1)} %bitcast.14, bf16[2048,256]{1,0:T(8,128)(2,1)} %get-tuple-element.39.active_ref, ...), custom_call_target="tpu_custom_call" | custom-call | tf_op jit(solution)/shard_map/pallas_call | solution.py:567
  66.1 14.7 %all_to_all.20.in_ref = bf16[32,24,256]{2,1,0:T(8,128)(2,1)} all-to-all(bf16[32,24,256]{2,1,0:T(8,128)(2,1)} %get-tuple-element.51), channel_id=1, replica_groups=mesh['tile_0'=4,'tile_1'=4,'tile_2'=2,'batch'=4] {'tile_0','tile_1','til..., dimensions={0} | all-to-all | bytes 786432 | tf_op jit(solution)/shard_map/all_to_all | solution.py:524
  80.8 1.7 %shard_map.142 = f32[24,256]{1,0:T(8,128)} custom-call(bf16[32,24,256]{2,1,0:T(8,128)(2,1)} %all_to_all.20.in_ref), custom_call_target="tpu_custom_call" | custom-call | tf_op jit(solution)/shard_map/pallas_call | solution.py:594
  82.5 1.2 collective-permute-start
  83.7 1.7 %collective-permute-done = f32[24,256]{1,0:T(8,128)S(1)} collective-permute-done((f32[24,256]{1,0:T(8,128)}, f32[24,256]{1,0:T(8,128)S(1)}, u32[]{:S(2)}, u32[]{:S(2)}) %collective-permute-start) | collective-permute-done | bytes 24608 | tf_op jit(solution)/shard_map/ppermute | solution.py:597
  85.4 0.7 add.9.a_ref
  86.1 2.7 %collective-permute-start.1 = (f32[24,256]{1,0:T(8,128)S(1)}, f32[24,256]{1,0:T(8,128)S(1)}, u32[]{:S(2)}, u32[]{:S(2)}) collective-permute-start(f32[24,256]{1,0:T(8,128)S(1)} %add.9.a_ref), channel_id=1, source_target_pairs={{0,2},{1,3},{2,0},{3,1},{4,6},{5,7},{6,4},{7,5},{8,10},{9,11},{10,... | collective-permute-start | bytes 73736 | tf_op jit(solution)/shard_map/ppermute | solution.py:599
  88.9 1.4 %collective-permute-done.1.b_ref = f32[24,256]{1,0:T(8,128)S(1)} collective-permute-done((f32[24,256]{1,0:T(8,128)S(1)}, f32[24,256]{1,0:T(8,128)S(1)}, u32[]{:S(2)}, u32[]{:S(2)}) %collective-permute-start.1) | collective-permute-done | bytes 24608 | tf_op jit(solution)/shard_map/ppermute | solution.py:599
  90.9 1.5 %shard_map.143 = bf16[32,24,256]{2,1,0:T(8,128)(2,1)} custom-call(f32[24,256]{1,0:T(8,128)} %copy-done.2, f32[24,256]{1,0:T(8,128)} %copy-done.3), custom_call_target="tpu_custom_call" | custom-call | tf_op jit(solution)/shard_map/pallas_call | solution.py:600
  92.4 16.8 %all_to_all.21.refs_0_ = bf16[32,24,256]{2,1,0:T(8,128)(2,1)} all-to-all(bf16[32,24,256]{2,1,0:T(8,128)(2,1)} %shard_map.143), channel_id=1, replica_groups=mesh['tile_0'=4,'tile_1'=4,'tile_2'=2,'batch'=4] {'tile_0','tile_1','til..., dimensions={0} | all-to-all | bytes 786432 | tf_op jit(solution)/shard_map/all_to_all | solution.py:524
  109.3 3.7 %all-to-all-start.1 = ((bf16[32,64,256]{2,1,0:T(8,128)(2,1)}), bf16[32,64,256]{2,1,0:T(8,128)(2,1)S(1)}, u32[]{:S(2)}, u32[]{:S(2)}) async-start(bf16[32,64,256]{2,1,0:T(8,128)(2,1)} %bitcast.4), calls=%async_computation.1 | async-start | bytes 2097152 | tf_op jit(solution)/shard_map/all_to_all | solution.py:524
  113.0 1.8 %shard_map.144 = (f32[2,256,256]{2,1,0:T(8,128)}, f32[2,9,256]{2,1,0:T(8,128)}, f32[2,256]{1,0:T(2,128)}) custom-call(bf16[32,24,256]{2,1,0:T(8,128)(2,1)} %all_to_all.21.refs_0_), custom_call_target="tpu_custom_call" | custom-call | tf_op jit(solution)/shard_map/pallas_call | solution.py:607
  114.8 1.4 copy.26
  116.2 13.6 %all-to-all-done.1 = bf16[32,64,256]{2,1,0:T(8,128)(2,1)S(1)} async-done(((bf16[32,64,256]{2,1,0:T(8,128)(2,1)}), bf16[32,64,256]{2,1,0:T(8,128)(2,1)S(1)}, u32[]{:S(2)}, u32[]{:S(2)}) %all-to-all-start.1) | async-done | bytes 1048608 | tf_op jit(solution)/shard_map/all_to_all | solution.py:524
  129.8 1.0 copy-done.1
  130.8 9.3 %shard_map.141 = (bf16[2048,256]{1,0:T(8,128)(2,1)}, bf16[2048,256]{1,0:T(8,128)(2,1)}) custom-call(s32[8,128]{1,0:T(8,128)} %get-tuple-element.30.tab_ref, bf16[64,32,256]{2,1,0:T(8,128)(2,1)} %bitcast.18, bf16[64,16,256]{2,1,0:T(8,128)(2,1)} %get-tuple-element.37.rims_ref.rims_in_ref, bf16[64,16,256]{2,1,0:T(8,128)(2,1)} %get-tuple-element.38.own_in_ref, ...), custom_call_target="tpu_custom_call" | custom-call | tf_op jit(solution)/shard_map/pallas_call | solution.py:587
  (11 shorter events, 1.5 us)
Async XLA Ops:
  2.2 14.9 %copy-start.4 = (f32[2,9,256]{2,0,1:T(2,128)S(1)}, f32[2,9,256]{2,0,1:T(2,128)}, u32[]{:S(2)}) copy-start(f32[2,9,256]{2,0,1:T(2,128)} %param.15) | copy-start | bytes 55300
  7.5 26.5 %all-to-all-start = ((bf16[32,64,256]{2,1,0:T(8,128)(2,1)}), bf16[32,64,256]{2,1,0:T(8,128)(2,1)S(1)}, u32[]{:S(2)}, u32[]{:S(2)}) async-start(bf16[32,64,256]{2,1,0:T(8,128)(2,1)} %bitcast.19), calls=%async_computation | async-start | bytes 2097152 | tf_op jit(solution)/shard_map/all_to_all | solution.py:524
  34.0 1.0 copy-start
  82.5 2.9 %collective-permute-start = (f32[24,256]{1,0:T(8,128)}, f32[24,256]{1,0:T(8,128)S(1)}, u32[]{:S(2)}, u32[]{:S(2)}) collective-permute-start(f32[24,256]{1,0:T(8,128)} %shard_map.142), channel_id=1, source_target_pairs={{0,1},{1,0},{2,3},{3,2},{4,5},{5,4},{6,7},{7,6},{8,9},{9,8},{10,11... | collective-permute-start | bytes 73736 | tf_op jit(solution)/shard_map/ppermute | solution.py:597
  86.1 4.2 %copy-start.2 = (f32[24,256]{1,0:T(8,128)}, f32[24,256]{1,0:T(8,128)S(1)}, u32[]{:S(2)}) copy-start(f32[24,256]{1,0:T(8,128)S(1)} %add.9.a_ref) | copy-start | bytes 73732
  86.1 4.2 %collective-permute-start.1 = (f32[24,256]{1,0:T(8,128)S(1)}, f32[24,256]{1,0:T(8,128)S(1)}, u32[]{:S(2)}, u32[]{:S(2)}) collective-permute-start(f32[24,256]{1,0:T(8,128)S(1)} %add.9.a_ref), channel_id=1, source_target_pairs={{0,2},{1,3},{2,0},{3,1},{4,6},{5,7},{6,4},{7,5},{8,10},{9,11},{10,... | collective-permute-start | bytes 73736 | tf_op jit(solution)/shard_map/ppermute | solution.py:599
  90.3 0.6 copy-start.3
  109.3 20.5 %all-to-all-start.1 = ((bf16[32,64,256]{2,1,0:T(8,128)(2,1)}), bf16[32,64,256]{2,1,0:T(8,128)(2,1)S(1)}, u32[]{:S(2)}, u32[]{:S(2)}) async-start(bf16[32,64,256]{2,1,0:T(8,128)(2,1)} %bitcast.4), calls=%async_computation.1 | async-start | bytes 2097152 | tf_op jit(solution)/shard_map/all_to_all | solution.py:524
  129.8 1.0 copy-start.1

commit v2 on v1

v2 whole, which is shorter than its diff:
```python
import math

import jax
import jax.numpy as jnp
import numpy as np
from jax import lax
from jax.experimental import pallas as pl
from jax.experimental.pallas import tpu as pltpu
from jax.sharding import Mesh
from jax.sharding import PartitionSpec as P


TILE = ("tile_0", "tile_1", "tile_2")
SQRT_HALF = 0.7071067811865476
INV_ROOT_TAU = 0.3989422804014327

F32 = jnp.float32
BF16 = jnp.bfloat16
I32 = jnp.int32

S = 16
T = 8
CELLS = S * S
SIDE_TAPS = {0: (0, 1, 2), 1: (2, 5, 8), 2: (6, 7, 8), 3: (0, 3, 6)}
CORNER_TAP = {4: 2, 5: 8, 6: 6, 7: 0}


def line_cell(d, i):
    if d == 0:
        return i
    if d == 1:
        return S * i + S - 1
    if d == 2:
        return S * (S - 1) + i
    if d == 3:
        return S * i
    if i != 0:
        return None
    return {4: S - 1, 5: CELLS - 1, 6: S * (S - 1), 7: 0}[d]


def selection():
    sel = np.zeros((256, CELLS), np.float32)
    for d in range(8):
        for f in range(2):
            for i in range(S):
                cell = line_cell(d, S - 1 - i if f else i)
                if cell is not None:
                    sel[(2 * d + f) * S + i, cell] = 1.0
    return sel


def spreading():
    out = np.zeros((CELLS, 128), np.float32)
    for d in range(4):
        for i in range(S):
            out[line_cell(d, i), d * S + i] = 1.0
            out[line_cell(d, i), 64 + d * S + i] = 1.0
    return out


def shifting():
    out = np.zeros((512, CELLS), np.float32)
    for i in range(S):
        for j in range(S):
            if j > 0:
                out[S * i + j, S * i + j - 1] = 1.0
            if j < S - 1:
                out[256 + S * i + j, S * i + j + 1] = 1.0
    return out


def dot(a, b):
    return jnp.dot(a, b, preferred_element_type=F32)


def dot_t(a, b):
    return lax.dot_general(a, b, (((1,), (1,)), ((), ())), preferred_element_type=F32)


def t_dot(a, b):
    return lax.dot_general(a, b, (((0,), (0,)), ((), ())), preferred_element_type=F32)


def iota(shape, axis):
    return lax.broadcasted_iota(I32, shape, axis)


def neighbours(x):
    place = iota(x.shape, 0)
    before = jnp.where(place == 0, 0.0, pltpu.roll(x, 1, 0))
    after = jnp.where(place == S - 1, 0.0, pltpu.roll(x, S - 1, 0))
    return before, after


def down(x):
    return jnp.concatenate([jnp.zeros((S, x.shape[1]), x.dtype), x[: CELLS - S]], axis=0)


def up(x):
    return jnp.concatenate([x[S:], jnp.zeros((S, x.shape[1]), x.dtype)], axis=0)


def conv_inner(left, centre, right, w):
    rows = [w[3 * a] * left + w[3 * a + 1] * centre + w[3 * a + 2] * right for a in range(3)]
    return rows[1] + down(rows[0]) + up(rows[2])


def back_inner(left, centre, right, w):
    rows = [w[3 * a] * right + w[3 * a + 1] * centre + w[3 * a + 2] * left for a in range(3)]
    return rows[1] + up(rows[0]) + down(rows[2])


def tap_rows(ref, layer):
    return [ref[k, layer : layer + 1, :] for k in range(9)]


def fill_tap_sets(taps_ref, stencil_ref, layer):
    w = tap_rows(stencil_ref, layer)
    zero = jnp.zeros_like(w[0])
    for d in range(8):
        if d < 4:
            three = [w[k] for k in SIDE_TAPS[d]]
        else:
            three = [zero, w[CORNER_TAP[d]], zero]
        for f in range(2):
            for m, row in enumerate(three[::-1] if f else three):
                taps_ref[2 * d + f, m : m + 1, :] = row


def tile_of(ref, t):
    return ref[pl.ds(pl.multiple_of(t * CELLS, CELLS), CELLS), :]


def put_tile(ref, t, value):
    ref[pl.ds(pl.multiple_of(t * CELLS, CELLS), CELLS), :] = value


def split_store(ref, t, first, value):
    high = value.astype(BF16)
    ref[t, pl.ds(first, value.shape[0]), :] = high
    ref[t, pl.ds(64 + first, value.shape[0]), :] = (value - high.astype(F32)).astype(BF16)


def forward_lines(split_ref, buf_ref, tab_ref, w):
    def one(t, carry):
        corner = {}
        for d in range(4, 8):
            row = buf_ref[tab_ref[0, t * 8 + d]][:8, :].astype(F32)[:1, :]
            corner[d] = w[CORNER_TAP[d]] * row
        for d in range(4):
            x = buf_ref[tab_ref[0, t * 8 + d]].astype(F32)
            before, after = neighbours(x)
            a, b, c = SIDE_TAPS[d]
            line = w[a] * before + w[b] * x + w[c] * after
            at = iota(line.shape, 0)
            if d == 0:
                line = line + jnp.where(at == 0, corner[7], 0.0)
                line = line + jnp.where(at == S - 1, corner[4], 0.0)
            if d == 2:
                line = line + jnp.where(at == 0, corner[6], 0.0)
                line = line + jnp.where(at == S - 1, corner[5], 0.0)
            split_store(split_ref, t, d * S, line)
        return carry

    lax.fori_loop(0, T, one, 0, unroll=2)


def rim_gradients(rim_ref, lines_ref, tab_ref, taps_ref, first, count):
    def one(i, carry):
        x = lines_ref[i].astype(F32)
        before, after = neighbours(x)
        u = taps_ref[tab_ref[3, first + i]]
        rim = tab_ref[2, first + i] >> 1
        rim_ref[rim] += u[0:1] * after + u[1:2] * x + u[2:3] * before
        return carry

    lax.fori_loop(0, count, one, 0, unroll=8)


def split_rims(split_ref, rim_ref):
    def split(t, carry):
        for e in range(4):
            split_store(split_ref, t, e * S, rim_ref[t * 4 + e])
        return carry

    lax.fori_loop(0, T, split, 0, unroll=2)


def live_lines(dst_ref, dst_first, src_ref, offset, tab_ref, tab_first):
    def one(i, carry):
        line = src_ref[i, offset : offset + S]
        live = tab_ref[4, tab_first + i] > 0
        dst_ref[dst_first + i] = jnp.where(live, line, jnp.zeros((S, 256), BF16))
        return carry

    lax.fori_loop(0, 64, one, 0, unroll=8)


def line_grads(g_ref, c_ref, mixers_ref):
    for b in range(4):
        part = c_ref[b * 16 : b * 16 + 16].reshape(256, 256)
        g_ref[b * 16 : b * 16 + 16] = dot_t(part, mixers_ref[1]).astype(BF16).reshape(16, S, 256)


def gather_out(leave, ports, out_ref, own_ref, rims_ref, lines_ref, tab_ref):
    def some(q, carry):
        for r in range(16):
            s = q * 16 + r
            out_ref[s, 0:S] = rims_ref[tab_ref[2, 64 + s]]
            out_ref[s, S : 2 * S] = lines_ref[tab_ref[1, s]]
            own_ref[s] = lines_ref[tab_ref[5, s]]
        leave(ports[0], q * 16, 16)
        leave(ports[1], q * 16, 16)
        return carry

    lax.fori_loop(0, 4, some, 0)


def banks(rims_ref, lines_ref, rim_field, line_field, sel_ref):
    def one(t, carry):
        rims = dot(sel_ref[0:128, :], tile_of(rim_field, t)).astype(BF16)
        rims_ref[pl.ds(t * 8, 8)] = rims.reshape(8, S, 256)
        lines = dot(sel_ref[...], tile_of(line_field, t)).astype(BF16)
        lines_ref[pl.ds(t * 16, 16)] = lines.reshape(16, S, 256)
        return carry

    lax.fori_loop(0, T, one, 0)


def own_position():
    a, b, c = (lax.axis_index(name) for name in TILE)
    return (a * lax.axis_size(TILE[1]) + b) * lax.axis_size(TILE[2]) + c


def first_kernel(
    arrive, leave, comb_ref, states_ref, cot_ref, sel_ref, tab_ref, out_ref, rims_ref, own_ref, lines_ref, smem, sem
):
    me = own_position()
    comb = comb_ref[...]
    lane = iota(comb.shape, 1)
    home = iota(comb.shape, 0)
    slot = comb >> 3
    wanted = (lane < 64) & ((slot >> 3) == me) & (home != me)
    wanted_f = wanted.astype(F32)
    before = (iota((128, 128), 0) < iota((128, 128), 1)).astype(F32).astype(BF16)
    place = dot(wanted_f.astype(BF16), before)
    code = comb & 7
    rim_code = (slot & 7) * 8 + code
    tap_set = (lane & 7) * 2 + (code & 1)
    packed = (rim_code * 16 + tap_set + 1024).astype(F32)
    asked = jnp.zeros((1, 128), F32)
    for k in range(2):
        value = jnp.sum(
            jnp.where(wanted & (place == k), packed, 0.0), axis=1, keepdims=True
        )
        at = (lane >= 64) & (((lane - 64) >> 1) == home) & ((lane & 1) == k)
        asked = asked + jnp.sum(jnp.where(at, value, 0.0), axis=0, keepdims=True)
    asked = asked.astype(I32)

    own = comb_ref[pl.ds(me, 1), :]
    sub2 = iota((128, 128), 0)
    lane2 = iota((128, 128), 1)
    own_wide = jnp.broadcast_to(own, (128, 128))
    own_col = jnp.sum(
        jnp.where(sub2 == lane2, own_wide, 0).astype(F32), axis=1, keepdims=True
    ).astype(I32)
    owner_col = own_col >> 6
    owner_row = own >> 6
    same = (owner_col == owner_row) & (sub2 < 64) & (lane2 < 64)
    place_col = jnp.sum((same & (lane2 < sub2)).astype(F32), axis=1, keepdims=True).astype(I32)
    place_row = jnp.sum((same & (sub2 < lane2)).astype(F32), axis=0, keepdims=True).astype(I32)
    lane1 = iota((1, 128), 1)
    sub1 = iota((128, 1), 0)
    remote_row = owner_row != me
    slot_col = jnp.where((owner_col != me) & (sub1 < 64), owner_col * 2 + place_col, -1)
    line_col = (sub1 * 2 + (own_col & 1)).astype(F32)
    sent = jnp.sum(jnp.where(slot_col == lane2, line_col, 0.0), axis=0, keepdims=True).astype(I32)
    own_rim = (own & 511)
    own_rim = ((own_rim >> 3) & 7) * 8 + (own_rim & 7)
    in_own = lane1 < 64
    panel = jnp.where(remote_row, 64 + owner_row * 2 + place_row, own_rim)
    tab_ref[...] = jnp.zeros_like(tab_ref)
    tab_ref[0:1, :] = jnp.where(in_own, panel, 0)
    tab_ref[1:2, :] = jnp.where(in_own, sent, 0)
    tab_ref[2:3, :] = jnp.where(in_own, own_rim, (asked & 1023) >> 4)
    tab_ref[3:4, :] = jnp.where(in_own, (lane1 & 7) * 2 + (own & 1), asked & 15)
    tab_ref[4:5, :] = jnp.where(in_own, (~remote_row).astype(I32), asked >> 10)
    tab_ref[5:6, :] = jnp.where(in_own, lane1 * 2 + (own & 1), 0)
    copy = pltpu.make_async_copy(tab_ref, smem, sem)
    copy.start()
    arrive(1)
    arrive(2)
    banks(rims_ref, lines_ref, states_ref, cot_ref, sel_ref)
    leave(2, 0, 64)
    copy.wait()
    gather_out(leave, (1, 3), out_ref, own_ref, rims_ref, lines_ref, smem)


def inner_kernel(
    arrive, leave, tab_ref, states_ref, cot_ref, own_in_ref, mixers_ref, stencils_ref, shift_ref,
    conv_ref, back_ref, g_ref, c_ref, gl_ref, rim_ref, taps_ref,
):
    w0 = tap_rows(stencils_ref, 0)
    w1 = tap_rows(stencils_ref, 1)
    arrive(1)
    arrive(2)

    def one(t, carry):
        x = tile_of(states_ref, t)
        moved = dot(shift_ref[...], x)
        put_tile(conv_ref, t, conv_inner(moved[:CELLS], x.astype(F32), moved[CELLS:], w0))
        leave(0, t * CELLS, CELLS)
        g = dot_t(tile_of(cot_ref, t), mixers_ref[1]).astype(BF16)
        put_tile(g_ref, t, g)
        leave(2, t * CELLS, CELLS)
        moved = dot(shift_ref[...], g)
        put_tile(back_ref, t, back_inner(moved[:CELLS], g.astype(F32), moved[CELLS:], w1))
        leave(1, t * CELLS, CELLS)
        return carry

    lax.fori_loop(0, T, one, 0)
    arrive(3)
    fill_tap_sets(taps_ref, stencils_ref, 1)
    live_lines(c_ref, 0, own_in_ref, 0, tab_ref, 0)
    leave(3, 0, 64)
    line_grads(gl_ref, c_ref, mixers_ref)
    leave(4, 0, 64)
    rim_ref[...] = jnp.zeros_like(rim_ref)
    rim_gradients(rim_ref, gl_ref, tab_ref, taps_ref, 0, 64)
    leave(5, 0, 32)


def middle_kernel(
    arrive, leave,
    tab_ref, in_ref, rims_in_ref, rim_ref, conv_ref, back_ref, mixers_ref, stencils_ref,
    shifts_ref, sel_ref, spread_ref,
    active_ref, first_ref, gh_ref, gc_ref, rims_ref, lines_ref, out_ref, own_ref, c_ref, g_ref,
    buf_ref, split_ref, split2_ref, taps_ref,
):
    w0 = tap_rows(stencils_ref, 0)
    fill_tap_sets(taps_ref, stencils_ref, 1)
    buf_ref[64:128] = in_ref[:, 0:S, :]
    live_lines(c_ref, 0, in_ref, S, tab_ref, 64)
    leave(8, 0, 64)
    line_grads(g_ref, c_ref, mixers_ref)
    leave(9, 0, 64)
    arrive(2)
    buf_ref[0:64] = rims_in_ref[...]
    forward_lines(split_ref, buf_ref, tab_ref, w0)
    arrive(3)
    rim_gradients(rim_ref, g_ref, tab_ref, taps_ref, 64, 64)
    split_rims(split2_ref, rim_ref)
    arrive(4)
    arrive(5)

    def one(t, carry):
        first = (tile_of(conv_ref, t) + dot(spread_ref[...], split_ref[t])).astype(BF16)
        put_tile(first_ref, t, first)
        leave(1, t * CELLS, CELLS)
        hidden = dot(first, mixers_ref[0]) + shifts_ref[0:1, :]
        cdf = 0.5 * (1.0 + lax.erf(hidden * SQRT_HALF))
        active = (hidden * cdf).astype(BF16)
        put_tile(active_ref, t, active)
        leave(0, t * CELLS, CELLS)
        slope = cdf + hidden * jnp.exp(-0.5 * hidden * hidden) * INV_ROOT_TAU
        grad = tile_of(back_ref, t) + dot(spread_ref[...], split2_ref[t])
        gh = (grad * slope).astype(BF16)
        put_tile(gh_ref, t, gh)
        leave(2, t * CELLS, CELLS)
        gc = dot_t(gh, mixers_ref[0]).astype(BF16)
        put_tile(gc_ref, t, gc)
        leave(3, t * CELLS, CELLS)
        return carry

    lax.fori_loop(0, T, one, 0, unroll=2)
    banks(rims_ref, lines_ref, active_ref, gc_ref, sel_ref)
    leave(4, 0, 64)
    leave(5, 0, 128)
    gather_out(leave, (6, 7), out_ref, own_ref, rims_ref, lines_ref, tab_ref)


def weight_kernel(
    arrive, leave,
    tab_ref, states_ref, cot_ref, active_ref, first_ref, gh_ref, gc_ref, g2_ref, rims_ref, lines_ref,
    rims_in_ref, in_ref, c_own_ref, g_own_ref, c_in_ref, g_in_ref, stencils_ref, shift_ref,
    pack_ref, conv_ref,
    second_ref, h_ref, taps_ref, acc1_ref, acc2_ref, accl_ref, sums_ref,
):
    w1 = tap_rows(stencils_ref, 1)
    acc1_ref[...] = jnp.zeros_like(acc1_ref)
    acc2_ref[...] = jnp.zeros_like(acc2_ref)
    accl_ref[...] = jnp.zeros_like(accl_ref)
    sums_ref[...] = jnp.zeros_like(sums_ref)
    fill_tap_sets(taps_ref, stencils_ref, 1)

    def folded(x):
        return jnp.sum(x.reshape(-1, 8, 256), axis=0)

    def taps_of(acc_ref, g, left, centre, right):
        for b, x in enumerate((left, centre, right)):
            acc_ref[b] += folded(g[S:] * x[: CELLS - S])
            acc_ref[3 + b] += folded(g * x)
            acc_ref[6 + b] += folded(g[: CELLS - S] * x[S:])

    def halves(x):
        return x[0:8] + x[8:16]

    def second_halo(source_ref):
        def one(i, carry):
            x = rims_ref[(tab_ref[2, i] >> 1) * 2].astype(F32)
            g = source_ref[i & 63].astype(F32)
            before, after = neighbours(x)
            kind = tab_ref[3, i]
            u = taps_ref[kind]
            h_ref[i] = (u[0:1] * before + u[1:2] * x + u[2:3] * after).astype(BF16)
            for m, y in enumerate((before, x, after)):
                accl_ref[kind, m] += halves(g * y)
            return carry

        return one

    arrive(8)
    arrive(13)
    lax.fori_loop(0, 64, second_halo(g_own_ref), 0, unroll=8)
    arrive(15)
    lax.fori_loop(64, 128, second_halo(g_in_ref), 0, unroll=8)

    for k in (9, 10, 11):
        arrive(k)

    def first_halo(t, carry):
        for d in range(8):
            place = tab_ref[0, t * 8 + d]
            own = rims_in_ref[jnp.minimum(place, 63)]
            sent = in_ref[jnp.maximum(place - 64, 0), 0:S]
            x = jnp.where(place < 64, own, sent).astype(F32)
            g = lines_ref[(t * 8 + d) * 2].astype(F32)
            if d < 4:
                before, after = neighbours(x)
                for k, y in zip(SIDE_TAPS[d], (before, x, after)):
                    acc1_ref[k] += halves(g * y)
            else:
                acc1_ref[CORNER_TAP[d]] += halves(g * x)
        return carry

    lax.fori_loop(0, T, first_halo, 0, unroll=2)

    for k in (6, 1, 3, 7, 5, 2):
        arrive(k)

    def one(t, carry):
        gcf = tile_of(gc_ref, t).astype(F32)
        x = tile_of(states_ref, t)
        moved = dot(shift_ref[...], x)
        taps_of(acc1_ref, gcf, moved[:CELLS], x.astype(F32), moved[CELLS:])
        x = tile_of(active_ref, t)
        moved = dot(shift_ref[...], x)
        xf = x.astype(F32)
        second = conv_inner(moved[:CELLS], xf, moved[CELLS:], w1)
        put_tile(conv_ref, t, second)
        leave(1, t * CELLS, CELLS)
        put_tile(second_ref, t, second.astype(BF16))
        taps_of(acc2_ref, tile_of(g2_ref, t).astype(F32), moved[:CELLS], xf, moved[CELLS:])
        sums_ref[0] += folded(tile_of(gh_ref, t).astype(F32))
        sums_ref[1] += folded(tile_of(cot_ref, t).astype(F32))
        return carry

    lax.fori_loop(0, T, one, 0)
    for k in (4, 12, 14):
        arrive(k)
    for d in range(8):
        for f in range(2):
            if d < 4:
                taps = SIDE_TAPS[d][::-1] if f else SIDE_TAPS[d]
                for m, k in enumerate(taps):
                    acc2_ref[k] += accl_ref[2 * d + f, m]
            else:
                acc2_ref[CORNER_TAP[d]] += accl_ref[2 * d + f, 1]

    rows = [jnp.sum(acc1_ref[k], axis=0, keepdims=True) for k in range(9)]
    rows += [jnp.sum(acc2_ref[k], axis=0, keepdims=True) for k in range(9)]
    rows += [jnp.sum(sums_ref[k], axis=0, keepdims=True) for k in range(2)]
    rows += [jnp.zeros_like(rows[0])] * 4
    for r in range(3):
        pack_ref[r, 16:24] = jnp.concatenate(rows[8 * r : 8 * r + 8], axis=0).astype(BF16)
    for r in range(3, pack_ref.shape[0]):
        pack_ref[r, 16:24] = jnp.zeros((8, 256), BF16)
    half = pack_ref.shape[0] // 2
    mixer_first = t_dot(first_ref[...], gh_ref[...])
    for r in range(half):
        pack_ref[r, 0:16] = mixer_first[16 * r : 16 * r + 16].astype(BF16)
    leave(0, 0, half)
    mixer_second = (
        t_dot(second_ref[...], cot_ref[...])
        + t_dot(h_ref[0:64].reshape(1024, 256), c_own_ref[...].reshape(1024, 256))
        + t_dot(h_ref[64:128].reshape(1024, 256), c_in_ref[...].reshape(1024, 256))
    )
    for r in range(half):
        pack_ref[half + r, 0:16] = mixer_second[16 * r : 16 * r + 16].astype(BF16)
    leave(0, half, half)


def back_kernel(arrive, leave, gc_ref, stencils_ref, shift_ref, back_ref):
    w0 = tap_rows(stencils_ref, 0)
    arrive(0)

    def one(t, carry):
        gc = tile_of(gc_ref, t)
        moved = dot(shift_ref[...], gc)
        put_tile(back_ref, t, back_inner(moved[:CELLS], gc.astype(F32), moved[CELLS:], w0))
        leave(0, t * CELLS, CELLS)
        return carry

    lax.fori_loop(0, T, one, 0, unroll=2)


def outcome_kernel(
    arrive, leave,
    tab_ref, in_ref, rims_in_ref, conv_ref, states_ref, mixers_ref, stencils_ref, shifts_ref, spread_ref,
    outcome_ref,
    buf_ref, split_ref,
):
    w1 = tap_rows(stencils_ref, 1)
    arrive(2)
    buf_ref[0:64] = rims_in_ref[...]
    arrive(1)
    buf_ref[64:128] = in_ref[:, 0:S, :]
    forward_lines(split_ref, buf_ref, tab_ref, w1)
    arrive(3)
    arrive(4)

    def one(t, carry):
        second = (tile_of(conv_ref, t) + dot(spread_ref[...], split_ref[t])).astype(BF16)
        out = tile_of(states_ref, t).astype(F32) + dot(second, mixers_ref[1]) + shifts_ref[1:2, :]
        put_tile(outcome_ref, t, out.astype(BF16))
        leave(0, t * CELLS, CELLS)
        return carry

    lax.fori_loop(0, T, one, 0, unroll=2)


def grad_kernel(
    arrive, leave,
    tab_ref, in_ref, own_in_ref, back_ref, cot_ref, stencils_ref, spread_ref,
    grad_ref,
    lines_ref, split_ref, rim_ref, taps_ref,
):
    fill_tap_sets(taps_ref, stencils_ref, 0)
    rim_ref[...] = jnp.zeros_like(rim_ref)
    arrive(2)
    live_lines(lines_ref, 0, own_in_ref, 0, tab_ref, 0)
    arrive(1)
    live_lines(lines_ref, 64, in_ref, S, tab_ref, 64)
    rim_gradients(rim_ref, lines_ref, tab_ref, taps_ref, 0, 128)
    split_rims(split_ref, rim_ref)
    arrive(3)
    arrive(4)

    def one(t, carry):
        grad = tile_of(back_ref, t) + dot(spread_ref[...], split_ref[t])
        put_tile(grad_ref, t, (tile_of(cot_ref, t).astype(F32) + grad).astype(BF16))
        leave(0, t * CELLS, CELLS)
        return carry

    lax.fori_loop(0, T, one, 0, unroll=2)


def sum_kernel(arrive, leave, in_ref, out_ref):
    total = in_ref[0].astype(F32)
    for r in range(1, in_ref.shape[0]):
        total = total + in_ref[r].astype(F32)
    for r in range(out_ref.shape[0]):
        out_ref[r] = total.astype(BF16)


def spread_kernel(arrive, leave, in_ref, out_ref):
    total = in_ref[0].astype(F32)
    for r in range(1, in_ref.shape[0]):
        total = total + in_ref[r].astype(F32)
    value = total.astype(BF16)
    for r in range(out_ref.shape[0]):
        out_ref[r] = value


def unpack_kernel(scale, arrive, leave, in_ref, mixer_ref, stencil_ref, shift_ref):
    half = in_ref.shape[0] // 2
    for k in range(2):
        for r in range(half):
            mixer_ref[k, 16 * r : 16 * r + 16, :] = in_ref[k * half + r, 0:16].astype(F32) * scale
        leave(0, k, 1)
    rows = [in_ref[r, 16:24].astype(F32) * scale for r in range(3)]
    rows = [row for block in rows for row in jnp.split(block, 8, axis=0)]
    for k in range(2):
        for j in range(9):
            stencil_ref[j, k : k + 1, :] = rows[9 * k + j]
        shift_ref[k : k + 1, :] = rows[18 + k]


def shape_of(*dims, dtype=BF16):
    return jax.ShapeDtypeStruct(dims, dtype)


def call(body, ins, in_modes, outs, out_modes, scratch=(), limit=60.0, order=None):
    spaces = {"s": pltpu.SMEM, "v": pltpu.VMEM, "h": pltpu.HBM}
    ports_in = order or [k for k, mode in enumerate(in_modes) if mode == "h"]
    ports_out = [k for k, mode in enumerate(out_modes) if mode == "h"]
    n_in, n_out, n_own = len(ins), len(outs), len(scratch)

    def kernel(*refs):
        in_refs = list(refs[:n_in])
        out_refs = list(refs[n_in : n_in + n_out])
        rest = list(refs[n_in + n_out :])
        own, rest = rest[:n_own], rest[n_own:]
        sem_in, sem_out = rest[-2:]
        inward, outward = {}, {}
        for q, k in enumerate(ports_in):
            inward[k] = pltpu.make_async_copy(in_refs[k], rest[q], sem_in.at[q])
            inward[k].start()
            in_refs[k] = rest[q]
        for q, k in enumerate(ports_out):
            buffer = rest[len(ports_in) + q]
            outward[k] = (buffer, out_refs[k], sem_out.at[q])
            out_refs[k] = buffer

        def arrive(k):
            if k in inward:
                inward[k].wait()

        def leave(k, first, count):
            if k in outward:
                source, target, sem = outward[k]
                part = pl.ds(first, count)
                pltpu.make_async_copy(source.at[part], target.at[part], sem).start()

        body(arrive, leave, *in_refs, *out_refs, *own)
        for source, target, sem in outward.values():
            pltpu.make_async_copy(source, target, sem).wait()

    buffers = [pltpu.VMEM(ins[k].shape, ins[k].dtype) for k in ports_in]
    buffers += [pltpu.VMEM(outs[k].shape, outs[k].dtype) for k in ports_out]
    sems = [pltpu.SemaphoreType.DMA((max(1, len(p)),)) for p in (ports_in, ports_out)]
    return pl.pallas_call(
        kernel,
        out_shape=[
            pltpu.HBM(o.shape, o.dtype) if m == "h" else o for o, m in zip(outs, out_modes)
        ],
        in_specs=[pl.BlockSpec(memory_space=spaces[m]) for m in in_modes],
        out_specs=[pl.BlockSpec(memory_space=spaces[m]) for m in out_modes],
        scratch_shapes=list(scratch) + buffers + sems,
        compiler_params=pltpu.CompilerParams(vmem_limit_bytes=int(limit * 1024 * 1024)),
    )(*ins)


def exchange(array):
    return lax.all_to_all(array, TILE, split_axis=0, concat_axis=0, tiled=True)


def whole_block(states, cotangent, beside_slot, beside_code, mixers, stencils, shifts):
    groups = lax.axis_size(TILE)
    batch = lax.axis_size("batch")
    shape = states.shape
    x = states.reshape(T * CELLS, 256)
    cot = cotangent.reshape(T * CELLS, 256)
    comb = (beside_slot * 8 + beside_code).astype(I32).reshape(groups, 64)
    comb = jnp.pad(comb, ((0, 0), (0, 64)))
    sel = jnp.asarray(selection(), BF16)
    spread = jnp.asarray(spreading(), BF16)
    shift = jnp.asarray(shifting(), BF16)
    taps = stencils.swapaxes(0, 1)
    lines16 = shape_of(128, S, 256)
    rims16 = shape_of(64, S, 256)
    sent16 = shape_of(64, 2 * S, 256)
    field = shape_of(T * CELLS, 256)
    wide = shape_of(T * CELLS, 256, dtype=F32)
    lines_scratch = pltpu.VMEM((128, S, 256), BF16)
    split_scratch = pltpu.VMEM((T, 128, 256), BF16)
    rim_scratch = pltpu.VMEM((32, S, 256), F32)
    taps_scratch = pltpu.VMEM((16, 3, 256), F32)
    tab, out1, rims1, own1 = call(
        first_kernel,
        (comb, x, cot, sel),
        "vhhv",
        [shape_of(8, 128, dtype=I32), sent16, rims16, rims16],
        "vhhh",
        [lines_scratch, pltpu.SMEM((8, 128), I32), pltpu.SemaphoreType.DMA],
    )
    in1 = exchange(out1.reshape(groups, 4 * S, 256)).reshape(64, 2 * S, 256)
    conv1, back2, g2, c_own, g_own, rim_own = call(
        inner_kernel,
        (tab, x, cot, own1, mixers, taps, shift),
        "shhhvvv",
        [wide, wide, field, rims16, rims16, shape_of(32, S, 256, dtype=F32)],
        "hhhhhh",
        [taps_scratch],
    )
    active, first, gh, gc, rims2, lines2, out2, own2, c_in, g_in = call(
        middle_kernel,
        (tab, in1, rims1, rim_own, conv1, back2, mixers, taps, shifts, sel, spread),
        "svhhhhvvvvv",
        [field, field, field, field, rims16, lines16, sent16, rims16, rims16, rims16],
        "hhhhhhhhhh",
        [lines_scratch, split_scratch, split_scratch, taps_scratch],
        limit=59.5,
    )
    in2 = exchange(out2.reshape(groups, 4 * S, 256)).reshape(64, 2 * S, 256)
    pack, conv2 = call(
        weight_kernel,
        (tab, x, cot, active, first, gh, gc, g2, rims2, lines2, rims1, in1, c_own, g_own, c_in, g_in,
         taps, shift),
        "shhhhhhhhhhhhhhhvv",
        [shape_of(groups, 24, 256), wide],
        "hh",
        [
            pltpu.VMEM((T * CELLS, 256), BF16),
            lines_scratch,
            taps_scratch,
            pltpu.VMEM((9, 8, 256), F32),
            pltpu.VMEM((9, 8, 256), F32),
            pltpu.VMEM((16, 3, 8, 256), F32),
            pltpu.VMEM((2, 8, 256), F32),
        ],
        order=(8, 13, 15, 9, 10, 11, 6, 1, 3, 7, 5, 2, 4, 12, 14),
    )
    (back1,) = call(back_kernel, (gc, taps, shift), "hvv", [wide], "h")
    parts = exchange(pack)
    (outcome,) = call(
        outcome_kernel,
        (tab, in2, rims2, conv2, x, mixers, taps, shifts, spread),
        "shhhhvvvv",
        [field],
        "h",
        [lines_scratch, split_scratch],
    )
    (part,) = call(sum_kernel, (parts,), "v", [shape_of(batch, 24, 256)], "v", limit=4)
    part = lax.all_to_all(part, "batch", split_axis=0, concat_axis=0, tiled=True)
    (spread_out,) = call(spread_kernel, (part,), "v", [shape_of(groups, 24, 256)], "v", limit=4)
    whole = exchange(spread_out)
    (state_grad,) = call(
        grad_kernel,
        (tab, in2, own2, back1, cot, taps, spread),
        "shhhhvv",
        [field],
        "h",
        [lines_scratch, split_scratch, rim_scratch, taps_scratch],
    )
    scale = 1.0 / math.sqrt(T * CELLS * groups * batch)

    def unpack(*refs):
        unpack_kernel(scale, *refs)

    mixer_grads, stencil_grads, shift_grads = call(
        unpack,
        (whole,),
        "v",
        [shape_of(2, 256, 256, dtype=F32), shape_of(9, 2, 256, dtype=F32), shape_of(2, 256, dtype=F32)],
        "hvv",
        limit=4,
    )
    stencil_grads = stencil_grads.swapaxes(0, 1)
    return (
        outcome.reshape(shape),
        state_grad.reshape(shape),
        mixer_grads,
        stencil_grads,
        shift_grads,
    )


def solution(mesh):
    torus = Mesh(
        mesh.devices.reshape(4, 4, 2, mesh.shape["batch"]), ("tile_0", "tile_1", "tile_2", "batch")
    )
    in_specs = (
        P("batch", TILE, None, None, None),
        P("batch", TILE, None, None, None),
        P(),
        P(),
        P(),
        P(),
        P(),
    )
    out_specs = (
        P("batch", TILE, None, None, None),
        P("batch", TILE, None, None, None),
        P(),
        P(),
        P(),
    )
    return jax.shard_map(
        whole_block, mesh=torus, in_specs=in_specs, out_specs=out_specs, check_vma=False
    )
```

time: 141 us -> 129 us (0.915)
  waiting for transfers between devices: 24.7 us -> 18.2 us
  blocking collectives: 31.6 us -> 37.5 us
  starting transfers between devices: 17.3 us -> 13.3 us
  Pallas kernels: 59.1 us -> 55.3 us
  local copies, waits for them, and re-layouts: 5.4 us -> 2.76 us
    all_to_all x0 -> x1, blocking collectives: none -> 8.21 us  [whole_block(): lax.all_to_all(part, 'batch', split_axis=0, concat_axis=0, tiled=True)]
    ppermute x2 -> x0, starting transfers between devices: 3.96 us -> none  [the longest x1 2.75 us: whole_block(): other = lax.ppermute(part, 'batch', [(i, i ^ step) for i in range(batch)])]
    pallas_call x8 -> x10, Pallas kernels: 59.1 us -> 55.3 us  [call(): pl.pallas_call(kernel, out_shape=[pltpu.HBM(o.shape, o.dtype) if m == 'h'...]
    all_to_all x2, waiting for transfers between devices: 21.5 us -> 18.2 us  [exchange(): return lax.all_to_all(array, TILE, split_axis=0, concat_axis=0, tiled=True)]
    ppermute x2 -> x0, waiting for transfers between devices: 3.11 us -> none  [the longest x1 1.68 us: whole_block(): lax.ppermute(part, 'batch', [(i, i ^ step) for i in range(batch)])]
    unnamed x12 -> x4, local copies, waits for them, and re-layouts: 4.57 us -> 1.93 us
    all_to_all x2, blocking collectives: 31.6 us -> 29.3 us  [exchange(): return lax.all_to_all(array, TILE, split_axis=0, concat_axis=0, tiled=True)]
  transfers between devices with their start and end apart: 4 -> 2, of which waited for: 4 -> 2; matrix products, arithmetic and copies ran while one was open for 1% -> 0% of each run, Pallas kernels for 7% -> 12%
where the time goes in v2:
time: 129 us; the launch traced here: 128 us
  Pallas kernels  55.3 us (43%)
  blocking collectives  37.5 us (29%)
  waiting for transfers between devices  18.2 us (14%)
  starting transfers between devices  13.3 us (10%)
  local copies, waits for them, and re-layouts  2.76 us (2%)
    pallas_call x10, Pallas kernels, call(): pl.pallas_call(kernel, out_shape=[pltpu.HBM(o.shape, o.dtype) if m == 'h'...  55.3 us
    all_to_all x2, blocking collectives, exchange(): return lax.all_to_all(array, TILE, split_axis=0, concat_axis=0, tiled=True)  29.3 us
    all_to_all x2, waiting for transfers between devices, exchange(): return lax.all_to_all(array, TILE, split_axis=0, concat_axis=0, tiled=True)  18.2 us
    all_to_all x2, starting transfers between devices, exchange(): return lax.all_to_all(array, TILE, split_axis=0, concat_axis=0, tiled=True)  13.3 us
    all_to_all x1, blocking collectives, whole_block(): lax.all_to_all(part, 'batch', split_axis=0, concat_axis=0, tiled=True)  8.21 us
  transfers between devices with their start and end apart: 2, of which 2 were waited for; matrix products, arithmetic and copies ran while one was open for 0% of the time, Pallas kernels for 12%

profile of v2, /device:TPU:1, one launch (start us, length us, event | category | flops | bytes accessed | tf_op | source)
XLA Modules:
  0.0 128.5 jit_solution(1149843936282768826)
XLA Ops:
  0.6 0.7 multiply_add_fusion
  1.4 0.1 copy.16
  1.5 0.1 reshape.37
  1.6 0.6 pad.4.refs_0_
  2.2 6.1 %shard_map.137 = (s32[8,128]{1,0:T(8,128)}, bf16[64,32,256]{2,1,0:T(8,128)(2,1)}, bf16[64,16,256]{2,1,0:T(8,128)(2,1)}, bf16[64,16,256]{2,1,0:T(8,128)(2,1)}) custom-call(s32[32,128]{1,0:T(8,128)} %pad.4.refs_0_, bf16[2048,256]{1,0:T(8,128)(2,1)} %bitcast.10, bf16[2048,256]{1,0:T(8,128)(2,1)} %bitcast.14, bf16[256,256]{1,0:T(8,128)(2,1)} %constant.10.clone.refs_3_.refs_9_), custom_call_target="tpu_custom_call" | custom-call | tf_op jit(solution)/shard_map/pallas_call | solution.py:643
  8.3 9.6 %all-to-all-start = ((bf16[32,64,256]{2,1,0:T(8,128)(2,1)}), bf16[32,64,256]{2,1,0:T(8,128)(2,1)S(1)}, u32[]{:S(2)}, u32[]{:S(2)}) async-start(bf16[32,64,256]{2,1,0:T(8,128)(2,1)} %bitcast.22), calls=%async_computation | async-start | bytes 2097152 | tf_op jit(solution)/shard_map/all_to_all | solution.py:656
  17.9 9.0 %shard_map.138 = (f32[2048,256]{1,0:T(8,128)}, f32[2048,256]{1,0:T(8,128)}, bf16[2048,256]{1,0:T(8,128)(2,1)}, bf16[64,16,256]{2,1,0:T(8,128)(2,1)}, bf16[64,16,...) custom-call(s32[8,128]{1,0:T(8,128)} %get-tuple-element.30.refs_0_, bf16[2048,256]{1,0:T(8,128)(2,1)} %bitcast.11, ...), custom_call_target="tpu_custom_call" | custom-call | tf_op jit(solution)/shard_map/pallas_call | solution.py:643
  26.9 7.9 %all-to-all-done = bf16[32,64,256]{2,1,0:T(8,128)(2,1)S(1)} async-done(((bf16[32,64,256]{2,1,0:T(8,128)(2,1)}), bf16[32,64,256]{2,1,0:T(8,128)(2,1)S(1)}, u32[]{:S(2)}, u32[]{:S(2)}) %all-to-all-start) | async-done | bytes 1048608 | tf_op jit(solution)/shard_map/all_to_all | solution.py:656
  34.8 0.0 copy-start
  34.8 1.0 copy-done
  35.8 11.0 %shard_map.139 = (bf16[2048,256]{1,0:T(8,128)(2,1)}, bf16[2048,256]{1,0:T(8,128)(2,1)}, bf16[2048,256]{1,0:T(8,128)(2,1)}, bf16[2048,256]{1,0:T(8,128)(2,1)}, bf...) custom-call(s32[8,128]{1,0:T(8,128)} %get-tuple-element.30.refs_0_, ...), custom_call_target="tpu_custom_call" | custom-call | tf_op jit(solution)/shard_map/pallas_call | solution.py:643
  46.8 11.6 %shard_map.140 = (bf16[32,24,256]{2,1,0:T(8,128)(2,1)}, f32[2048,256]{1,0:T(8,128)}) custom-call(s32[8,128]{1,0:T(8,128)} %get-tuple-element.30.refs_0_, bf16[2048,256]{1,0:T(8,128)(2,1)} %bitcast.12, bf16[2048,256]{1,0:T(8,128)(2,1)} %bitcast.16, bf16[2048,256]{1,0:T(8,128)(2,1)} %get-tuple-element.39.refs_3_, bf16[2048,256]{1,0:T(8,128)(2,1)} %get-tuple-element.40.refs_4_, ...), custom_call_target="tpu_custom_call" | custom-call | tf_op jit(solution)/shard_map/pallas_call | solution.py:643
  58.5 14.2 %all_to_all.25.refs_0_ = bf16[32,24,256]{2,1,0:T(8,128)(2,1)S(1)} all-to-all(bf16[32,24,256]{2,1,0:T(8,128)(2,1)} %get-tuple-element.51), channel_id=1, replica_groups=mesh['tile_0'=4,'tile_1'=4,'tile_2'=2,'batch'=4] {'tile_0','tile_1','til..., dimensions={0} | all-to-all | bytes 786432 | tf_op jit(solution)/shard_map/all_to_all | solution.py:656
  72.7 0.1 shard_map.144
  72.8 8.2 %all_to_all.26.refs_0_ = bf16[4,24,256]{2,1,0:T(8,128)(2,1)S(1)} all-to-all(bf16[4,24,256]{2,1,0:T(8,128)(2,1)S(1)} %shard_map.144), channel_id=1, replica_groups=mesh['tile_0'=4,'tile_1'=4,'tile_2'=2,'batch'=4] {'batch'}, dimensions={0} | all-to-all | bytes 98304 | tf_op jit(solution)/shard_map/all_to_all | solution.py:736
  81.0 15.0 %all_to_all.27.refs_0_ = bf16[32,24,256]{2,1,0:T(8,128)(2,1)S(1)} all-to-all(bf16[32,24,256]{2,1,0:T(8,128)(2,1)S(1)} %shard_map.145), channel_id=1, replica_groups=mesh['tile_0'=4,'tile_1'=4,'tile_2'=2,'batch'=4] {'tile_0','tile_1','til..., dimensions={0} | all-to-all | bytes 786432 | tf_op jit(solution)/shard_map/all_to_all | solution.py:656
  96.1 3.7 %all-to-all-start.1 = ((bf16[32,64,256]{2,1,0:T(8,128)(2,1)}), bf16[32,64,256]{2,1,0:T(8,128)(2,1)S(1)}, u32[]{:S(2)}, u32[]{:S(2)}) async-start(bf16[32,64,256]{2,1,0:T(8,128)(2,1)} %bitcast.5), calls=%async_computation.1 | async-start | bytes 2097152 | tf_op jit(solution)/shard_map/all_to_all | solution.py:656
  99.8 5.1 %shard_map.142.refs_3_ = f32[2048,256]{1,0:T(8,128)} custom-call(bf16[2048,256]{1,0:T(8,128)(2,1)} %get-tuple-element.42.refs_6_.refs_0_, f32[9,2,256]{2,1,0:T(2,128)} %bitcast.28, bf16[512,256]{1,0:T(8,128)(2,1)} %constant.12.clone.refs_6_.refs_17_.refs_2_), custom_call_target="tpu_custom_call" | custom-call | tf_op jit(solution)/shard_map/pallas_call | solution.py:643
  104.9 1.4 %shard_map.146 = (f32[2,256,256]{2,1,0:T(8,128)}, f32[9,2,256]{2,1,0:T(2,128)}, f32[2,256]{1,0:T(2,128)}) custom-call(bf16[32,24,256]{2,1,0:T(8,128)(2,1)S(1)} %all_to_all.27.refs_0_), custom_call_target="tpu_custom_call" | custom-call | tf_op jit(solution)/shard_map/pallas_call | solution.py:643
  106.3 10.2 %all-to-all-done.1 = bf16[32,64,256]{2,1,0:T(8,128)(2,1)S(1)} async-done(((bf16[32,64,256]{2,1,0:T(8,128)(2,1)}), bf16[32,64,256]{2,1,0:T(8,128)(2,1)S(1)}, u32[]{:S(2)}, u32[]{:S(2)}) %all-to-all-start.1) | async-done | bytes 1048608 | tf_op jit(solution)/shard_map/all_to_all | solution.py:656
  116.6 0.0 copy-start.1
  116.6 1.0 copy-done.1
  117.6 5.6 %shard_map.141 = bf16[2048,256]{1,0:T(8,128)(2,1)} custom-call(s32[8,128]{1,0:T(8,128)} %get-tuple-element.30.refs_0_, bf16[64,32,256]{2,1,0:T(8,128)(2,1)} %bitcast.20, bf16[64,16,256]{2,1,0:T(8,128)(2,1)} %get-tuple-element.38.refs_8_.refs_2_, f32[2048,256]{1,0:T(8,128)} %get-tuple-element.49.refs_3_, bf16[2048,256]{1,0:T(8,128)(2,1)} %bitcast.13, ...), custom_call_target="tpu_custom_call" | custom-call | tf_op jit(solution)/shard_map/pallas_call | solution.py:643
  123.1 5.3 %shard_map.143 = bf16[2048,256]{1,0:T(8,128)(2,1)} custom-call(s32[8,128]{1,0:T(8,128)} %get-tuple-element.30.refs_0_, bf16[64,32,256]{2,1,0:T(8,128)(2,1)} %bitcast.21, bf16[64,16,256]{2,1,0:T(8,128)(2,1)} %get-tuple-element.50.refs_2_, f32[2048,256]{1,0:T(8,128)} %shard_map.142.refs_3_, bf16[2048,256]{1,0:T(8,128)(2,1)} %bitcast.17, ...), custom_call_target="tpu_custom_call" | custom-call | tf_op jit(solution)/shard_map/pallas_call | solution.py:643
  (1 shorter events, 0.0 us)
Async XLA Ops:
  8.3 26.5 %all-to-all-start = ((bf16[32,64,256]{2,1,0:T(8,128)(2,1)}), bf16[32,64,256]{2,1,0:T(8,128)(2,1)S(1)}, u32[]{:S(2)}, u32[]{:S(2)}) async-start(bf16[32,64,256]{2,1,0:T(8,128)(2,1)} %bitcast.22), calls=%async_computation | async-start | bytes 2097152 | tf_op jit(solution)/shard_map/all_to_all | solution.py:656
  34.8 1.0 copy-start
  96.1 20.5 %all-to-all-start.1 = ((bf16[32,64,256]{2,1,0:T(8,128)(2,1)}), bf16[32,64,256]{2,1,0:T(8,128)(2,1)S(1)}, u32[]{:S(2)}, u32[]{:S(2)}) async-start(bf16[32,64,256]{2,1,0:T(8,128)(2,1)} %bitcast.5), calls=%async_computation.1 | async-start | bytes 2097152 | tf_op jit(solution)/shard_map/all_to_all | solution.py:656
  116.6 1.0 copy-start.1

commit v3 on v2

--- a/solution.py
+++ b/solution.py
@@ -142,14 +142,20 @@
     ref[t, pl.ds(64 + first, value.shape[0]), :] = (value - high.astype(F32)).astype(BF16)
 
 
-def forward_lines(split_ref, buf_ref, tab_ref, w):
+def forward_lines(split_ref, buf_ref, tab_ref, w, panels_ref=None):
     def one(t, carry):
         corner = {}
         for d in range(4, 8):
-            row = buf_ref[tab_ref[0, t * 8 + d]][:8, :].astype(F32)[:1, :]
+            panel = buf_ref[tab_ref[0, t * 8 + d]]
+            if panels_ref is not None:
+                panels_ref[t * 8 + d] = panel
+            row = panel[:8, :].astype(F32)[:1, :]
             corner[d] = w[CORNER_TAP[d]] * row
         for d in range(4):
-            x = buf_ref[tab_ref[0, t * 8 + d]].astype(F32)
+            panel = buf_ref[tab_ref[0, t * 8 + d]]
+            if panels_ref is not None:
+                panels_ref[t * 8 + d] = panel
+            x = panel.astype(F32)
             before, after = neighbours(x)
             a, b, c = SIDE_TAPS[d]
             line = w[a] * before + w[b] * x + w[c] * after
@@ -166,22 +172,26 @@
     lax.fori_loop(0, T, one, 0, unroll=2)
 
 
-def rim_gradients(rim_ref, lines_ref, tab_ref, taps_ref, first, count):
+def rim_rows_at(base, rim):
+    return pl.ds(pl.multiple_of(base + rim * S, S), S)
+
+
+def rim_gradients(rim_ref, base, lines_ref, tab_ref, taps_ref, first, count):
     def one(i, carry):
         x = lines_ref[i].astype(F32)
         before, after = neighbours(x)
         u = taps_ref[tab_ref[3, first + i]]
         rim = tab_ref[2, first + i] >> 1
-        rim_ref[rim] += u[0:1] * after + u[1:2] * x + u[2:3] * before
+        rim_ref[rim_rows_at(base, rim)] += u[0:1] * after + u[1:2] * x + u[2:3] * before
         return carry
 
     lax.fori_loop(0, count, one, 0, unroll=8)
 
 
-def split_rims(split_ref, rim_ref):
+def split_rims(split_ref, rim_ref, base):
     def split(t, carry):
         for e in range(4):
-            split_store(split_ref, t, e * S, rim_ref[t * 4 + e])
+            split_store(split_ref, t, e * S, rim_ref[rim_rows_at(base, t * 4 + e)])
         return carry
 
     lax.fori_loop(0, T, split, 0, unroll=2)
@@ -217,15 +227,11 @@
     lax.fori_loop(0, 4, some, 0)
 
 
-def banks(rims_ref, lines_ref, rim_field, line_field, sel_ref):
-    def one(t, carry):
-        rims = dot(sel_ref[0:128, :], tile_of(rim_field, t)).astype(BF16)
-        rims_ref[pl.ds(t * 8, 8)] = rims.reshape(8, S, 256)
-        lines = dot(sel_ref[...], tile_of(line_field, t)).astype(BF16)
-        lines_ref[pl.ds(t * 16, 16)] = lines.reshape(16, S, 256)
-        return carry
-
-    lax.fori_loop(0, T, one, 0)
+def banks(rims_ref, lines_ref, t, rim_tile, line_tile, sel_ref):
+    rims = dot(sel_ref[0:128, :], rim_tile).astype(BF16)
+    rims_ref[pl.ds(t * 8, 8)] = rims.reshape(8, S, 256)
+    lines = dot(sel_ref[...], line_tile).astype(BF16)
+    lines_ref[pl.ds(t * 16, 16)] = lines.reshape(16, S, 256)
 
 
 def own_position():
@@ -234,10 +240,23 @@
 
 
 def first_kernel(
-    arrive, leave, comb_ref, states_ref, cot_ref, sel_ref, tab_ref, out_ref, rims_ref, own_ref, lines_ref, smem, sem
+    arrive, leave, slot_ref, code_ref, states_ref, cot_ref, sel_ref, tab_ref, out_ref, rims_ref, own_ref,
+    lines_ref, comb_ref, smem, sem,
 ):
     me = own_position()
-    comb = comb_ref[...]
+    entries = slot_ref.shape[1]
+    groups = entries // T
+    sub = iota((128, entries), 0)
+    tile = iota((128, entries), 1)
+    belongs = (tile & (T - 1)) == (sub >> 3)
+    member = (iota((groups, entries), 0) == (iota((groups, entries), 1) >> 3)).astype(F32).astype(BF16)
+
+    def by_block(ref):
+        copies = jnp.concatenate([ref[...].astype(F32)] * 16, axis=0)
+        return dot_t(member, jnp.where(belongs, copies, 0.0).astype(BF16)).astype(I32)
+
+    comb = by_block(slot_ref) * 8 + by_block(code_ref)
+    comb_ref[...] = comb
     lane = iota(comb.shape, 1)
     home = iota(comb.shape, 0)
     slot = comb >> 3
@@ -289,9 +308,14 @@
     tab_ref[5:6, :] = jnp.where(in_own, lane1 * 2 + (own & 1), 0)
     copy = pltpu.make_async_copy(tab_ref, smem, sem)
     copy.start()
-    arrive(1)
     arrive(2)
-    banks(rims_ref, lines_ref, states_ref, cot_ref, sel_ref)
+    arrive(3)
+
+    def lines_of(t, carry):
+        banks(rims_ref, lines_ref, t, tile_of(states_ref, t), tile_of(cot_ref, t), sel_ref)
+        return carry
+
+    lax.fori_loop(0, T, lines_of, 0, unroll=4)
     leave(2, 0, 64)
     copy.wait()
     gather_out(leave, (1, 3), out_ref, own_ref, rims_ref, lines_ref, smem)
@@ -299,7 +323,7 @@
 
 def inner_kernel(
     arrive, leave, tab_ref, states_ref, cot_ref, own_in_ref, mixers_ref, stencils_ref, shift_ref,
-    conv_ref, back_ref, g_ref, c_ref, gl_ref, rim_ref, taps_ref,
+    conv_ref, back_ref, g_ref, c_ref, gl_ref, taps_ref,
 ):
     w0 = tap_rows(stencils_ref, 0)
     w1 = tap_rows(stencils_ref, 1)
@@ -326,16 +350,16 @@
     leave(3, 0, 64)
     line_grads(gl_ref, c_ref, mixers_ref)
     leave(4, 0, 64)
-    rim_ref[...] = jnp.zeros_like(rim_ref)
-    rim_gradients(rim_ref, gl_ref, tab_ref, taps_ref, 0, 64)
-    leave(5, 0, 32)
+    back_ref[T * CELLS :] = jnp.zeros((2 * CELLS, 256), F32)
+    rim_gradients(back_ref, T * CELLS, gl_ref, tab_ref, taps_ref, 0, 64)
+    leave(1, T * CELLS, 2 * CELLS)
 
 
 def middle_kernel(
     arrive, leave,
-    tab_ref, in_ref, rims_in_ref, rim_ref, conv_ref, back_ref, mixers_ref, stencils_ref,
+    tab_ref, in_ref, rims_in_ref, back_ref, conv_ref, mixers_ref, stencils_ref,
     shifts_ref, sel_ref, spread_ref,
-    active_ref, first_ref, gh_ref, gc_ref, rims_ref, lines_ref, out_ref, own_ref, c_ref, g_ref,
+    active_ref, first_ref, gh_ref, gc_ref, rims_ref, lines_ref, out_ref, own_ref, c_ref, g_ref, panels_ref,
     buf_ref, split_ref, split2_ref, taps_ref,
 ):
     w0 = tap_rows(stencils_ref, 0)
@@ -347,12 +371,12 @@
     leave(9, 0, 64)
     arrive(2)
     buf_ref[0:64] = rims_in_ref[...]
-    forward_lines(split_ref, buf_ref, tab_ref, w0)
+    forward_lines(split_ref, buf_ref, tab_ref, w0, panels_ref)
+    leave(10, 0, 64)
     arrive(3)
-    rim_gradients(rim_ref, g_ref, tab_ref, taps_ref, 64, 64)
-    split_rims(split2_ref, rim_ref)
+    rim_gradients(back_ref, T * CELLS, g_ref, tab_ref, taps_ref, 64, 64)
+    split_rims(split2_ref, back_ref, T * CELLS)
     arrive(4)
-    arrive(5)
 
     def one(t, carry):
         first = (tile_of(conv_ref, t) + dot(spread_ref[...], split_ref[t])).astype(BF16)
@@ -371,10 +395,10 @@
         gc = dot_t(gh, mixers_ref[0]).astype(BF16)
         put_tile(gc_ref, t, gc)
         leave(3, t * CELLS, CELLS)
+        banks(rims_ref, lines_ref, t, active, gc, sel_ref)
         return carry
 
     lax.fori_loop(0, T, one, 0, unroll=2)
-    banks(rims_ref, lines_ref, active_ref, gc_ref, sel_ref)
     leave(4, 0, 64)
     leave(5, 0, 128)
     gather_out(leave, (6, 7), out_ref, own_ref, rims_ref, lines_ref, tab_ref)
@@ -383,7 +407,7 @@
 def weight_kernel(
     arrive, leave,
     tab_ref, states_ref, cot_ref, active_ref, first_ref, gh_ref, gc_ref, g2_ref, rims_ref, lines_ref,
-    rims_in_ref, in_ref, c_own_ref, g_own_ref, c_in_ref, g_in_ref, stencils_ref, shift_ref,
+    panels_ref, c_own_ref, g_own_ref, c_in_ref, g_in_ref, stencils_ref, shift_ref,
     pack_ref, conv_ref,
     second_ref, h_ref, taps_ref, acc1_ref, acc2_ref, accl_ref, sums_ref,
 ):
@@ -421,20 +445,17 @@
         return one
 
     arrive(8)
-    arrive(13)
+    arrive(12)
     lax.fori_loop(0, 64, second_halo(g_own_ref), 0, unroll=8)
-    arrive(15)
+    arrive(14)
     lax.fori_loop(64, 128, second_halo(g_in_ref), 0, unroll=8)
 
-    for k in (9, 10, 11):
+    for k in (9, 10):
         arrive(k)
 
     def first_halo(t, carry):
         for d in range(8):
-            place = tab_ref[0, t * 8 + d]
-            own = rims_in_ref[jnp.minimum(place, 63)]
-            sent = in_ref[jnp.maximum(place - 64, 0), 0:S]
-            x = jnp.where(place < 64, own, sent).astype(F32)
+            x = panels_ref[t * 8 + d].astype(F32)
             g = lines_ref[(t * 8 + d) * 2].astype(F32)
             if d < 4:
                 before, after = neighbours(x)
@@ -467,7 +488,7 @@
         return carry
 
     lax.fori_loop(0, T, one, 0)
-    for k in (4, 12, 14):
+    for k in (4, 11, 13):
         arrive(k)
     for d in range(8):
         for f in range(2):
@@ -481,15 +502,21 @@
     rows = [jnp.sum(acc1_ref[k], axis=0, keepdims=True) for k in range(9)]
     rows += [jnp.sum(acc2_ref[k], axis=0, keepdims=True) for k in range(9)]
     rows += [jnp.sum(sums_ref[k], axis=0, keepdims=True) for k in range(2)]
-    rows += [jnp.zeros_like(rows[0])] * 4
-    for r in range(3):
-        pack_ref[r, 16:24] = jnp.concatenate(rows[8 * r : 8 * r + 8], axis=0).astype(BF16)
-    for r in range(3, pack_ref.shape[0]):
-        pack_ref[r, 16:24] = jnp.zeros((8, 256), BF16)
+    rows = [row[:, 128 * h : 128 * h + 128] for row in rows for h in range(2)]
+    for r in range(5):
+        pack_ref[r, 32:40] = jnp.concatenate(rows[8 * r : 8 * r + 8], axis=0).astype(BF16)
+    for r in range(5, pack_ref.shape[0]):
+        pack_ref[r, 32:40] = jnp.zeros((8, 128), BF16)
     half = pack_ref.shape[0] // 2
+
+    def put_rows(r, rows16):
+        for q in range(4):
+            at = (q // 2) * 8, (q % 2) * 128
+            pack_ref[r, 8 * q : 8 * q + 8] = rows16[at[0] : at[0] + 8, at[1] : at[1] + 128].astype(BF16)
+
     mixer_first = t_dot(first_ref[...], gh_ref[...])
     for r in range(half):
-        pack_ref[r, 0:16] = mixer_first[16 * r : 16 * r + 16].astype(BF16)
+        put_rows(r, mixer_first[16 * r : 16 * r + 16])
     leave(0, 0, half)
     mixer_second = (
         t_dot(second_ref[...], cot_ref[...])
@@ -497,7 +524,7 @@
         + t_dot(h_ref[64:128].reshape(1024, 256), c_in_ref[...].reshape(1024, 256))
     )
     for r in range(half):
-        pack_ref[half + r, 0:16] = mixer_second[16 * r : 16 * r + 16].astype(BF16)
+        put_rows(half + r, mixer_second[16 * r : 16 * r + 16])
     leave(0, half, half)
 
 
@@ -512,7 +539,7 @@
         leave(0, t * CELLS, CELLS)
         return carry
 
-    lax.fori_loop(0, T, one, 0, unroll=2)
+    lax.fori_loop(0, T, one, 0)
 
 
 def outcome_kernel(
@@ -552,8 +579,8 @@
     live_lines(lines_ref, 0, own_in_ref, 0, tab_ref, 0)
     arrive(1)
     live_lines(lines_ref, 64, in_ref, S, tab_ref, 64)
-    rim_gradients(rim_ref, lines_ref, tab_ref, taps_ref, 0, 128)
-    split_rims(split_ref, rim_ref)
+    rim_gradients(rim_ref, 0, lines_ref, tab_ref, taps_ref, 0, 128)
+    split_rims(split_ref, rim_ref, 0)
     arrive(3)
     arrive(4)
 
@@ -587,14 +614,19 @@
     half = in_ref.shape[0] // 2
     for k in range(2):
         for r in range(half):
-            mixer_ref[k, 16 * r : 16 * r + 16, :] = in_ref[k * half + r, 0:16].astype(F32) * scale
+            for q in range(4):
+                block = in_ref[k * half + r, 8 * q : 8 * q + 8].astype(F32) * scale
+                row, col = 16 * r + (q // 2) * 8, (q % 2) * 128
+                mixer_ref[k, row : row + 8, col : col + 128] = block
         leave(0, k, 1)
-    rows = [in_ref[r, 16:24].astype(F32) * scale for r in range(3)]
+    rows = [in_ref[r, 32:40].astype(F32) * scale for r in range(5)]
     rows = [row for block in rows for row in jnp.split(block, 8, axis=0)]
     for k in range(2):
-        for j in range(9):
-            stencil_ref[j, k : k + 1, :] = rows[9 * k + j]
-        shift_ref[k : k + 1, :] = rows[18 + k]
+        for h in range(2):
+            part = slice(128 * h, 128 * h + 128)
+            for j in range(9):
+                stencil_ref[j, k : k + 1, part] = rows[2 * (9 * k + j) + h]
+            shift_ref[k : k + 1, part] = rows[2 * (18 + k) + h]
 
 
 def shape_of(*dims, dtype=BF16):
@@ -662,8 +694,6 @@
     shape = states.shape
     x = states.reshape(T * CELLS, 256)
     cot = cotangent.reshape(T * CELLS, 256)
-    comb = (beside_slot * 8 + beside_code).astype(I32).reshape(groups, 64)
-    comb = jnp.pad(comb, ((0, 0), (0, 64)))
     sel = jnp.asarray(selection(), BF16)
     spread = jnp.asarray(spreading(), BF16)
     shift = jnp.asarray(shifting(), BF16)
@@ -675,41 +705,46 @@
     wide = shape_of(T * CELLS, 256, dtype=F32)
     lines_scratch = pltpu.VMEM((128, S, 256), BF16)
     split_scratch = pltpu.VMEM((T, 128, 256), BF16)
-    rim_scratch = pltpu.VMEM((32, S, 256), F32)
+    rim_scratch = pltpu.VMEM((2 * CELLS, 256), F32)
     taps_scratch = pltpu.VMEM((16, 3, 256), F32)
     tab, out1, rims1, own1 = call(
         first_kernel,
-        (comb, x, cot, sel),
-        "vhhv",
+        (beside_slot.astype(I32).T, beside_code.astype(I32).T, x, cot, sel),
+        "vvhhv",
         [shape_of(8, 128, dtype=I32), sent16, rims16, rims16],
         "vhhh",
-        [lines_scratch, pltpu.SMEM((8, 128), I32), pltpu.SemaphoreType.DMA],
+        [
+            lines_scratch,
+            pltpu.VMEM((groups, 128), I32),
+            pltpu.SMEM((8, 128), I32),
+            pltpu.SemaphoreType.DMA,
+        ],
     )
     in1 = exchange(out1.reshape(groups, 4 * S, 256)).reshape(64, 2 * S, 256)
-    conv1, back2, g2, c_own, g_own, rim_own = call(
+    conv1, back2, g2, c_own, g_own = call(
         inner_kernel,
         (tab, x, cot, own1, mixers, taps, shift),
         "shhhvvv",
-        [wide, wide, field, rims16, rims16, shape_of(32, S, 256, dtype=F32)],
-        "hhhhhh",
+        [wide, shape_of((T + 2) * CELLS, 256, dtype=F32), field, rims16, rims16],
+        "hhhhh",
         [taps_scratch],
     )
-    active, first, gh, gc, rims2, lines2, out2, own2, c_in, g_in = call(
+    active, first, gh, gc, rims2, lines2, out2, own2, c_in, g_in, panels = call(
         middle_kernel,
-        (tab, in1, rims1, rim_own, conv1, back2, mixers, taps, shifts, sel, spread),
-        "svhhhhvvvvv",
-        [field, field, field, field, rims16, lines16, sent16, rims16, rims16, rims16],
-        "hhhhhhhhhh",
+        (tab, in1, rims1, back2, conv1, mixers, taps, shifts, sel, spread),
+        "svhhhvvvvv",
+        [field, field, field, field, rims16, lines16, sent16, rims16, rims16, rims16, rims16],
+        "hhhhhhhhhhh",
         [lines_scratch, split_scratch, split_scratch, taps_scratch],
-        limit=59.5,
+        limit=51.0,
     )
     in2 = exchange(out2.reshape(groups, 4 * S, 256)).reshape(64, 2 * S, 256)
     pack, conv2 = call(
         weight_kernel,
-        (tab, x, cot, active, first, gh, gc, g2, rims2, lines2, rims1, in1, c_own, g_own, c_in, g_in,
+        (tab, x, cot, active, first, gh, gc, g2, rims2, lines2, panels, c_own, g_own, c_in, g_in,
          taps, shift),
-        "shhhhhhhhhhhhhhhvv",
-        [shape_of(groups, 24, 256), wide],
+        "shhhhhhhhhhhhhhvv",
+        [shape_of(groups, 40, 128), wide],
         "hh",
         [
             pltpu.VMEM((T * CELLS, 256), BF16),
@@ -720,7 +755,7 @@
             pltpu.VMEM((16, 3, 8, 256), F32),
             pltpu.VMEM((2, 8, 256), F32),
         ],
-        order=(8, 13, 15, 9, 10, 11, 6, 1, 3, 7, 5, 2, 4, 12, 14),
+        order=(8, 12, 14, 9, 10, 6, 1, 3, 7, 5, 2, 4, 11, 13),
     )
     (back1,) = call(back_kernel, (gc, taps, shift), "hvv", [wide], "h")
     parts = exchange(pack)
@@ -732,9 +767,9 @@
         "h",
         [lines_scratch, split_scratch],
     )
-    (part,) = call(sum_kernel, (parts,), "v", [shape_of(batch, 24, 256)], "v", limit=4)
+    (part,) = call(sum_kernel, (parts,), "v", [shape_of(batch, 40, 128)], "v", limit=4)
     part = lax.all_to_all(part, "batch", split_axis=0, concat_axis=0, tiled=True)
-    (spread_out,) = call(spread_kernel, (part,), "v", [shape_of(groups, 24, 256)], "v", limit=4)
+    (spread_out,) = call(spread_kernel, (part,), "v", [shape_of(groups, 40, 128)], "v", limit=4)
     whole = exchange(spread_out)
     (state_grad,) = call(
         grad_kernel,

time: 129 us -> 123 us (0.953)
  Pallas kernels: 55.3 us -> 53.1 us
  local copies, waits for them, and re-layouts: 2.76 us -> 1.03 us
  blocking collectives: 37.5 us -> 36.2 us
    pallas_call x10, Pallas kernels: 55.3 us -> 53.1 us  [call(): pl.pallas_call(kernel, out_shape=[pltpu.HBM(o.shape, o.dtype) if m == 'h'...]
  transfers between devices with their start and end apart: 2 -> 2, of which waited for: 2 -> 2; matrix products, arithmetic and copies ran while one was open for 0% -> 0% of each run, Pallas kernels for 12% -> 13%
where the time goes in v3:
time: 123 us; the launch traced here: 122 us
  Pallas kernels  53.1 us (43%)
  blocking collectives  36.2 us (29%)
  waiting for transfers between devices  18 us (15%)
  starting transfers between devices  13.3 us (11%)
    pallas_call x10, Pallas kernels, call(): pl.pallas_call(kernel, out_shape=[pltpu.HBM(o.shape, o.dtype) if m == 'h'...  53.1 us
    all_to_all x2, blocking collectives, exchange(): return lax.all_to_all(array, TILE, split_axis=0, concat_axis=0, tiled=True)  28 us
    all_to_all x2, waiting for transfers between devices, exchange(): return lax.all_to_all(array, TILE, split_axis=0, concat_axis=0, tiled=True)  18 us
    all_to_all x2, starting transfers between devices, exchange(): return lax.all_to_all(array, TILE, split_axis=0, concat_axis=0, tiled=True)  13.3 us
    all_to_all x1, blocking collectives, whole_block(): lax.all_to_all(part, 'batch', split_axis=0, concat_axis=0, tiled=True)  8.16 us
  transfers between devices with their start and end apart: 2, of which 2 were waited for; matrix products, arithmetic and copies ran while one was open for 0% of the time, Pallas kernels for 13%

profile of v3, /device:TPU:1, one launch (start us, length us, event | category | flops | bytes accessed | tf_op | source)
XLA Modules:
  0.0 122.5 jit_solution(9248146954598241221)
XLA Ops:
  0.6 5.2 %shard_map.137 = (s32[8,128]{1,0:T(8,128)}, bf16[64,32,256]{2,1,0:T(8,128)(2,1)}, bf16[64,16,256]{2,1,0:T(8,128)(2,1)}, bf16[64,16,256]{2,1,0:T(8,128)(2,1)}) custom-call(s32[8,256]{1,0:T(8,128)} %bitcast.32, s32[8,256]{1,0:T(8,128)} %bitcast.33, bf16[2048,256]{1,0:T(8,128)(2,1)} %bitcast.19, bf16[2048,256]{1,0:T(8,128)(2,1)} %bitcast.23, ...), custom_call_target="tpu_custom_call" | custom-call | tf_op jit(solution)/shard_map/pallas_call | solution.py:675
  5.8 9.6 %all-to-all-start = ((bf16[32,64,256]{2,1,0:T(8,128)(2,1)}), bf16[32,64,256]{2,1,0:T(8,128)(2,1)S(1)}, u32[]{:S(2)}, u32[]{:S(2)}) async-start(bf16[32,64,256]{2,1,0:T(8,128)(2,1)} %bitcast.29), calls=%async_computation | async-start | bytes 2097152 | tf_op jit(solution)/shard_map/all_to_all | solution.py:688
  15.4 0.0 copy-start
  15.4 0.0 copy-start.1
  15.4 0.0 copy-start.2
  15.4 0.0 copy-start.3
  15.5 0.0 copy-start.4
  15.5 0.0 copy-start.5
  15.5 0.0 copy-start.6
  15.5 9.0 %shard_map.138 = (f32[2048,256]{1,0:T(8,128)}, f32[2560,256]{1,0:T(8,128)}, bf16[2048,256]{1,0:T(8,128)(2,1)}, bf16[64,16,256]{2,1,0:T(8,128)(2,1)}, bf16[64,16,256]{2,1,0:T(8,128)(2,1)}) custom-call(s32[8,128]{1,0:T(8,128)} %get-tuple-element.30.refs_0_, bf16[2048,256]{1,0:T(8,128)(2,1)} %bitcast.20, bf16[2048,256]{1,0:T(8,128)(2,1)} %bitcast.24, ...), custom_call_target="tpu_custom_call" | custom-call | tf_op jit(solution)/shard_map/pallas_call | solution.py:675
  24.5 7.8 %all-to-all-done = bf16[32,64,256]{2,1,0:T(8,128)(2,1)S(1)} async-done(((bf16[32,64,256]{2,1,0:T(8,128)(2,1)}), bf16[32,64,256]{2,1,0:T(8,128)(2,1)S(1)}, u32[]{:S(2)}, u32[]{:S(2)}) %all-to-all-start) | async-done | bytes 1048608 | tf_op jit(solution)/shard_map/all_to_all | solution.py:688
  32.4 9.9 %shard_map.139 = (bf16[2048,256]{1,0:T(8,128)(2,1)}, bf16[2048,256]{1,0:T(8,128)(2,1)}, bf16[2048,256]{1,0:T(8,128)(2,1)}, bf16[2048,256]{1,0:T(8,128)(2,1)}, bf...) custom-call(s32[8,128]{1,0:T(8,128)S(1)} %copy-done.5, ...), custom_call_target="tpu_custom_call" | custom-call | tf_op jit(solution)/shard_map/pallas_call | solution.py:675
  42.3 11.2 %shard_map.140 = (bf16[32,40,128]{2,1,0:T(8,128)(2,1)}, f32[2048,256]{1,0:T(8,128)}) custom-call(s32[8,128]{1,0:T(8,128)} %get-tuple-element.30.refs_0_, bf16[2048,256]{1,0:T(8,128)(2,1)} %bitcast.21, bf16[2048,256]{1,0:T(8,128)(2,1)} %bitcast.25, bf16[2048,256]{1,0:T(8,128)(2,1)} %get-tuple-element.38.refs_3_, bf16[2048,256]{1,0:T(8,128)(2,1)} %get-tuple-element.39.refs_4_, ...), custom_call_target="tpu_custom_call" | custom-call | tf_op jit(solution)/shard_map/pallas_call | solution.py:675
  53.6 13.6 %all_to_all.25.refs_0_ = bf16[32,40,128]{2,1,0:T(8,128)(2,1)S(1)} all-to-all(bf16[32,40,128]{2,1,0:T(8,128)(2,1)} %get-tuple-element.51), channel_id=1, replica_groups=mesh['tile_0'=4,'tile_1'=4,'tile_2'=2,'batch'=4] {'tile_0','tile_1','til..., dimensions={0} | all-to-all | bytes 655360 | tf_op jit(solution)/shard_map/all_to_all | solution.py:688
  67.2 0.1 shard_map.144
  67.2 8.2 %all_to_all.26.refs_0_ = bf16[4,40,128]{2,1,0:T(8,128)(2,1)S(1)} all-to-all(bf16[4,40,128]{2,1,0:T(8,128)(2,1)S(1)} %shard_map.144), channel_id=1, replica_groups=mesh['tile_0'=4,'tile_1'=4,'tile_2'=2,'batch'=4] {'batch'}, dimensions={0} | all-to-all | bytes 81920 | tf_op jit(solution)/shard_map/all_to_all | solution.py:771
  75.5 14.5 %all_to_all.27.refs_0_ = bf16[32,40,128]{2,1,0:T(8,128)(2,1)S(1)} all-to-all(bf16[32,40,128]{2,1,0:T(8,128)(2,1)S(1)} %shard_map.145), channel_id=1, replica_groups=mesh['tile_0'=4,'tile_1'=4,'tile_2'=2,'batch'=4] {'tile_0','tile_1','til..., dimensions={0} | all-to-all | bytes 655360 | tf_op jit(solution)/shard_map/all_to_all | solution.py:688
  89.9 3.7 %all-to-all-start.1 = ((bf16[32,64,256]{2,1,0:T(8,128)(2,1)}), bf16[32,64,256]{2,1,0:T(8,128)(2,1)S(1)}, u32[]{:S(2)}, u32[]{:S(2)}) async-start(bf16[32,64,256]{2,1,0:T(8,128)(2,1)} %bitcast.7), calls=%async_computation.1 | async-start | bytes 2097152 | tf_op jit(solution)/shard_map/all_to_all | solution.py:688
  93.6 5.3 %shard_map.142.refs_3_ = f32[2048,256]{1,0:T(8,128)} custom-call(bf16[2048,256]{1,0:T(8,128)(2,1)} %get-tuple-element.41.refs_6_.refs_0_, f32[9,2,256]{2,1,0:T(2,128)} %bitcast.15, bf16[512,256]{1,0:T(8,128)(2,1)} %constant.8.clone.refs_6_.refs_16_.refs_2_), custom_call_target="tpu_custom_call" | custom-call | tf_op jit(solution)/shard_map/pallas_call | solution.py:675
  99.0 1.4 %shard_map.146 = (f32[2,256,256]{2,1,0:T(8,128)}, f32[9,2,256]{2,1,0:T(2,128)}, f32[2,256]{1,0:T(2,128)}) custom-call(bf16[32,40,128]{2,1,0:T(8,128)(2,1)S(1)} %all_to_all.27.refs_0_), custom_call_target="tpu_custom_call" | custom-call | tf_op jit(solution)/shard_map/pallas_call | solution.py:675
  100.4 10.2 %all-to-all-done.1 = bf16[32,64,256]{2,1,0:T(8,128)(2,1)S(1)} async-done(((bf16[32,64,256]{2,1,0:T(8,128)(2,1)}), bf16[32,64,256]{2,1,0:T(8,128)(2,1)S(1)}, u32[]{:S(2)}, u32[]{:S(2)}) %all-to-all-start.1) | async-done | bytes 1048608 | tf_op jit(solution)/shard_map/all_to_all | solution.py:688
  110.6 1.0 copy-done.7
  111.6 5.6 %shard_map.141 = bf16[2048,256]{1,0:T(8,128)(2,1)} custom-call(s32[8,128]{1,0:T(8,128)} %get-tuple-element.30.refs_0_, bf16[64,32,256]{2,1,0:T(8,128)(2,1)} %bitcast.27, bf16[64,16,256]{2,1,0:T(8,128)(2,1)} %get-tuple-element.37.refs_8_.refs_2_, f32[2048,256]{1,0:T(8,128)} %get-tuple-element.49.refs_3_, bf16[2048,256]{1,0:T(8,128)(2,1)} %bitcast.22, ...), custom_call_target="tpu_custom_call" | custom-call | tf_op jit(solution)/shard_map/pallas_call | solution.py:675
  117.2 5.3 %shard_map.143 = bf16[2048,256]{1,0:T(8,128)(2,1)} custom-call(s32[8,128]{1,0:T(8,128)} %get-tuple-element.30.refs_0_, bf16[64,32,256]{2,1,0:T(8,128)(2,1)} %bitcast.28, bf16[64,16,256]{2,1,0:T(8,128)(2,1)} %get-tuple-element.50.refs_2_, f32[2048,256]{1,0:T(8,128)} %shard_map.142.refs_3_, bf16[2048,256]{1,0:T(8,128)(2,1)} %bitcast.26, ...), custom_call_target="tpu_custom_call" | custom-call | tf_op jit(solution)/shard_map/pallas_call | solution.py:675
  (9 shorter events, 0.1 us)
Async XLA Ops:
  5.8 26.5 %all-to-all-start = ((bf16[32,64,256]{2,1,0:T(8,128)(2,1)}), bf16[32,64,256]{2,1,0:T(8,128)(2,1)S(1)}, u32[]{:S(2)}, u32[]{:S(2)}) async-start(bf16[32,64,256]{2,1,0:T(8,128)(2,1)} %bitcast.29), calls=%async_computation | async-start | bytes 2097152 | tf_op jit(solution)/shard_map/all_to_all | solution.py:688
  15.4 16.9 %copy-start = (bf16[2,256,256]{2,1,0:T(8,128)(2,1)S(1)}, bf16[2,256,256]{2,1,0:T(8,128)(2,1)}, u32[]{:S(2)}) copy-start(bf16[2,256,256]{2,1,0:T(8,128)(2,1)} %refs_5_.3) | copy-start | bytes 786436
  15.4 16.9 %copy-start.1 = (f32[2,9,256]{2,0,1:T(2,128)S(1)}, f32[2,9,256]{2,0,1:T(2,128)}, u32[]{:S(2)}) copy-start(f32[2,9,256]{2,0,1:T(2,128)} %param.15) | copy-start | bytes 55300
  15.4 16.9 %copy-start.2 = (bf16[256,128]{1,0:T(8,128)(2,1)S(1)}, bf16[256,128]{1,0:T(8,128)(2,1)}, u32[]{:S(2)}) copy-start(bf16[256,128]{1,0:T(8,128)(2,1)} %constant.7.clone.refs_9_.refs_8_.refs_6_) | copy-start | bytes 196612
  15.4 16.9 %copy-start.3 = (bf16[64,16,256]{2,1,0:T(8,128)(2,1)S(1)}, bf16[64,16,256]{2,1,0:T(8,128)(2,1)}, u32[]{:S(2)}) copy-start(bf16[64,16,256]{2,1,0:T(8,128)(2,1)} %get-tuple-element.32.refs_2_) | copy-start | bytes 1572868
  15.5 16.9 %copy-start.4 = (bf16[256,256]{1,0:T(8,128)(2,1)S(1)}, bf16[256,256]{1,0:T(8,128)(2,1)}, u32[]{:S(2)}) copy-start(bf16[256,256]{1,0:T(8,128)(2,1)} %constant.6.clone.refs_4_.refs_8_) | copy-start | bytes 393220
  15.5 16.9 %copy-start.5 = (s32[8,128]{1,0:T(8,128)S(1)}, s32[8,128]{1,0:T(8,128)}, u32[]{:S(2)}) copy-start(s32[8,128]{1,0:T(8,128)} %get-tuple-element.30.refs_0_) | copy-start | bytes 12292
  15.5 16.9 %copy-start.6 = (f32[2,256]{1,0:T(2,128)S(1)}, f32[2,256]{1,0:T(2,128)}, u32[]{:S(2)}) copy-start(f32[2,256]{1,0:T(2,128)} %refs_7_.3) | copy-start | bytes 6148
  89.9 20.7 %all-to-all-start.1 = ((bf16[32,64,256]{2,1,0:T(8,128)(2,1)}), bf16[32,64,256]{2,1,0:T(8,128)(2,1)S(1)}, u32[]{:S(2)}, u32[]{:S(2)}) async-start(bf16[32,64,256]{2,1,0:T(8,128)(2,1)} %bitcast.7), calls=%async_computation.1 | async-start | bytes 2097152 | tf_op jit(solution)/shard_map/all_to_all | solution.py:688
  110.6 1.0 copy-start.7

commit v4 on v3

--- a/solution.py
+++ b/solution.py
@@ -68,6 +68,23 @@
             if j < S - 1:
                 out[256 + S * i + j, S * i + j + 1] = 1.0
     return out
+
+
+def line_matrices():
+    sel = selection()
+    lines = np.concatenate([sel[32 * d : 32 * d + S] for d in range(4)])
+    bank = np.zeros((256, 64), np.float32)
+    for row in range(256):
+        cells = np.flatnonzero(sel[row])
+        if cells.size:
+            bank[row, np.flatnonzero(lines[:, cells[0]])[0]] = 1.0
+    place = np.zeros((CELLS, 64), np.float32)
+    for cell in range(CELLS):
+        at = np.flatnonzero(lines[:, cell])
+        if at.size:
+            home = [q for q in at if (q // S) % 2 == 0] or list(at)
+            place[cell, home[0]] = 1.0
+    return bank, lines @ spreading(), place
 
 
 def dot(a, b):
@@ -321,44 +338,85 @@
     gather_out(leave, (1, 3), out_ref, own_ref, rims_ref, lines_ref, smem)
 
 
+def edge_cells():
+    row = iota((CELLS, 1), 0)
+    i, j = row >> 4, row & (S - 1)
+    return (i == 0) | (i == S - 1) | (j == 0) | (j == S - 1)
+
+
+def keep_lines(lines_ref, t, tile_ref):
+    at = [pl.ds(0, S), pl.ds(S - 1, S, stride=S), pl.ds(S * (S - 1), S), pl.ds(0, S, stride=S)]
+    for d in range(4):
+        for h in range(2):
+            lines_ref[pl.ds(pl.multiple_of(t * 64 + d * S, S), S), 128 * h : 128 * h + 128] = tile_ref[
+                h, at[d], :
+            ]
+
+
+def put_halves(tile_ref, value):
+    tile_ref[0] = value[:, 0:128]
+    tile_ref[1] = value[:, 128:256]
+
+
+def activation(hidden):
+    cdf = 0.5 * (1.0 + lax.erf(hidden * SQRT_HALF))
+    slope = cdf + hidden * jnp.exp(-0.5 * hidden * hidden) * INV_ROOT_TAU
+    return (hidden * cdf).astype(BF16), slope
+
+
 def inner_kernel(
-    arrive, leave, tab_ref, states_ref, cot_ref, own_in_ref, mixers_ref, stencils_ref, shift_ref,
-    conv_ref, back_ref, g_ref, c_ref, gl_ref, taps_ref,
+    arrive, leave, tab_ref, states_ref, cot_ref, own_in_ref, mixers_ref, stencils_ref, shifts_ref, shift_ref,
+    back_ref, g_ref, c_ref, gl_ref, active_ref, first_ref, gh_ref, gc_ref,
+    taps_ref, tile1_ref, tile2_ref,
 ):
     w0 = tap_rows(stencils_ref, 0)
     w1 = tap_rows(stencils_ref, 1)
     arrive(1)
     arrive(2)
+    edge = edge_cells()
 
     def one(t, carry):
         x = tile_of(states_ref, t)
         moved = dot(shift_ref[...], x)
-        put_tile(conv_ref, t, conv_inner(moved[:CELLS], x.astype(F32), moved[CELLS:], w0))
-        leave(0, t * CELLS, CELLS)
+        conv = conv_inner(moved[:CELLS], x.astype(F32), moved[CELLS:], w0)
+        put_halves(tile1_ref, conv)
+        keep_lines(back_ref, t + 2 * T, tile1_ref)
+        first = conv.astype(BF16)
+        put_tile(first_ref, t, first)
+        leave(5, t * CELLS, CELLS)
+        active, slope = activation(dot(first, mixers_ref[0]) + shifts_ref[0:1, :])
+        put_tile(active_ref, t, jnp.where(edge, 0.0, active.astype(F32)).astype(BF16))
+        leave(4, t * CELLS, CELLS)
         g = dot_t(tile_of(cot_ref, t), mixers_ref[1]).astype(BF16)
         put_tile(g_ref, t, g)
-        leave(2, t * CELLS, CELLS)
+        leave(1, t * CELLS, CELLS)
         moved = dot(shift_ref[...], g)
-        put_tile(back_ref, t, back_inner(moved[:CELLS], g.astype(F32), moved[CELLS:], w1))
-        leave(1, t * CELLS, CELLS)
+        back = back_inner(moved[:CELLS], g.astype(F32), moved[CELLS:], w1)
+        put_halves(tile2_ref, back)
+        keep_lines(back_ref, t, tile2_ref)
+        gh = jnp.where(edge, 0.0, back * slope).astype(BF16)
+        put_tile(gh_ref, t, gh)
+        leave(6, t * CELLS, CELLS)
+        put_tile(gc_ref, t, dot_t(gh, mixers_ref[0]).astype(BF16))
+        leave(7, t * CELLS, CELLS)
         return carry
 
     lax.fori_loop(0, T, one, 0)
     arrive(3)
     fill_tap_sets(taps_ref, stencils_ref, 1)
     live_lines(c_ref, 0, own_in_ref, 0, tab_ref, 0)
+    leave(2, 0, 64)
+    line_grads(gl_ref, c_ref, mixers_ref)
     leave(3, 0, 64)
-    line_grads(gl_ref, c_ref, mixers_ref)
-    leave(4, 0, 64)
-    back_ref[T * CELLS :] = jnp.zeros((2 * CELLS, 256), F32)
-    rim_gradients(back_ref, T * CELLS, gl_ref, tab_ref, taps_ref, 0, 64)
-    leave(1, T * CELLS, 2 * CELLS)
+    back_ref[2 * CELLS : 4 * CELLS] = jnp.zeros((2 * CELLS, 256), F32)
+    rim_gradients(back_ref, 2 * CELLS, gl_ref, tab_ref, taps_ref, 0, 64)
+    leave(0, 0, 6 * CELLS)
 
 
 def middle_kernel(
     arrive, leave,
-    tab_ref, in_ref, rims_in_ref, back_ref, conv_ref, mixers_ref, stencils_ref,
-    shifts_ref, sel_ref, spread_ref,
+    tab_ref, in_ref, rims_in_ref, back_ref, mixers_ref, stencils_ref,
+    shifts_ref, bank_ref, cross_ref,
     active_ref, first_ref, gh_ref, gc_ref, rims_ref, lines_ref, out_ref, own_ref, c_ref, g_ref, panels_ref,
     buf_ref, split_ref, split2_ref, taps_ref,
 ):
@@ -374,31 +432,34 @@
     forward_lines(split_ref, buf_ref, tab_ref, w0, panels_ref)
     leave(10, 0, 64)
     arrive(3)
-    rim_gradients(back_ref, T * CELLS, g_ref, tab_ref, taps_ref, 64, 64)
-    split_rims(split2_ref, back_ref, T * CELLS)
-    arrive(4)
-
-    def one(t, carry):
-        first = (tile_of(conv_ref, t) + dot(spread_ref[...], split_ref[t])).astype(BF16)
-        put_tile(first_ref, t, first)
-        leave(1, t * CELLS, CELLS)
-        hidden = dot(first, mixers_ref[0]) + shifts_ref[0:1, :]
-        cdf = 0.5 * (1.0 + lax.erf(hidden * SQRT_HALF))
-        active = (hidden * cdf).astype(BF16)
-        put_tile(active_ref, t, active)
-        leave(0, t * CELLS, CELLS)
-        slope = cdf + hidden * jnp.exp(-0.5 * hidden * hidden) * INV_ROOT_TAU
-        grad = tile_of(back_ref, t) + dot(spread_ref[...], split2_ref[t])
-        gh = (grad * slope).astype(BF16)
-        put_tile(gh_ref, t, gh)
-        leave(2, t * CELLS, CELLS)
-        gc = dot_t(gh, mixers_ref[0]).astype(BF16)
-        put_tile(gc_ref, t, gc)
-        leave(3, t * CELLS, CELLS)
-        banks(rims_ref, lines_ref, t, active, gc, sel_ref)
-        return carry
-
-    lax.fori_loop(0, T, one, 0, unroll=2)
+    rim_gradients(back_ref, 2 * CELLS, g_ref, tab_ref, taps_ref, 64, 64)
+    split_rims(split2_ref, back_ref, 2 * CELLS)
+    at = iota((CELLS, 1), 0)
+    twice = (((at >> 4) & 1) == 1) & (((at & (S - 1)) == 0) | ((at & (S - 1)) == S - 1))
+
+    def updates(ref, u):
+        return jnp.concatenate([dot(cross_ref[...], ref[4 * u + q]) for q in range(4)], axis=0)
+
+    for u in range(2):
+        part = slice(u * CELLS, (u + 1) * CELLS)
+        conv = back_ref[(u + 4) * CELLS : (u + 5) * CELLS]
+        first = (conv + updates(split_ref, u)).astype(BF16)
+        first_ref[part] = first
+        active, slope = activation(dot(first, mixers_ref[0]) + shifts_ref[0:1, :])
+        active_ref[part] = active
+        grad = (back_ref[part] + updates(split2_ref, u)) * slope
+        gh_ref[part] = jnp.where(twice, 0.0, grad).astype(BF16)
+        gc = dot_t(grad.astype(BF16), mixers_ref[0]).astype(BF16)
+        gc_ref[part] = gc
+        for q in range(4):
+            t = 4 * u + q
+            rows = slice(64 * q, 64 * q + 64)
+            rims = dot(bank_ref[0:128, :], active[rows]).astype(BF16)
+            rims_ref[8 * t : 8 * t + 8] = rims.reshape(8, S, 256)
+            lines = dot(bank_ref[...], gc[rows]).astype(BF16)
+            lines_ref[16 * t : 16 * t + 16] = lines.reshape(16, S, 256)
+    for k in range(4):
+        leave(k, 0, 2 * CELLS)
     leave(4, 0, 64)
     leave(5, 0, 128)
     gather_out(leave, (6, 7), out_ref, own_ref, rims_ref, lines_ref, tab_ref)
@@ -407,8 +468,9 @@
 def weight_kernel(
     arrive, leave,
     tab_ref, states_ref, cot_ref, active_ref, first_ref, gh_ref, gc_ref, g2_ref, rims_ref, lines_ref,
-    panels_ref, c_own_ref, g_own_ref, c_in_ref, g_in_ref, stencils_ref, shift_ref,
-    pack_ref, conv_ref,
+    panels_ref, c_own_ref, g_own_ref, c_in_ref, g_in_ref,
+    active_edge_ref, first_edge_ref, gh_edge_ref, gc_edge_ref, stencils_ref, shift_ref, place_ref,
+    pack_ref, conv_ref, gc_out_ref,
     second_ref, h_ref, taps_ref, acc1_ref, acc2_ref, accl_ref, sums_ref,
 ):
     w1 = tap_rows(stencils_ref, 1)
@@ -467,17 +529,24 @@
 
     lax.fori_loop(0, T, first_halo, 0, unroll=2)
 
-    for k in (6, 1, 3, 7, 5, 2):
+    for k in (6, 18, 1, 3, 15, 7, 5, 17, 2):
         arrive(k)
 
+    def whole(inner_ref, edge_ref, t):
+        edges = edge_ref[pl.ds(pl.multiple_of(t * 64, 64), 64), :]
+        return tile_of(inner_ref, t).astype(F32) + dot(place_ref[...], edges)
+
+    sums_ref[0] += folded(gh_edge_ref[...].astype(F32))
+
     def one(t, carry):
-        gcf = tile_of(gc_ref, t).astype(F32)
+        gcf = whole(gc_ref, gc_edge_ref, t)
+        put_tile(gc_out_ref, t, gcf.astype(BF16))
+        leave(2, t * CELLS, CELLS)
         x = tile_of(states_ref, t)
         moved = dot(shift_ref[...], x)
         taps_of(acc1_ref, gcf, moved[:CELLS], x.astype(F32), moved[CELLS:])
-        x = tile_of(active_ref, t)
-        moved = dot(shift_ref[...], x)
-        xf = x.astype(F32)
+        xf = whole(active_ref, active_edge_ref, t)
+        moved = dot(shift_ref[...], xf.astype(BF16))
         second = conv_inner(moved[:CELLS], xf, moved[CELLS:], w1)
         put_tile(conv_ref, t, second)
         leave(1, t * CELLS, CELLS)
@@ -488,7 +557,7 @@
         return carry
 
     lax.fori_loop(0, T, one, 0)
-    for k in (4, 11, 13):
+    for k in (4, 16, 11, 13):
         arrive(k)
     for d in range(8):
         for f in range(2):
@@ -514,7 +583,7 @@
             at = (q // 2) * 8, (q % 2) * 128
             pack_ref[r, 8 * q : 8 * q + 8] = rows16[at[0] : at[0] + 8, at[1] : at[1] + 128].astype(BF16)
 
-    mixer_first = t_dot(first_ref[...], gh_ref[...])
+    mixer_first = t_dot(first_ref[...], gh_ref[...]) + t_dot(first_edge_ref[...], gh_edge_ref[...])
     for r in range(half):
         put_rows(r, mixer_first[16 * r : 16 * r + 16])
     leave(0, 0, half)
@@ -528,25 +597,12 @@
     leave(0, half, half)
 
 
-def back_kernel(arrive, leave, gc_ref, stencils_ref, shift_ref, back_ref):
-    w0 = tap_rows(stencils_ref, 0)
-    arrive(0)
-
-    def one(t, carry):
-        gc = tile_of(gc_ref, t)
-        moved = dot(shift_ref[...], gc)
-        put_tile(back_ref, t, back_inner(moved[:CELLS], gc.astype(F32), moved[CELLS:], w0))
-        leave(0, t * CELLS, CELLS)
-        return carry
-
-    lax.fori_loop(0, T, one, 0)
-
-
 def outcome_kernel(
     arrive, leave,
-    tab_ref, in_ref, rims_in_ref, conv_ref, states_ref, mixers_ref, stencils_ref, shifts_ref, spread_ref,
-    outcome_ref,
-    buf_ref, split_ref,
+    tab_ref, in_ref, rims_in_ref, own_in_ref, conv_ref, states_ref, mixers_ref, stencils_ref, shifts_ref,
+    spread_ref,
+    outcome_ref, halo_ref,
+    buf_ref, split_ref, rim_ref, taps_ref, lines_ref,
 ):
     w1 = tap_rows(stencils_ref, 1)
     arrive(2)
@@ -554,8 +610,8 @@
     arrive(1)
     buf_ref[64:128] = in_ref[:, 0:S, :]
     forward_lines(split_ref, buf_ref, tab_ref, w1)
-    arrive(3)
     arrive(4)
+    arrive(5)
 
     def one(t, carry):
         second = (tile_of(conv_ref, t) + dot(spread_ref[...], split_ref[t])).astype(BF16)
@@ -565,32 +621,35 @@
         return carry
 
     lax.fori_loop(0, T, one, 0, unroll=2)
+    fill_tap_sets(taps_ref, stencils_ref, 0)
+    rim_ref[...] = jnp.zeros_like(rim_ref)
+    arrive(3)
+    live_lines(lines_ref, 0, own_in_ref, 0, tab_ref, 0)
+    live_lines(lines_ref, 64, in_ref, S, tab_ref, 64)
+    rim_gradients(rim_ref, 0, lines_ref, tab_ref, taps_ref, 0, 128)
+    split_rims(halo_ref, rim_ref, 0)
+    leave(1, 0, T)
 
 
 def grad_kernel(
     arrive, leave,
-    tab_ref, in_ref, own_in_ref, back_ref, cot_ref, stencils_ref, spread_ref,
+    gc_ref, halo_ref, cot_ref, stencils_ref, shift_ref, spread_ref,
     grad_ref,
-    lines_ref, split_ref, rim_ref, taps_ref,
 ):
-    fill_tap_sets(taps_ref, stencils_ref, 0)
-    rim_ref[...] = jnp.zeros_like(rim_ref)
-    arrive(2)
-    live_lines(lines_ref, 0, own_in_ref, 0, tab_ref, 0)
-    arrive(1)
-    live_lines(lines_ref, 64, in_ref, S, tab_ref, 64)
-    rim_gradients(rim_ref, 0, lines_ref, tab_ref, taps_ref, 0, 128)
-    split_rims(split_ref, rim_ref, 0)
-    arrive(3)
-    arrive(4)
+    w0 = tap_rows(stencils_ref, 0)
+    for k in range(3):
+        arrive(k)
 
     def one(t, carry):
-        grad = tile_of(back_ref, t) + dot(spread_ref[...], split_ref[t])
-        put_tile(grad_ref, t, (tile_of(cot_ref, t).astype(F32) + grad).astype(BF16))
+        gc = tile_of(gc_ref, t)
+        moved = dot(shift_ref[...], gc)
+        grad = back_inner(moved[:CELLS], gc.astype(F32), moved[CELLS:], w0)
+        grad = grad + dot(spread_ref[...], halo_ref[t]) + tile_of(cot_ref, t).astype(F32)
+        put_tile(grad_ref, t, grad.astype(BF16))
         leave(0, t * CELLS, CELLS)
         return carry
 
-    lax.fori_loop(0, T, one, 0, unroll=2)
+    lax.fori_loop(0, T, one, 0)
 
 
 def sum_kernel(arrive, leave, in_ref, out_ref):
@@ -721,31 +780,43 @@
         ],
     )
     in1 = exchange(out1.reshape(groups, 4 * S, 256)).reshape(64, 2 * S, 256)
-    conv1, back2, g2, c_own, g_own = call(
+    bank, cross, place = (jnp.asarray(m, BF16) for m in line_matrices())
+    edge = shape_of(2 * CELLS, 256)
+    tile_scratch = pltpu.VMEM((2, CELLS, 128), F32)
+    back2, g2, c_own, g_own, active, first, gh, gc = call(
         inner_kernel,
-        (tab, x, cot, own1, mixers, taps, shift),
-        "shhhvvv",
-        [wide, shape_of((T + 2) * CELLS, 256, dtype=F32), field, rims16, rims16],
-        "hhhhh",
-        [taps_scratch],
-    )
-    active, first, gh, gc, rims2, lines2, out2, own2, c_in, g_in, panels = call(
+        (tab, x, cot, own1, mixers, taps, shifts, shift),
+        "shhhvvvv",
+        [
+            shape_of(6 * CELLS, 256, dtype=F32),
+            field,
+            rims16,
+            rims16,
+            field,
+            field,
+            field,
+            field,
+        ],
+        "hhhhhhhh",
+        [taps_scratch, tile_scratch, tile_scratch],
+    )
+    active_e, first_e, gh_e, gc_e, rims2, lines2, out2, own2, c_in, g_in, panels = call(
         middle_kernel,
-        (tab, in1, rims1, back2, conv1, mixers, taps, shifts, sel, spread),
-        "svhhhvvvvv",
-        [field, field, field, field, rims16, lines16, sent16, rims16, rims16, rims16, rims16],
+        (tab, in1, rims1, back2, mixers, taps, shifts, bank, cross),
+        "svhhvvvvv",
+        [edge, edge, edge, edge, rims16, lines16, sent16, rims16, rims16, rims16, rims16],
         "hhhhhhhhhhh",
         [lines_scratch, split_scratch, split_scratch, taps_scratch],
         limit=51.0,
     )
     in2 = exchange(out2.reshape(groups, 4 * S, 256)).reshape(64, 2 * S, 256)
-    pack, conv2 = call(
+    pack, conv2, gc_all = call(
         weight_kernel,
         (tab, x, cot, active, first, gh, gc, g2, rims2, lines2, panels, c_own, g_own, c_in, g_in,
-         taps, shift),
-        "shhhhhhhhhhhhhhvv",
-        [shape_of(groups, 40, 128), wide],
-        "hh",
+         active_e, first_e, gh_e, gc_e, taps, shift, place),
+        "shhhhhhhhhhhhhhhhhhvvv",
+        [shape_of(groups, 40, 128), wide, field],
+        "hhh",
         [
             pltpu.VMEM((T * CELLS, 256), BF16),
             lines_scratch,
@@ -755,29 +826,24 @@
             pltpu.VMEM((16, 3, 8, 256), F32),
             pltpu.VMEM((2, 8, 256), F32),
         ],
-        order=(8, 12, 14, 9, 10, 6, 1, 3, 7, 5, 2, 4, 11, 13),
-    )
-    (back1,) = call(back_kernel, (gc, taps, shift), "hvv", [wide], "h")
+        order=(8, 12, 14, 9, 10, 6, 18, 1, 3, 15, 7, 5, 17, 2, 4, 16, 11, 13),
+    )
     parts = exchange(pack)
-    (outcome,) = call(
+    outcome, halo = call(
         outcome_kernel,
-        (tab, in2, rims2, conv2, x, mixers, taps, shifts, spread),
-        "shhhhvvvv",
-        [field],
-        "h",
-        [lines_scratch, split_scratch],
+        (tab, in2, rims2, own2, conv2, x, mixers, taps, shifts, spread),
+        "shhhhhvvvv",
+        [field, shape_of(T, 128, 256)],
+        "hh",
+        [lines_scratch, split_scratch, rim_scratch, taps_scratch, lines_scratch],
+        order=(2, 1, 4, 5, 3),
     )
     (part,) = call(sum_kernel, (parts,), "v", [shape_of(batch, 40, 128)], "v", limit=4)
     part = lax.all_to_all(part, "batch", split_axis=0, concat_axis=0, tiled=True)
     (spread_out,) = call(spread_kernel, (part,), "v", [shape_of(groups, 40, 128)], "v", limit=4)
     whole = exchange(spread_out)
     (state_grad,) = call(
-        grad_kernel,
-        (tab, in2, own2, back1, cot, taps, spread),
-        "shhhhvv",
-        [field],
-        "h",
-        [lines_scratch, split_scratch, rim_scratch, taps_scratch],
+        grad_kernel, (gc_all, halo, cot, taps, shift, spread), "hhhvvv", [field], "h"
     )
     scale = 1.0 / math.sqrt(T * CELLS * groups * batch)
 

time: 123 us -> 123 us (level)
  Pallas kernels: 53.1 us -> 51.5 us
    pallas_call x10 -> x9, Pallas kernels: 53.1 us -> 51.5 us  [call(): pl.pallas_call(kernel, out_shape=[pltpu.HBM(o.shape, o.dtype) if m == 'h'...]
  transfers between devices with their start and end apart: 2 -> 2, of which waited for: 2 -> 2; matrix products, arithmetic and copies ran while one was open for 0% -> 0% of each run, Pallas kernels for 13% -> 12%
where the time goes in v4:
time: 123 us; the launch traced here: 122 us
  Pallas kernels  51.5 us (42%)
  blocking collectives  36.2 us (29%)
  waiting for transfers between devices  19.2 us (16%)
  starting transfers between devices  13.3 us (11%)
    pallas_call x9, Pallas kernels, call(): pl.pallas_call(kernel, out_shape=[pltpu.HBM(o.shape, o.dtype) if m == 'h'...  51.5 us
    all_to_all x2, blocking collectives, exchange(): return lax.all_to_all(array, TILE, split_axis=0, concat_axis=0, tiled=True)  28 us
    all_to_all x2, waiting for transfers between devices, exchange(): return lax.all_to_all(array, TILE, split_axis=0, concat_axis=0, tiled=True)  19.2 us
    all_to_all x2, starting transfers between devices, exchange(): return lax.all_to_all(array, TILE, split_axis=0, concat_axis=0, tiled=True)  13.3 us
    all_to_all x1, blocking collectives, whole_block(): lax.all_to_all(part, 'batch', split_axis=0, concat_axis=0, tiled=True)  8.14 us
  transfers between devices with their start and end apart: 2, of which 2 were waited for; matrix products, arithmetic and copies ran while one was open for 0% of the time, Pallas kernels for 12%

profile of v4, /device:TPU:1, one launch (start us, length us, event | category | flops | bytes accessed | tf_op | source)
XLA Modules:
  0.0 122.0 jit_solution(11054406697971344638)
XLA Ops:
  0.6 5.1 %shard_map.164 = (s32[8,128]{1,0:T(8,128)}, bf16[64,32,256]{2,1,0:T(8,128)(2,1)}, bf16[64,16,256]{2,1,0:T(8,128)(2,1)}, bf16[64,16,256]{2,1,0:T(8,128)(2,1)}) custom-call(s32[8,256]{1,0:T(8,128)} %bitcast.29, s32[8,256]{1,0:T(8,128)} %bitcast.30, bf16[2048,256]{1,0:T(8,128)(2,1)} %bitcast.22, bf16[2048,256]{1,0:T(8,128)(2,1)} %bitcast.18, ...), custom_call_target="tpu_custom_call" | custom-call | tf_op jit(solution)/shard_map/pallas_call | solution.py:734
  5.8 9.6 %all-to-all-start = ((bf16[32,64,256]{2,1,0:T(8,128)(2,1)}), bf16[32,64,256]{2,1,0:T(8,128)(2,1)S(1)}, u32[]{:S(2)}, u32[]{:S(2)}) async-start(bf16[32,64,256]{2,1,0:T(8,128)(2,1)} %bitcast.28), calls=%async_computation | async-start | bytes 2097152 | tf_op jit(solution)/shard_map/all_to_all | solution.py:747
  15.4 0.0 copy-start
  15.4 0.0 copy-start.1
  15.4 0.0 copy-start.2
  15.4 0.0 copy-start.3
  15.4 0.0 copy-start.4
  15.4 0.0 copy-start.5
  15.5 0.0 copy-start.6
  15.5 13.2 %shard_map.165 = (f32[1536,256]{1,0:T(8,128)}, bf16[2048,256]{1,0:T(8,128)(2,1)}, bf16[64,16,256]{2,1,0:T(8,128)(2,1)}, bf16[64,16,256]{2,1,0:T(8,128)(2,1)}, bf...) custom-call(s32[8,128]{1,0:T(8,128)} %get-tuple-element.36.refs_0_, ...), custom_call_target="tpu_custom_call" | custom-call | tf_op jit(solution)/shard_map/pallas_call | solution.py:734
  28.7 3.6 %all-to-all-done = bf16[32,64,256]{2,1,0:T(8,128)(2,1)S(1)} async-done(((bf16[32,64,256]{2,1,0:T(8,128)(2,1)}), bf16[32,64,256]{2,1,0:T(8,128)(2,1)S(1)}, u32[]{:S(2)}, u32[]{:S(2)}) %all-to-all-start) | async-done | bytes 1048608 | tf_op jit(solution)/shard_map/all_to_all | solution.py:747
  32.3 0.0 copy-done
  32.3 6.0 %shard_map.166 = (bf16[512,256]{1,0:T(8,128)(2,1)}, bf16[512,256]{1,0:T(8,128)(2,1)}, bf16[512,256]{1,0:T(8,128)(2,1)}, bf16[512,256]{1,0:T(8,128)(2,1)}, bf16[6...) custom-call(s32[8,128]{1,0:T(8,128)S(1)} %copy-done.3, ...), custom_call_target="tpu_custom_call" | custom-call | tf_op jit(solution)/shard_map/pallas_call | solution.py:734
  38.4 12.3 %shard_map.167 = (bf16[32,40,128]{2,1,0:T(8,128)(2,1)}, f32[2048,256]{1,0:T(8,128)}, bf16[2048,256]{1,0:T(8,128)(2,1)}) custom-call(s32[8,128]{1,0:T(8,128)} %get-tuple-element.36.refs_0_, bf16[2048,256]{1,0:T(8,128)(2,1)} %bitcast.24, bf16[2048,256]{1,0:T(8,128)(2,1)} %bitcast.20, bf16[2048,256]{1,0:T(8,128)(2,1)} %get-tuple-element.44.refs_3_, ...), custom_call_target="tpu_custom_call" | custom-call | tf_op jit(solution)/shard_map/pallas_call | solution.py:734
  50.7 13.6 %all_to_all.25.refs_0_ = bf16[32,40,128]{2,1,0:T(8,128)(2,1)S(1)} all-to-all(bf16[32,40,128]{2,1,0:T(8,128)(2,1)} %get-tuple-element.63), channel_id=1, replica_groups=mesh['tile_0'=4,'tile_1'=4,'tile_2'=2,'batch'=4] {'tile_0','tile_1','til..., dimensions={0} | all-to-all | bytes 655360 | tf_op jit(solution)/shard_map/all_to_all | solution.py:747
  64.3 0.1 shard_map.170
  64.3 8.1 %all_to_all.26.refs_0_ = bf16[4,40,128]{2,1,0:T(8,128)(2,1)S(1)} all-to-all(bf16[4,40,128]{2,1,0:T(8,128)(2,1)S(1)} %shard_map.170), channel_id=1, replica_groups=mesh['tile_0'=4,'tile_1'=4,'tile_2'=2,'batch'=4] {'batch'}, dimensions={0} | all-to-all | bytes 81920 | tf_op jit(solution)/shard_map/all_to_all | solution.py:842
  72.5 14.5 %all_to_all.27.refs_0_ = bf16[32,40,128]{2,1,0:T(8,128)(2,1)S(1)} all-to-all(bf16[32,40,128]{2,1,0:T(8,128)(2,1)S(1)} %shard_map.171), channel_id=1, replica_groups=mesh['tile_0'=4,'tile_1'=4,'tile_2'=2,'batch'=4] {'tile_0','tile_1','til..., dimensions={0} | all-to-all | bytes 655360 | tf_op jit(solution)/shard_map/all_to_all | solution.py:747
  87.0 3.7 %all-to-all-start.1 = ((bf16[32,64,256]{2,1,0:T(8,128)(2,1)}), bf16[32,64,256]{2,1,0:T(8,128)(2,1)S(1)}, u32[]{:S(2)}, u32[]{:S(2)}) async-start(bf16[32,64,256]{2,1,0:T(8,128)(2,1)} %bitcast.7), calls=%async_computation.1 | async-start | bytes 2097152 | tf_op jit(solution)/shard_map/all_to_all | solution.py:747
  90.7 1.4 %shard_map.172 = (f32[2,256,256]{2,1,0:T(8,128)}, f32[9,2,256]{2,1,0:T(2,128)}, f32[2,256]{1,0:T(2,128)}) custom-call(bf16[32,40,128]{2,1,0:T(8,128)(2,1)S(1)} %all_to_all.27.refs_0_), custom_call_target="tpu_custom_call" | custom-call | tf_op jit(solution)/shard_map/pallas_call | solution.py:734
  92.2 15.5 %all-to-all-done.1 = bf16[32,64,256]{2,1,0:T(8,128)(2,1)S(1)} async-done(((bf16[32,64,256]{2,1,0:T(8,128)(2,1)}), bf16[32,64,256]{2,1,0:T(8,128)(2,1)S(1)}, u32[]{:S(2)}, u32[]{:S(2)}) %all-to-all-start.1) | async-done | bytes 1048608 | tf_op jit(solution)/shard_map/all_to_all | solution.py:747
  107.7 1.0 copy-done.7
  108.7 7.2 %shard_map.168 = (bf16[2048,256]{1,0:T(8,128)(2,1)}, bf16[8,128,256]{2,1,0:T(8,128)(2,1)}) custom-call(s32[8,128]{1,0:T(8,128)} %get-tuple-element.36.refs_0_, bf16[64,32,256]{2,1,0:T(8,128)(2,1)} %bitcast.26, bf16[64,16,256]{2,1,0:T(8,128)(2,1)} %get-tuple-element.42.refs_8_.refs_2_, bf16[64,16,256]{2,1,0:T(8,128)(2,1)} %get-tuple-element.43.refs_3_, ...), custom_call_target="tpu_custom_call" | custom-call | tf_op jit(solution)/shard_map/pallas_call | solution.py:734
  115.9 6.1 %shard_map.169 = bf16[2048,256]{1,0:T(8,128)(2,1)} custom-call(bf16[2048,256]{1,0:T(8,128)(2,1)} %get-tuple-element.61.refs_0_, bf16[8,128,256]{2,1,0:T(8,128)(2,1)} %get-tuple-element.62.refs_1_, bf16[2048,256]{1,0:T(8,128)(2,1)} %bitcast.21, f32[9,2,256]{2,1,0:T(2,128)} %bitcast.16, bf16[512,256]{1,0:T(8,128)(2,1)} %constant.14.clone.refs_7_.refs_20_.refs_4_, ...), custom_call_target="tpu_custom_call" | custom-call | tf_op jit(solution)/shard_map/pallas_call | solution.py:734
  (8 shorter events, 0.1 us)
Async XLA Ops:
  5.8 26.5 %all-to-all-start = ((bf16[32,64,256]{2,1,0:T(8,128)(2,1)}), bf16[32,64,256]{2,1,0:T(8,128)(2,1)S(1)}, u32[]{:S(2)}, u32[]{:S(2)}) async-start(bf16[32,64,256]{2,1,0:T(8,128)(2,1)} %bitcast.28), calls=%async_computation | async-start | bytes 2097152 | tf_op jit(solution)/shard_map/all_to_all | solution.py:747
  15.4 16.9 %copy-start = (bf16[2,256,256]{2,1,0:T(8,128)(2,1)S(1)}, bf16[2,256,256]{2,1,0:T(8,128)(2,1)}, u32[]{:S(2)}) copy-start(bf16[2,256,256]{2,1,0:T(8,128)(2,1)} %refs_6_.5) | copy-start | bytes 786436
  15.4 16.9 %copy-start.1 = (bf16[64,16,256]{2,1,0:T(8,128)(2,1)S(1)}, bf16[64,16,256]{2,1,0:T(8,128)(2,1)}, u32[]{:S(2)}) copy-start(bf16[64,16,256]{2,1,0:T(8,128)(2,1)} %get-tuple-element.38.refs_2_) | copy-start | bytes 1572868
  15.4 16.9 %copy-start.2 = (f32[2,9,256]{2,0,1:T(2,128)S(1)}, f32[2,9,256]{2,0,1:T(2,128)}, u32[]{:S(2)}) copy-start(f32[2,9,256]{2,0,1:T(2,128)} %param.18) | copy-start | bytes 55300
  15.4 16.9 %copy-start.3 = (s32[8,128]{1,0:T(8,128)S(1)}, s32[8,128]{1,0:T(8,128)}, u32[]{:S(2)}) copy-start(s32[8,128]{1,0:T(8,128)} %get-tuple-element.36.refs_0_) | copy-start | bytes 12292
  15.4 16.9 %copy-start.4 = (bf16[256,64]{1,0:T(8,128)(2,1)S(1)}, bf16[256,64]{1,0:T(8,128)(2,1)}, u32[]{:S(2)}) copy-start(bf16[256,64]{1,0:T(8,128)(2,1)} %constant.15.clone.refs_7_) | copy-start | bytes 98308
  15.4 16.9 %copy-start.5 = (f32[2,256]{1,0:T(2,128)S(1)}, f32[2,256]{1,0:T(2,128)}, u32[]{:S(2)}) copy-start(f32[2,256]{1,0:T(2,128)} %refs_8_.2) | copy-start | bytes 6148
  15.5 16.9 %copy-start.6 = (bf16[64,128]{1,0:T(8,128)(2,1)S(1)}, bf16[64,128]{1,0:T(8,128)(2,1)}, u32[]{:S(2)}) copy-start(bf16[64,128]{1,0:T(8,128)(2,1)} %constant.16.clone.refs_8_) | copy-start | bytes 49156
  87.0 20.7 %all-to-all-start.1 = ((bf16[32,64,256]{2,1,0:T(8,128)(2,1)}), bf16[32,64,256]{2,1,0:T(8,128)(2,1)S(1)}, u32[]{:S(2)}, u32[]{:S(2)}) async-start(bf16[32,64,256]{2,1,0:T(8,128)(2,1)} %bitcast.7), calls=%async_computation.1 | async-start | bytes 2097152 | tf_op jit(solution)/shard_map/all_to_all | solution.py:747
  107.7 1.0 copy-start.7

commit v5 on v4

--- a/solution.py
+++ b/solution.py
@@ -73,18 +73,14 @@
 def line_matrices():
     sel = selection()
     lines = np.concatenate([sel[32 * d : 32 * d + S] for d in range(4)])
-    bank = np.zeros((256, 64), np.float32)
-    for row in range(256):
-        cells = np.flatnonzero(sel[row])
-        if cells.size:
-            bank[row, np.flatnonzero(lines[:, cells[0]])[0]] = 1.0
+    turn = np.kron(np.eye(4), np.eye(S)[::-1]).astype(np.float32)
     place = np.zeros((CELLS, 64), np.float32)
     for cell in range(CELLS):
         at = np.flatnonzero(lines[:, cell])
         if at.size:
             home = [q for q in at if (q // S) % 2 == 0] or list(at)
             place[cell, home[0]] = 1.0
-    return bank, lines @ spreading(), place
+    return turn, lines @ spreading(), place
 
 
 def dot(a, b):
@@ -214,11 +210,10 @@
     lax.fori_loop(0, T, split, 0, unroll=2)
 
 
-def live_lines(dst_ref, dst_first, src_ref, offset, tab_ref, tab_first):
+def live_lines(dst_ref, dst_first, line_of, tab_ref, tab_first):
     def one(i, carry):
-        line = src_ref[i, offset : offset + S]
         live = tab_ref[4, tab_first + i] > 0
-        dst_ref[dst_first + i] = jnp.where(live, line, jnp.zeros((S, 256), BF16))
+        dst_ref[dst_first + i] = jnp.where(live, line_of(i), jnp.zeros((S, 256), BF16))
         return carry
 
     lax.fori_loop(0, 64, one, 0, unroll=8)
@@ -230,25 +225,50 @@
         g_ref[b * 16 : b * 16 + 16] = dot_t(part, mixers_ref[1]).astype(BF16).reshape(16, S, 256)
 
 
-def gather_out(leave, ports, out_ref, own_ref, rims_ref, lines_ref, tab_ref):
+def gather_out(leave, port, out_ref, rims_ref, lines_ref, tab_ref):
     def some(q, carry):
-        for r in range(16):
-            s = q * 16 + r
+        for r in range(8):
+            s = q * 8 + r
             out_ref[s, 0:S] = rims_ref[tab_ref[2, 64 + s]]
             out_ref[s, S : 2 * S] = lines_ref[tab_ref[1, s]]
-            own_ref[s] = lines_ref[tab_ref[5, s]]
-        leave(ports[0], q * 16, 16)
-        leave(ports[1], q * 16, 16)
-        return carry
-
-    lax.fori_loop(0, 4, some, 0)
+        leave(port, q * 8, 8)
+        return carry
+
+    lax.fori_loop(0, 8, some, 0)
+
+
+CORNER_SOURCE = {4: (0, 1), 5: (2, 1), 6: (2, 0), 7: (0, 0)}
+
+
+def put_corners(lines_ref, t, sides):
+    at = iota((S, 1), 0)
+    for d, (side, flip) in CORNER_SOURCE.items():
+        for f in range(2):
+            value = jnp.where(at == (S - 1 if f else 0), sides[side][flip ^ f], 0.0)
+            lines_ref[16 * t + 2 * d + f] = value.astype(BF16)
 
 
 def banks(rims_ref, lines_ref, t, rim_tile, line_tile, sel_ref):
-    rims = dot(sel_ref[0:128, :], rim_tile).astype(BF16)
+    rims = dot(sel_ref[...], rim_tile).astype(BF16)
     rims_ref[pl.ds(t * 8, 8)] = rims.reshape(8, S, 256)
-    lines = dot(sel_ref[...], line_tile).astype(BF16)
-    lines_ref[pl.ds(t * 16, 16)] = lines.reshape(16, S, 256)
+    lines = dot(sel_ref[...], line_tile)
+    lines_ref[pl.ds(t * 16, 8)] = lines.astype(BF16).reshape(8, S, 256)
+    groups = [lines[S * k : S * k + S] for k in range(8)]
+    put_corners(lines_ref, t, [groups[2 * d : 2 * d + 2] for d in range(4)])
+
+
+def edge_banks(rims_ref, lines_ref, t, active, gc, turn_ref):
+    turned = dot(turn_ref[...], active).astype(BF16)
+    back = dot(turn_ref[...], gc)
+    sides = []
+    for d in range(4):
+        part = slice(S * d, S * d + S)
+        rims_ref[8 * t + 2 * d] = active[part]
+        rims_ref[8 * t + 2 * d + 1] = turned[part]
+        lines_ref[16 * t + 2 * d] = gc[part]
+        lines_ref[16 * t + 2 * d + 1] = back[part].astype(BF16)
+        sides.append((gc[part].astype(F32), back[part]))
+    put_corners(lines_ref, t, sides)
 
 
 def own_position():
@@ -257,8 +277,8 @@
 
 
 def first_kernel(
-    arrive, leave, slot_ref, code_ref, states_ref, cot_ref, sel_ref, tab_ref, out_ref, rims_ref, own_ref,
-    lines_ref, comb_ref, smem, sem,
+    arrive, leave, slot_ref, code_ref, states_ref, cot_ref, sel_ref, tab_ref, out_ref, rims_ref, lines_ref,
+    comb_ref, smem, sem,
 ):
     me = own_position()
     entries = slot_ref.shape[1]
@@ -334,8 +354,9 @@
 
     lax.fori_loop(0, T, lines_of, 0, unroll=4)
     leave(2, 0, 64)
+    leave(3, 0, 128)
     copy.wait()
-    gather_out(leave, (1, 3), out_ref, own_ref, rims_ref, lines_ref, smem)
+    gather_out(leave, 1, out_ref, rims_ref, lines_ref, smem)
 
 
 def edge_cells():
@@ -365,7 +386,7 @@
 
 
 def inner_kernel(
-    arrive, leave, tab_ref, states_ref, cot_ref, own_in_ref, mixers_ref, stencils_ref, shifts_ref, shift_ref,
+    arrive, leave, tab_ref, states_ref, cot_ref, bank_ref, mixers_ref, stencils_ref, shifts_ref, shift_ref,
     back_ref, g_ref, c_ref, gl_ref, active_ref, first_ref, gh_ref, gc_ref,
     taps_ref, tile1_ref, tile2_ref,
 ):
@@ -404,7 +425,7 @@
     lax.fori_loop(0, T, one, 0)
     arrive(3)
     fill_tap_sets(taps_ref, stencils_ref, 1)
-    live_lines(c_ref, 0, own_in_ref, 0, tab_ref, 0)
+    live_lines(c_ref, 0, lambda i: bank_ref[tab_ref[5, i]], tab_ref, 0)
     leave(2, 0, 64)
     line_grads(gl_ref, c_ref, mixers_ref)
     leave(3, 0, 64)
@@ -416,21 +437,21 @@
 def middle_kernel(
     arrive, leave,
     tab_ref, in_ref, rims_in_ref, back_ref, mixers_ref, stencils_ref,
-    shifts_ref, bank_ref, cross_ref,
-    active_ref, first_ref, gh_ref, gc_ref, rims_ref, lines_ref, out_ref, own_ref, c_ref, g_ref, panels_ref,
+    shifts_ref, turn_ref, cross_ref,
+    active_ref, first_ref, gh_ref, gc_ref, rims_ref, lines_ref, out_ref, c_ref, g_ref, panels_ref,
     buf_ref, split_ref, split2_ref, taps_ref,
 ):
     w0 = tap_rows(stencils_ref, 0)
     fill_tap_sets(taps_ref, stencils_ref, 1)
     buf_ref[64:128] = in_ref[:, 0:S, :]
-    live_lines(c_ref, 0, in_ref, S, tab_ref, 64)
+    live_lines(c_ref, 0, lambda i: in_ref[i, S : 2 * S], tab_ref, 64)
+    leave(7, 0, 64)
+    line_grads(g_ref, c_ref, mixers_ref)
     leave(8, 0, 64)
-    line_grads(g_ref, c_ref, mixers_ref)
-    leave(9, 0, 64)
     arrive(2)
     buf_ref[0:64] = rims_in_ref[...]
     forward_lines(split_ref, buf_ref, tab_ref, w0, panels_ref)
-    leave(10, 0, 64)
+    leave(9, 0, 64)
     arrive(3)
     rim_gradients(back_ref, 2 * CELLS, g_ref, tab_ref, taps_ref, 64, 64)
     split_rims(split2_ref, back_ref, 2 * CELLS)
@@ -454,15 +475,12 @@
         for q in range(4):
             t = 4 * u + q
             rows = slice(64 * q, 64 * q + 64)
-            rims = dot(bank_ref[0:128, :], active[rows]).astype(BF16)
-            rims_ref[8 * t : 8 * t + 8] = rims.reshape(8, S, 256)
-            lines = dot(bank_ref[...], gc[rows]).astype(BF16)
-            lines_ref[16 * t : 16 * t + 16] = lines.reshape(16, S, 256)
+            edge_banks(rims_ref, lines_ref, t, active[rows], gc[rows], turn_ref)
     for k in range(4):
         leave(k, 0, 2 * CELLS)
     leave(4, 0, 64)
     leave(5, 0, 128)
-    gather_out(leave, (6, 7), out_ref, own_ref, rims_ref, lines_ref, tab_ref)
+    gather_out(leave, 6, out_ref, rims_ref, lines_ref, tab_ref)
 
 
 def weight_kernel(
@@ -599,7 +617,7 @@
 
 def outcome_kernel(
     arrive, leave,
-    tab_ref, in_ref, rims_in_ref, own_in_ref, conv_ref, states_ref, mixers_ref, stencils_ref, shifts_ref,
+    tab_ref, in_ref, rims_in_ref, bank_ref, conv_ref, states_ref, mixers_ref, stencils_ref, shifts_ref,
     spread_ref,
     outcome_ref, halo_ref,
     buf_ref, split_ref, rim_ref, taps_ref, lines_ref,
@@ -624,8 +642,8 @@
     fill_tap_sets(taps_ref, stencils_ref, 0)
     rim_ref[...] = jnp.zeros_like(rim_ref)
     arrive(3)
-    live_lines(lines_ref, 0, own_in_ref, 0, tab_ref, 0)
-    live_lines(lines_ref, 64, in_ref, S, tab_ref, 64)
+    live_lines(lines_ref, 0, lambda i: bank_ref[tab_ref[5, i]], tab_ref, 0)
+    live_lines(lines_ref, 64, lambda i: in_ref[i, S : 2 * S], tab_ref, 64)
     rim_gradients(rim_ref, 0, lines_ref, tab_ref, taps_ref, 0, 128)
     split_rims(halo_ref, rim_ref, 0)
     leave(1, 0, T)
@@ -753,7 +771,7 @@
     shape = states.shape
     x = states.reshape(T * CELLS, 256)
     cot = cotangent.reshape(T * CELLS, 256)
-    sel = jnp.asarray(selection(), BF16)
+    sel = jnp.asarray(selection()[:128], BF16)
     spread = jnp.asarray(spreading(), BF16)
     shift = jnp.asarray(shifting(), BF16)
     taps = stencils.swapaxes(0, 1)
@@ -766,26 +784,25 @@
     split_scratch = pltpu.VMEM((T, 128, 256), BF16)
     rim_scratch = pltpu.VMEM((2 * CELLS, 256), F32)
     taps_scratch = pltpu.VMEM((16, 3, 256), F32)
-    tab, out1, rims1, own1 = call(
+    tab, out1, rims1, lines1 = call(
         first_kernel,
         (beside_slot.astype(I32).T, beside_code.astype(I32).T, x, cot, sel),
         "vvhhv",
-        [shape_of(8, 128, dtype=I32), sent16, rims16, rims16],
+        [shape_of(8, 128, dtype=I32), sent16, rims16, lines16],
         "vhhh",
         [
-            lines_scratch,
             pltpu.VMEM((groups, 128), I32),
             pltpu.SMEM((8, 128), I32),
             pltpu.SemaphoreType.DMA,
         ],
     )
     in1 = exchange(out1.reshape(groups, 4 * S, 256)).reshape(64, 2 * S, 256)
-    bank, cross, place = (jnp.asarray(m, BF16) for m in line_matrices())
+    turn, cross, place = (jnp.asarray(m, BF16) for m in line_matrices())
     edge = shape_of(2 * CELLS, 256)
     tile_scratch = pltpu.VMEM((2, CELLS, 128), F32)
     back2, g2, c_own, g_own, active, first, gh, gc = call(
         inner_kernel,
-        (tab, x, cot, own1, mixers, taps, shifts, shift),
+        (tab, x, cot, lines1, mixers, taps, shifts, shift),
         "shhhvvvv",
         [
             shape_of(6 * CELLS, 256, dtype=F32),
@@ -800,12 +817,12 @@
         "hhhhhhhh",
         [taps_scratch, tile_scratch, tile_scratch],
     )
-    active_e, first_e, gh_e, gc_e, rims2, lines2, out2, own2, c_in, g_in, panels = call(
+    active_e, first_e, gh_e, gc_e, rims2, lines2, out2, c_in, g_in, panels = call(
         middle_kernel,
-        (tab, in1, rims1, back2, mixers, taps, shifts, bank, cross),
+        (tab, in1, rims1, back2, mixers, taps, shifts, turn, cross),
         "svhhvvvvv",
-        [edge, edge, edge, edge, rims16, lines16, sent16, rims16, rims16, rims16, rims16],
-        "hhhhhhhhhhh",
+        [edge, edge, edge, edge, rims16, lines16, sent16, rims16, rims16, rims16],
+        "hhhhhhhhhh",
         [lines_scratch, split_scratch, split_scratch, taps_scratch],
         limit=51.0,
     )
@@ -831,7 +848,7 @@
     parts = exchange(pack)
     outcome, halo = call(
         outcome_kernel,
-        (tab, in2, rims2, own2, conv2, x, mixers, taps, shifts, spread),
+        (tab, in2, rims2, lines2, conv2, x, mixers, taps, shifts, spread),
         "shhhhhvvvv",
         [field, shape_of(T, 128, 256)],
         "hh",

time: 123 us -> 123 us (level)
  no operation moved by 1% of the time
where the time goes in v5:
time: 123 us; the launch traced here: 122 us
  Pallas kernels  51.3 us (42%)
  blocking collectives  36.2 us (29%)
  waiting for transfers between devices  19.1 us (16%)
  starting transfers between devices  13.3 us (11%)
    pallas_call x9, Pallas kernels, call(): pl.pallas_call(kernel, out_shape=[pltpu.HBM(o.shape, o.dtype) if m == 'h'...  51.3 us
    all_to_all x2, blocking collectives, exchange(): return lax.all_to_all(array, TILE, split_axis=0, concat_axis=0, tiled=True)  28 us
    all_to_all x2, waiting for transfers between devices, exchange(): return lax.all_to_all(array, TILE, split_axis=0, concat_axis=0, tiled=True)  19.1 us
    all_to_all x2, starting transfers between devices, exchange(): return lax.all_to_all(array, TILE, split_axis=0, concat_axis=0, tiled=True)  13.3 us
    all_to_all x1, blocking collectives, whole_block(): lax.all_to_all(part, 'batch', split_axis=0, concat_axis=0, tiled=True)  8.13 us
  transfers between devices with their start and end apart: 2, of which 2 were waited for; matrix products, arithmetic and copies ran while one was open for 0% of the time, Pallas kernels for 12%

profile of v5, /device:TPU:1, one launch (start us, length us, event | category | flops | bytes accessed | tf_op | source)
XLA Modules:
  0.0 121.8 jit_solution(7646677022589706776)
XLA Ops:
  0.6 5.2 %shard_map.164 = (s32[8,128]{1,0:T(8,128)}, bf16[64,32,256]{2,1,0:T(8,128)(2,1)}, bf16[64,16,256]{2,1,0:T(8,128)(2,1)}, bf16[128,16,256]{2,1,0:T(8,128)(2,1)}) custom-call(s32[8,256]{1,0:T(8,128)} %bitcast.29, s32[8,256]{1,0:T(8,128)} %bitcast.30, bf16[2048,256]{1,0:T(8,128)(2,1)} %bitcast.22, bf16[2048,256]{1,0:T(8,128)(2,1)} %bitcast.18, ...), custom_call_target="tpu_custom_call" | custom-call | tf_op jit(solution)/shard_map/pallas_call | solution.py:752
  5.8 9.6 %all-to-all-start = ((bf16[32,64,256]{2,1,0:T(8,128)(2,1)}), bf16[32,64,256]{2,1,0:T(8,128)(2,1)S(1)}, u32[]{:S(2)}, u32[]{:S(2)}) async-start(bf16[32,64,256]{2,1,0:T(8,128)(2,1)} %bitcast.28), calls=%async_computation | async-start | bytes 2097152 | tf_op jit(solution)/shard_map/all_to_all | solution.py:765
  15.4 0.0 copy-start
  15.4 0.0 copy-start.1
  15.4 0.0 copy-start.2
  15.5 0.0 copy-start.3
  15.5 0.0 copy-start.4
  15.5 0.0 copy-start.5
  15.5 0.0 copy-start.6
  15.5 13.2 %shard_map.165 = (f32[1536,256]{1,0:T(8,128)}, bf16[2048,256]{1,0:T(8,128)(2,1)}, bf16[64,16,256]{2,1,0:T(8,128)(2,1)}, bf16[64,16,256]{2,1,0:T(8,128)(2,1)}, bf...) custom-call(s32[8,128]{1,0:T(8,128)} %get-tuple-element.35.refs_0_, ...), custom_call_target="tpu_custom_call" | custom-call | tf_op jit(solution)/shard_map/pallas_call | solution.py:752
  28.7 3.6 %all-to-all-done = bf16[32,64,256]{2,1,0:T(8,128)(2,1)S(1)} async-done(((bf16[32,64,256]{2,1,0:T(8,128)(2,1)}), bf16[32,64,256]{2,1,0:T(8,128)(2,1)S(1)}, u32[]{:S(2)}, u32[]{:S(2)}) %all-to-all-start) | async-done | bytes 1048608 | tf_op jit(solution)/shard_map/all_to_all | solution.py:765
  32.3 0.0 copy-done
  32.4 5.7 %shard_map.166 = (bf16[512,256]{1,0:T(8,128)(2,1)}, bf16[512,256]{1,0:T(8,128)(2,1)}, bf16[512,256]{1,0:T(8,128)(2,1)}, bf16[512,256]{1,0:T(8,128)(2,1)}, bf16[6...) custom-call(s32[8,128]{1,0:T(8,128)S(1)} %copy-done.3, ...), custom_call_target="tpu_custom_call" | custom-call | tf_op jit(solution)/shard_map/pallas_call | solution.py:752
  38.1 12.3 %shard_map.167 = (bf16[32,40,128]{2,1,0:T(8,128)(2,1)}, f32[2048,256]{1,0:T(8,128)}, bf16[2048,256]{1,0:T(8,128)(2,1)}) custom-call(s32[8,128]{1,0:T(8,128)} %get-tuple-element.35.refs_0_, bf16[2048,256]{1,0:T(8,128)(2,1)} %bitcast.24, bf16[2048,256]{1,0:T(8,128)(2,1)} %bitcast.20, bf16[2048,256]{1,0:T(8,128)(2,1)} %get-tuple-element.43.refs_3_, ...), custom_call_target="tpu_custom_call" | custom-call | tf_op jit(solution)/shard_map/pallas_call | solution.py:752
  50.4 13.6 %all_to_all.25.refs_0_ = bf16[32,40,128]{2,1,0:T(8,128)(2,1)S(1)} all-to-all(bf16[32,40,128]{2,1,0:T(8,128)(2,1)} %get-tuple-element.61), channel_id=1, replica_groups=mesh['tile_0'=4,'tile_1'=4,'tile_2'=2,'batch'=4] {'tile_0','tile_1','til..., dimensions={0} | all-to-all | bytes 655360 | tf_op jit(solution)/shard_map/all_to_all | solution.py:765
  64.0 0.1 shard_map.170
  64.1 8.1 %all_to_all.26.refs_0_ = bf16[4,40,128]{2,1,0:T(8,128)(2,1)S(1)} all-to-all(bf16[4,40,128]{2,1,0:T(8,128)(2,1)S(1)} %shard_map.170), channel_id=1, replica_groups=mesh['tile_0'=4,'tile_1'=4,'tile_2'=2,'batch'=4] {'batch'}, dimensions={0} | all-to-all | bytes 81920 | tf_op jit(solution)/shard_map/all_to_all | solution.py:859
  72.2 14.5 %all_to_all.27.refs_0_ = bf16[32,40,128]{2,1,0:T(8,128)(2,1)S(1)} all-to-all(bf16[32,40,128]{2,1,0:T(8,128)(2,1)S(1)} %shard_map.171), channel_id=1, replica_groups=mesh['tile_0'=4,'tile_1'=4,'tile_2'=2,'batch'=4] {'tile_0','tile_1','til..., dimensions={0} | all-to-all | bytes 655360 | tf_op jit(solution)/shard_map/all_to_all | solution.py:765
  86.7 3.7 %all-to-all-start.1 = ((bf16[32,64,256]{2,1,0:T(8,128)(2,1)}), bf16[32,64,256]{2,1,0:T(8,128)(2,1)S(1)}, u32[]{:S(2)}, u32[]{:S(2)}) async-start(bf16[32,64,256]{2,1,0:T(8,128)(2,1)} %bitcast.7), calls=%async_computation.1 | async-start | bytes 2097152 | tf_op jit(solution)/shard_map/all_to_all | solution.py:765
  90.4 1.4 %shard_map.172 = (f32[2,256,256]{2,1,0:T(8,128)}, f32[9,2,256]{2,1,0:T(2,128)}, f32[2,256]{1,0:T(2,128)}) custom-call(bf16[32,40,128]{2,1,0:T(8,128)(2,1)S(1)} %all_to_all.27.refs_0_), custom_call_target="tpu_custom_call" | custom-call | tf_op jit(solution)/shard_map/pallas_call | solution.py:752
  91.9 15.5 %all-to-all-done.1 = bf16[32,64,256]{2,1,0:T(8,128)(2,1)S(1)} async-done(((bf16[32,64,256]{2,1,0:T(8,128)(2,1)}), bf16[32,64,256]{2,1,0:T(8,128)(2,1)S(1)}, u32[]{:S(2)}, u32[]{:S(2)}) %all-to-all-start.1) | async-done | bytes 1048608 | tf_op jit(solution)/shard_map/all_to_all | solution.py:765
  107.4 1.0 copy-done.7
  108.4 7.3 %shard_map.168 = (bf16[2048,256]{1,0:T(8,128)(2,1)}, bf16[8,128,256]{2,1,0:T(8,128)(2,1)}) custom-call(s32[8,128]{1,0:T(8,128)} %get-tuple-element.35.refs_0_, bf16[64,32,256]{2,1,0:T(8,128)(2,1)} %bitcast.26, bf16[64,16,256]{2,1,0:T(8,128)(2,1)} %get-tuple-element.41.refs_8_.refs_2_, bf16[128,16,256]{2,1,0:T(8,128)(2,1)} %get-tuple-element.42.refs_9_.refs_3_, ...), custom_call_target="tpu_custom_call" | custom-call | tf_op jit(solution)/shard_map/pallas_call | solution.py:752
  115.7 6.1 %shard_map.169 = bf16[2048,256]{1,0:T(8,128)(2,1)} custom-call(bf16[2048,256]{1,0:T(8,128)(2,1)} %get-tuple-element.59.refs_0_, bf16[8,128,256]{2,1,0:T(8,128)(2,1)} %get-tuple-element.60.refs_1_, bf16[2048,256]{1,0:T(8,128)(2,1)} %bitcast.21, f32[9,2,256]{2,1,0:T(2,128)} %bitcast.16, bf16[512,256]{1,0:T(8,128)(2,1)} %constant.14.clone.refs_7_.refs_20_.refs_4_, ...), custom_call_target="tpu_custom_call" | custom-call | tf_op jit(solution)/shard_map/pallas_call | solution.py:752
  (8 shorter events, 0.1 us)
Async XLA Ops:
  5.8 26.5 %all-to-all-start = ((bf16[32,64,256]{2,1,0:T(8,128)(2,1)}), bf16[32,64,256]{2,1,0:T(8,128)(2,1)S(1)}, u32[]{:S(2)}, u32[]{:S(2)}) async-start(bf16[32,64,256]{2,1,0:T(8,128)(2,1)} %bitcast.28), calls=%async_computation | async-start | bytes 2097152 | tf_op jit(solution)/shard_map/all_to_all | solution.py:765
  15.4 16.9 %copy-start = (bf16[2,256,256]{2,1,0:T(8,128)(2,1)S(1)}, bf16[2,256,256]{2,1,0:T(8,128)(2,1)}, u32[]{:S(2)}) copy-start(bf16[2,256,256]{2,1,0:T(8,128)(2,1)} %refs_6_.5) | copy-start | bytes 786436
  15.4 16.9 %copy-start.1 = (bf16[64,16,256]{2,1,0:T(8,128)(2,1)S(1)}, bf16[64,16,256]{2,1,0:T(8,128)(2,1)}, u32[]{:S(2)}) copy-start(bf16[64,16,256]{2,1,0:T(8,128)(2,1)} %get-tuple-element.37.refs_2_) | copy-start | bytes 1572868
  15.4 16.9 %copy-start.2 = (f32[2,9,256]{2,0,1:T(2,128)S(1)}, f32[2,9,256]{2,0,1:T(2,128)}, u32[]{:S(2)}) copy-start(f32[2,9,256]{2,0,1:T(2,128)} %param.18) | copy-start | bytes 55300
  15.5 16.9 %copy-start.3 = (s32[8,128]{1,0:T(8,128)S(1)}, s32[8,128]{1,0:T(8,128)}, u32[]{:S(2)}) copy-start(s32[8,128]{1,0:T(8,128)} %get-tuple-element.35.refs_0_) | copy-start | bytes 12292
  15.5 16.9 %copy-start.4 = (f32[2,256]{1,0:T(2,128)S(1)}, f32[2,256]{1,0:T(2,128)}, u32[]{:S(2)}) copy-start(f32[2,256]{1,0:T(2,128)} %refs_8_.2) | copy-start | bytes 6148
  15.5 16.9 %copy-start.5 = (bf16[64,64]{1,0:T(8,128)(2,1)S(1)}, bf16[64,64]{1,0:T(8,128)(2,1)}, u32[]{:S(2)}) copy-start(bf16[64,64]{1,0:T(8,128)(2,1)} %constant.15.clone.refs_7_) | copy-start | bytes 24580
  15.5 16.9 %copy-start.6 = (bf16[64,128]{1,0:T(8,128)(2,1)S(1)}, bf16[64,128]{1,0:T(8,128)(2,1)}, u32[]{:S(2)}) copy-start(bf16[64,128]{1,0:T(8,128)(2,1)} %constant.16.clone.refs_8_) | copy-start | bytes 49156
  86.7 20.7 %all-to-all-start.1 = ((bf16[32,64,256]{2,1,0:T(8,128)(2,1)}), bf16[32,64,256]{2,1,0:T(8,128)(2,1)S(1)}, u32[]{:S(2)}, u32[]{:S(2)}) async-start(bf16[32,64,256]{2,1,0:T(8,128)(2,1)} %bitcast.7), calls=%async_computation.1 | async-start | bytes 2097152 | tf_op jit(solution)/shard_map/all_to_all | solution.py:765
  107.4 1.0 copy-start.7

commit v6 on v5

--- a/solution.py
+++ b/solution.py
@@ -155,17 +155,23 @@
     ref[t, pl.ds(64 + first, value.shape[0]), :] = (value - high.astype(F32)).astype(BF16)
 
 
-def forward_lines(split_ref, buf_ref, tab_ref, w, panels_ref=None):
+def forward_lines(split_ref, rims_ref, in_ref, tab_ref, w, panels_ref=None):
+    def panel_of(k):
+        place = tab_ref[0, k]
+        own = rims_ref[jnp.minimum(place, 63)]
+        sent = in_ref[jnp.maximum(place - 64, 0), 0:S]
+        return jnp.where(place < 64, own, sent)
+
     def one(t, carry):
         corner = {}
         for d in range(4, 8):
-            panel = buf_ref[tab_ref[0, t * 8 + d]]
+            panel = panel_of(t * 8 + d)
             if panels_ref is not None:
                 panels_ref[t * 8 + d] = panel
             row = panel[:8, :].astype(F32)[:1, :]
             corner[d] = w[CORNER_TAP[d]] * row
         for d in range(4):
-            panel = buf_ref[tab_ref[0, t * 8 + d]]
+            panel = panel_of(t * 8 + d)
             if panels_ref is not None:
                 panels_ref[t * 8 + d] = panel
             x = panel.astype(F32)
@@ -248,10 +254,13 @@
             lines_ref[16 * t + 2 * d + f] = value.astype(BF16)
 
 
-def banks(rims_ref, lines_ref, t, rim_tile, line_tile, sel_ref):
-    rims = dot(sel_ref[...], rim_tile).astype(BF16)
+def bank_rims(rims_ref, t, tile, sel_ref):
+    rims = dot(sel_ref[...], tile).astype(BF16)
     rims_ref[pl.ds(t * 8, 8)] = rims.reshape(8, S, 256)
-    lines = dot(sel_ref[...], line_tile)
+
+
+def bank_lines(lines_ref, t, tile, sel_ref):
+    lines = dot(sel_ref[...], tile)
     lines_ref[pl.ds(t * 16, 8)] = lines.astype(BF16).reshape(8, S, 256)
     groups = [lines[S * k : S * k + S] for k in range(8)]
     put_corners(lines_ref, t, [groups[2 * d : 2 * d + 2] for d in range(4)])
@@ -277,8 +286,8 @@
 
 
 def first_kernel(
-    arrive, leave, slot_ref, code_ref, states_ref, cot_ref, sel_ref, tab_ref, out_ref, rims_ref, lines_ref,
-    comb_ref, smem, sem,
+    arrive, leave, slot_ref, code_ref, states_ref, cot_ref, sel_ref, tab_ref, out_ref, rims_ref,
+    lines_ref, comb_ref, smem, sem,
 ):
     me = own_position()
     entries = slot_ref.shape[1]
@@ -346,15 +355,12 @@
     copy = pltpu.make_async_copy(tab_ref, smem, sem)
     copy.start()
     arrive(2)
+    for t in range(T):
+        bank_rims(rims_ref, t, tile_of(states_ref, t), sel_ref)
+    leave(2, 0, 64)
     arrive(3)
-
-    def lines_of(t, carry):
-        banks(rims_ref, lines_ref, t, tile_of(states_ref, t), tile_of(cot_ref, t), sel_ref)
-        return carry
-
-    lax.fori_loop(0, T, lines_of, 0, unroll=4)
-    leave(2, 0, 64)
-    leave(3, 0, 128)
+    for t in range(T):
+        bank_lines(lines_ref, t, tile_of(cot_ref, t), sel_ref)
     copy.wait()
     gather_out(leave, 1, out_ref, rims_ref, lines_ref, smem)
 
@@ -386,9 +392,9 @@
 
 
 def inner_kernel(
-    arrive, leave, tab_ref, states_ref, cot_ref, bank_ref, mixers_ref, stencils_ref, shifts_ref, shift_ref,
+    arrive, leave, tab_ref, states_ref, cot_ref, mixers_ref, stencils_ref, shifts_ref, shift_ref, sel_ref,
     back_ref, g_ref, c_ref, gl_ref, active_ref, first_ref, gh_ref, gc_ref,
-    taps_ref, tile1_ref, tile2_ref,
+    bank_ref, taps_ref, tile1_ref, tile2_ref,
 ):
     w0 = tap_rows(stencils_ref, 0)
     w1 = tap_rows(stencils_ref, 1)
@@ -398,6 +404,7 @@
 
     def one(t, carry):
         x = tile_of(states_ref, t)
+        bank_lines(bank_ref, t, tile_of(cot_ref, t), sel_ref)
         moved = dot(shift_ref[...], x)
         conv = conv_inner(moved[:CELLS], x.astype(F32), moved[CELLS:], w0)
         put_halves(tile1_ref, conv)
@@ -423,7 +430,6 @@
         return carry
 
     lax.fori_loop(0, T, one, 0)
-    arrive(3)
     fill_tap_sets(taps_ref, stencils_ref, 1)
     live_lines(c_ref, 0, lambda i: bank_ref[tab_ref[5, i]], tab_ref, 0)
     leave(2, 0, 64)
@@ -438,20 +444,18 @@
     arrive, leave,
     tab_ref, in_ref, rims_in_ref, back_ref, mixers_ref, stencils_ref,
     shifts_ref, turn_ref, cross_ref,
-    active_ref, first_ref, gh_ref, gc_ref, rims_ref, lines_ref, out_ref, c_ref, g_ref, panels_ref,
-    buf_ref, split_ref, split2_ref, taps_ref,
+    active_ref, first_ref, gh_ref, gc_ref, out_ref, c_ref, g_ref, panels_ref,
+    rims_ref, lines_ref, split_ref, split2_ref, taps_ref,
 ):
     w0 = tap_rows(stencils_ref, 0)
     fill_tap_sets(taps_ref, stencils_ref, 1)
-    buf_ref[64:128] = in_ref[:, 0:S, :]
     live_lines(c_ref, 0, lambda i: in_ref[i, S : 2 * S], tab_ref, 64)
+    leave(5, 0, 64)
+    line_grads(g_ref, c_ref, mixers_ref)
+    leave(6, 0, 64)
+    arrive(2)
+    forward_lines(split_ref, rims_in_ref, in_ref, tab_ref, w0, panels_ref)
     leave(7, 0, 64)
-    line_grads(g_ref, c_ref, mixers_ref)
-    leave(8, 0, 64)
-    arrive(2)
-    buf_ref[0:64] = rims_in_ref[...]
-    forward_lines(split_ref, buf_ref, tab_ref, w0, panels_ref)
-    leave(9, 0, 64)
     arrive(3)
     rim_gradients(back_ref, 2 * CELLS, g_ref, tab_ref, taps_ref, 64, 64)
     split_rims(split2_ref, back_ref, 2 * CELLS)
@@ -476,19 +480,17 @@
             t = 4 * u + q
             rows = slice(64 * q, 64 * q + 64)
             edge_banks(rims_ref, lines_ref, t, active[rows], gc[rows], turn_ref)
-    for k in range(4):
-        leave(k, 0, 2 * CELLS)
-    leave(4, 0, 64)
-    leave(5, 0, 128)
-    gather_out(leave, 6, out_ref, rims_ref, lines_ref, tab_ref)
+        for k in range(4):
+            leave(k, u * CELLS, CELLS)
+    gather_out(leave, 4, out_ref, rims_ref, lines_ref, tab_ref)
 
 
 def weight_kernel(
     arrive, leave,
-    tab_ref, states_ref, cot_ref, active_ref, first_ref, gh_ref, gc_ref, g2_ref, rims_ref, lines_ref,
-    panels_ref, c_own_ref, g_own_ref, c_in_ref, g_in_ref,
-    active_edge_ref, first_edge_ref, gh_edge_ref, gc_edge_ref, stencils_ref, shift_ref, place_ref,
-    pack_ref, conv_ref, gc_out_ref,
+    tab_ref, states_ref, cot_ref, active_ref, first_ref, gh_ref, gc_ref, g2_ref, panels_ref,
+    c_own_ref, g_own_ref, c_in_ref, g_in_ref,
+    active_edge_ref, first_edge_ref, gh_edge_ref, gc_edge_ref, stencils_ref, shift_ref, place_ref, turn_ref,
+    pack_ref, conv_ref, gc_out_ref, rims_ref, lines_ref,
     second_ref, h_ref, taps_ref, acc1_ref, acc2_ref, accl_ref, sums_ref,
 ):
     w1 = tap_rows(stencils_ref, 1)
@@ -524,13 +526,19 @@
 
         return one
 
-    arrive(8)
+    arrive(13)
+    arrive(16)
+    for t in range(T):
+        rows = slice(64 * t, 64 * t + 64)
+        edge_banks(rims_ref, lines_ref, t, active_edge_ref[rows], gc_edge_ref[rows], turn_ref)
+    leave(3, 0, 64)
+    leave(4, 0, 128)
+    arrive(10)
+    lax.fori_loop(0, 64, second_halo(g_own_ref), 0, unroll=8)
     arrive(12)
-    lax.fori_loop(0, 64, second_halo(g_own_ref), 0, unroll=8)
-    arrive(14)
     lax.fori_loop(64, 128, second_halo(g_in_ref), 0, unroll=8)
 
-    for k in (9, 10):
+    for k in (8,):
         arrive(k)
 
     def first_halo(t, carry):
@@ -547,7 +555,7 @@
 
     lax.fori_loop(0, T, first_halo, 0, unroll=2)
 
-    for k in (6, 18, 1, 3, 15, 7, 5, 17, 2):
+    for k in (6, 1, 3, 7, 5, 15, 2):
         arrive(k)
 
     def whole(inner_ref, edge_ref, t):
@@ -575,7 +583,7 @@
         return carry
 
     lax.fori_loop(0, T, one, 0)
-    for k in (4, 16, 11, 13):
+    for k in (4, 14, 9, 11):
         arrive(k)
     for d in range(8):
         for f in range(2):
@@ -620,14 +628,12 @@
     tab_ref, in_ref, rims_in_ref, bank_ref, conv_ref, states_ref, mixers_ref, stencils_ref, shifts_ref,
     spread_ref,
     outcome_ref, halo_ref,
-    buf_ref, split_ref, rim_ref, taps_ref, lines_ref,
+    split_ref, rim_ref, taps_ref, lines_ref,
 ):
     w1 = tap_rows(stencils_ref, 1)
     arrive(2)
-    buf_ref[0:64] = rims_in_ref[...]
     arrive(1)
-    buf_ref[64:128] = in_ref[:, 0:S, :]
-    forward_lines(split_ref, buf_ref, tab_ref, w1)
+    forward_lines(split_ref, rims_in_ref, in_ref, tab_ref, w1)
     arrive(4)
     arrive(5)
 
@@ -784,13 +790,15 @@
     split_scratch = pltpu.VMEM((T, 128, 256), BF16)
     rim_scratch = pltpu.VMEM((2 * CELLS, 256), F32)
     taps_scratch = pltpu.VMEM((16, 3, 256), F32)
-    tab, out1, rims1, lines1 = call(
+    rims_scratch = pltpu.VMEM((64, S, 256), BF16)
+    tab, out1, rims1 = call(
         first_kernel,
         (beside_slot.astype(I32).T, beside_code.astype(I32).T, x, cot, sel),
         "vvhhv",
-        [shape_of(8, 128, dtype=I32), sent16, rims16, lines16],
-        "vhhh",
+        [shape_of(8, 128, dtype=I32), sent16, rims16],
+        "vhh",
         [
+            lines_scratch,
             pltpu.VMEM((groups, 128), I32),
             pltpu.SMEM((8, 128), I32),
             pltpu.SemaphoreType.DMA,
@@ -802,8 +810,8 @@
     tile_scratch = pltpu.VMEM((2, CELLS, 128), F32)
     back2, g2, c_own, g_own, active, first, gh, gc = call(
         inner_kernel,
-        (tab, x, cot, lines1, mixers, taps, shifts, shift),
-        "shhhvvvv",
+        (tab, x, cot, mixers, taps, shifts, shift, sel),
+        "shhvvvvv",
         [
             shape_of(6 * CELLS, 256, dtype=F32),
             field,
@@ -815,25 +823,25 @@
             field,
         ],
         "hhhhhhhh",
-        [taps_scratch, tile_scratch, tile_scratch],
-    )
-    active_e, first_e, gh_e, gc_e, rims2, lines2, out2, c_in, g_in, panels = call(
+        [lines_scratch, taps_scratch, tile_scratch, tile_scratch],
+    )
+    active_e, first_e, gh_e, gc_e, out2, c_in, g_in, panels = call(
         middle_kernel,
         (tab, in1, rims1, back2, mixers, taps, shifts, turn, cross),
         "svhhvvvvv",
-        [edge, edge, edge, edge, rims16, lines16, sent16, rims16, rims16, rims16],
-        "hhhhhhhhhh",
-        [lines_scratch, split_scratch, split_scratch, taps_scratch],
+        [edge, edge, edge, edge, sent16, rims16, rims16, rims16],
+        "hhhhhhhh",
+        [rims_scratch, lines_scratch, split_scratch, split_scratch, taps_scratch],
         limit=51.0,
     )
     in2 = exchange(out2.reshape(groups, 4 * S, 256)).reshape(64, 2 * S, 256)
-    pack, conv2, gc_all = call(
+    pack, conv2, gc_all, rims2, lines2 = call(
         weight_kernel,
-        (tab, x, cot, active, first, gh, gc, g2, rims2, lines2, panels, c_own, g_own, c_in, g_in,
-         active_e, first_e, gh_e, gc_e, taps, shift, place),
-        "shhhhhhhhhhhhhhhhhhvvv",
-        [shape_of(groups, 40, 128), wide, field],
-        "hhh",
+        (tab, x, cot, active, first, gh, gc, g2, panels, c_own, g_own, c_in, g_in,
+         active_e, first_e, gh_e, gc_e, taps, shift, place, turn),
+        "shhhhhhhhhhhhhhhhvvvv",
+        [shape_of(groups, 40, 128), wide, field, rims16, lines16],
+        "hhhhh",
         [
             pltpu.VMEM((T * CELLS, 256), BF16),
             lines_scratch,
@@ -843,7 +851,7 @@
             pltpu.VMEM((16, 3, 8, 256), F32),
             pltpu.VMEM((2, 8, 256), F32),
         ],
-        order=(8, 12, 14, 9, 10, 6, 18, 1, 3, 15, 7, 5, 17, 2, 4, 16, 11, 13),
+        order=(13, 16, 10, 12, 8, 6, 1, 3, 7, 5, 15, 2, 4, 14, 9, 11),
     )
     parts = exchange(pack)
     outcome, halo = call(
@@ -852,7 +860,7 @@
         "shhhhhvvvv",
         [field, shape_of(T, 128, 256)],
         "hh",
-        [lines_scratch, split_scratch, rim_scratch, taps_scratch, lines_scratch],
+        [split_scratch, rim_scratch, taps_scratch, lines_scratch],
         order=(2, 1, 4, 5, 3),
     )
     (part,) = call(sum_kernel, (parts,), "v", [shape_of(batch, 40, 128)], "v", limit=4)

time: 123 us -> 122 us (level)
  no operation moved by 1% of the time
where the time goes in v6:
time: 122 us; the launch traced here: 121 us
  Pallas kernels  50.1 us (41%)
  blocking collectives  36.2 us (30%)
  waiting for transfers between devices  19.3 us (16%)
  starting transfers between devices  13.5 us (11%)
    pallas_call x9, Pallas kernels, call(): pl.pallas_call(kernel, out_shape=[pltpu.HBM(o.shape, o.dtype) if m == 'h'...  50.1 us
    all_to_all x2, blocking collectives, exchange(): return lax.all_to_all(array, TILE, split_axis=0, concat_axis=0, tiled=True)  28 us
    all_to_all x2, waiting for transfers between devices, exchange(): return lax.all_to_all(array, TILE, split_axis=0, concat_axis=0, tiled=True)  19.3 us
    all_to_all x2, starting transfers between devices, exchange(): return lax.all_to_all(array, TILE, split_axis=0, concat_axis=0, tiled=True)  13.5 us
    all_to_all x1, blocking collectives, whole_block(): lax.all_to_all(part, 'batch', split_axis=0, concat_axis=0, tiled=True)  8.15 us
  transfers between devices with their start and end apart: 2, of which 2 were waited for; matrix products, arithmetic and copies ran while one was open for 0% of the time, Pallas kernels for 12%

profile of v6, /device:TPU:1, one launch (start us, length us, event | category | flops | bytes accessed | tf_op | source)
XLA Modules:
  0.0 120.9 jit_solution(10393344739325940328)
XLA Ops:
  0.6 4.4 %shard_map.164 = (s32[8,128]{1,0:T(8,128)}, bf16[64,32,256]{2,1,0:T(8,128)(2,1)}, bf16[64,16,256]{2,1,0:T(8,128)(2,1)}) custom-call(s32[8,256]{1,0:T(8,128)} %bitcast.29, s32[8,256]{1,0:T(8,128)} %bitcast.30, bf16[2048,256]{1,0:T(8,128)(2,1)} %bitcast.22, bf16[2048,256]{1,0:T(8,128)(2,1)} %bitcast.18, bf16[128,256]{1,0:T(8,128)(2,1)} %constant.12.clone.refs_4_.refs_7_), custom_call_target="tpu_custom_call" | custom-call | tf_op jit(solution)/shard_map/pallas_call | solution.py:758
  5.0 0.0 copy-start
  5.0 0.0 copy-start.1
  5.1 0.0 copy-start.2
  5.1 0.0 copy-start.3
  5.1 0.0 copy-start.4
  5.1 0.0 copy-start.5
  5.1 0.0 copy-start.6
  5.1 9.7 %all-to-all-start = ((bf16[32,64,256]{2,1,0:T(8,128)(2,1)}), bf16[32,64,256]{2,1,0:T(8,128)(2,1)S(1)}, u32[]{:S(2)}, u32[]{:S(2)}) async-start(bf16[32,64,256]{2,1,0:T(8,128)(2,1)} %bitcast.28), calls=%async_computation | async-start | bytes 2097152 | tf_op jit(solution)/shard_map/all_to_all | solution.py:771
  14.9 13.1 %shard_map.165 = (f32[1536,256]{1,0:T(8,128)}, bf16[2048,256]{1,0:T(8,128)(2,1)}, bf16[64,16,256]{2,1,0:T(8,128)(2,1)}, bf16[64,16,256]{2,1,0:T(8,128)(2,1)}, bf...) custom-call(s32[8,128]{1,0:T(8,128)} %get-tuple-element.34.refs_0_, ...), custom_call_target="tpu_custom_call" | custom-call | tf_op jit(solution)/shard_map/pallas_call | solution.py:758
  28.0 3.8 %all-to-all-done = bf16[32,64,256]{2,1,0:T(8,128)(2,1)S(1)} async-done(((bf16[32,64,256]{2,1,0:T(8,128)(2,1)}), bf16[32,64,256]{2,1,0:T(8,128)(2,1)S(1)}, u32[]{:S(2)}, u32[]{:S(2)}) %all-to-all-start) | async-done | bytes 1048608 | tf_op jit(solution)/shard_map/all_to_all | solution.py:771
  31.8 0.0 copy-done
  31.8 5.2 %shard_map.166 = (bf16[512,256]{1,0:T(8,128)(2,1)}, bf16[512,256]{1,0:T(8,128)(2,1)}, bf16[512,256]{1,0:T(8,128)(2,1)}, bf16[512,256]{1,0:T(8,128)(2,1)}, bf16[6...) custom-call(s32[8,128]{1,0:T(8,128)S(1)} %copy-done.4, ...), custom_call_target="tpu_custom_call" | custom-call | tf_op jit(solution)/shard_map/pallas_call | solution.py:758
  37.1 12.4 %shard_map.167 = (bf16[32,40,128]{2,1,0:T(8,128)(2,1)}, f32[2048,256]{1,0:T(8,128)}, bf16[2048,256]{1,0:T(8,128)(2,1)}, bf16[64,16,256]{2,1,0:T(8,128)(2,1)}, bf16[128,16,256]{2,1,0:T(8,128)(2,1)}) custom-call(s32[8,128]{1,0:T(8,128)} %get-tuple-element.34.refs_0_, bf16[2048,256]{1,0:T(8,128)(2,1)} %bitcast.24, bf16[2048,256]{1,0:T(8,128)(2,1)} %bitcast.20, ...), custom_call_target="tpu_custom_call" | custom-call | tf_op jit(solution)/shard_map/pallas_call | solution.py:758
  49.5 13.6 %all_to_all.25.refs_0_ = bf16[32,40,128]{2,1,0:T(8,128)(2,1)S(1)} all-to-all(bf16[32,40,128]{2,1,0:T(8,128)(2,1)} %get-tuple-element.59), channel_id=1, replica_groups=mesh['tile_0'=4,'tile_1'=4,'tile_2'=2,'batch'=4] {'tile_0','tile_1','til..., dimensions={0} | all-to-all | bytes 655360 | tf_op jit(solution)/shard_map/all_to_all | solution.py:771
  63.0 0.1 shard_map.170
  63.1 8.2 %all_to_all.26.refs_0_ = bf16[4,40,128]{2,1,0:T(8,128)(2,1)S(1)} all-to-all(bf16[4,40,128]{2,1,0:T(8,128)(2,1)S(1)} %shard_map.170), channel_id=1, replica_groups=mesh['tile_0'=4,'tile_1'=4,'tile_2'=2,'batch'=4] {'batch'}, dimensions={0} | all-to-all | bytes 81920 | tf_op jit(solution)/shard_map/all_to_all | solution.py:867
  71.3 14.5 %all_to_all.27.refs_0_ = bf16[32,40,128]{2,1,0:T(8,128)(2,1)S(1)} all-to-all(bf16[32,40,128]{2,1,0:T(8,128)(2,1)S(1)} %shard_map.171), channel_id=1, replica_groups=mesh['tile_0'=4,'tile_1'=4,'tile_2'=2,'batch'=4] {'tile_0','tile_1','til..., dimensions={0} | all-to-all | bytes 655360 | tf_op jit(solution)/shard_map/all_to_all | solution.py:771
  85.8 3.7 %all-to-all-start.1 = ((bf16[32,64,256]{2,1,0:T(8,128)(2,1)}), bf16[32,64,256]{2,1,0:T(8,128)(2,1)S(1)}, u32[]{:S(2)}, u32[]{:S(2)}) async-start(bf16[32,64,256]{2,1,0:T(8,128)(2,1)} %bitcast.7), calls=%async_computation.1 | async-start | bytes 2097152 | tf_op jit(solution)/shard_map/all_to_all | solution.py:771
  89.5 1.4 %shard_map.172 = (f32[2,256,256]{2,1,0:T(8,128)}, f32[9,2,256]{2,1,0:T(2,128)}, f32[2,256]{1,0:T(2,128)}) custom-call(bf16[32,40,128]{2,1,0:T(8,128)(2,1)S(1)} %all_to_all.27.refs_0_), custom_call_target="tpu_custom_call" | custom-call | tf_op jit(solution)/shard_map/pallas_call | solution.py:758
  91.0 15.5 %all-to-all-done.1 = bf16[32,64,256]{2,1,0:T(8,128)(2,1)S(1)} async-done(((bf16[32,64,256]{2,1,0:T(8,128)(2,1)}), bf16[32,64,256]{2,1,0:T(8,128)(2,1)S(1)}, u32[]{:S(2)}, u32[]{:S(2)}) %all-to-all-start.1) | async-done | bytes 1048608 | tf_op jit(solution)/shard_map/all_to_all | solution.py:771
  106.5 1.0 copy-done.7
  107.5 7.3 %shard_map.168 = (bf16[2048,256]{1,0:T(8,128)(2,1)}, bf16[8,128,256]{2,1,0:T(8,128)(2,1)}) custom-call(s32[8,128]{1,0:T(8,128)} %get-tuple-element.34.refs_0_, bf16[64,32,256]{2,1,0:T(8,128)(2,1)} %bitcast.26, bf16[64,16,256]{2,1,0:T(8,128)(2,1)} %get-tuple-element.53.refs_2_, bf16[128,16,256]{2,1,0:T(8,128)(2,1)} %get-tuple-element.54.refs_3_, ...), custom_call_target="tpu_custom_call" | custom-call | tf_op jit(solution)/shard_map/pallas_call | solution.py:758
  114.8 6.1 %shard_map.169 = bf16[2048,256]{1,0:T(8,128)(2,1)} custom-call(bf16[2048,256]{1,0:T(8,128)(2,1)} %get-tuple-element.57.refs_0_, bf16[8,128,256]{2,1,0:T(8,128)(2,1)} %get-tuple-element.58.refs_1_, bf16[2048,256]{1,0:T(8,128)(2,1)} %bitcast.21, f32[9,2,256]{2,1,0:T(2,128)} %bitcast.16, bf16[512,256]{1,0:T(8,128)(2,1)} %constant.14.clone.refs_6_.refs_18_.refs_4_, ...), custom_call_target="tpu_custom_call" | custom-call | tf_op jit(solution)/shard_map/pallas_call | solution.py:758
  (8 shorter events, 0.1 us)
Async XLA Ops:
  5.0 26.7 %copy-start = (bf16[2,256,256]{2,1,0:T(8,128)(2,1)S(1)}, bf16[2,256,256]{2,1,0:T(8,128)(2,1)}, u32[]{:S(2)}) copy-start(bf16[2,256,256]{2,1,0:T(8,128)(2,1)} %refs_6_.4) | copy-start | bytes 786436
  5.0 26.7 %copy-start.1 = (bf16[64,16,256]{2,1,0:T(8,128)(2,1)S(1)}, bf16[64,16,256]{2,1,0:T(8,128)(2,1)}, u32[]{:S(2)}) copy-start(bf16[64,16,256]{2,1,0:T(8,128)(2,1)} %get-tuple-element.36.refs_2_) | copy-start | bytes 1572868
  5.1 26.7 %copy-start.2 = (f32[2,9,256]{2,0,1:T(2,128)S(1)}, f32[2,9,256]{2,0,1:T(2,128)}, u32[]{:S(2)}) copy-start(f32[2,9,256]{2,0,1:T(2,128)} %param.18) | copy-start | bytes 55300
  5.1 26.7 %copy-start.3 = (bf16[64,64]{1,0:T(8,128)(2,1)S(1)}, bf16[64,64]{1,0:T(8,128)(2,1)}, u32[]{:S(2)}) copy-start(bf16[64,64]{1,0:T(8,128)(2,1)} %constant.15.clone.refs_7_.refs_20_) | copy-start | bytes 24580
  5.1 26.7 %copy-start.4 = (s32[8,128]{1,0:T(8,128)S(1)}, s32[8,128]{1,0:T(8,128)}, u32[]{:S(2)}) copy-start(s32[8,128]{1,0:T(8,128)} %get-tuple-element.34.refs_0_) | copy-start | bytes 12292
  5.1 26.7 %copy-start.5 = (f32[2,256]{1,0:T(2,128)S(1)}, f32[2,256]{1,0:T(2,128)}, u32[]{:S(2)}) copy-start(f32[2,256]{1,0:T(2,128)} %refs_8_.2) | copy-start | bytes 6148
  5.1 26.7 %copy-start.6 = (bf16[64,128]{1,0:T(8,128)(2,1)S(1)}, bf16[64,128]{1,0:T(8,128)(2,1)}, u32[]{:S(2)}) copy-start(bf16[64,128]{1,0:T(8,128)(2,1)} %constant.16.clone.refs_8_) | copy-start | bytes 49156
  5.1 26.7 %all-to-all-start = ((bf16[32,64,256]{2,1,0:T(8,128)(2,1)}), bf16[32,64,256]{2,1,0:T(8,128)(2,1)S(1)}, u32[]{:S(2)}, u32[]{:S(2)}) async-start(bf16[32,64,256]{2,1,0:T(8,128)(2,1)} %bitcast.28), calls=%async_computation | async-start | bytes 2097152 | tf_op jit(solution)/shard_map/all_to_all | solution.py:771
  85.8 20.7 %all-to-all-start.1 = ((bf16[32,64,256]{2,1,0:T(8,128)(2,1)}), bf16[32,64,256]{2,1,0:T(8,128)(2,1)S(1)}, u32[]{:S(2)}, u32[]{:S(2)}) async-start(bf16[32,64,256]{2,1,0:T(8,128)(2,1)} %bitcast.7), calls=%async_computation.1 | async-start | bytes 2097152 | tf_op jit(solution)/shard_map/all_to_all | solution.py:771
  106.5 1.0 copy-start.7

commit v7 on v6

--- a/solution.py
+++ b/solution.py
@@ -188,7 +188,7 @@
             split_store(split_ref, t, d * S, line)
         return carry
 
-    lax.fori_loop(0, T, one, 0, unroll=2)
+    lax.fori_loop(0, T, one, 0, unroll=4)
 
 
 def rim_rows_at(base, rim):
@@ -204,7 +204,7 @@
         rim_ref[rim_rows_at(base, rim)] += u[0:1] * after + u[1:2] * x + u[2:3] * before
         return carry
 
-    lax.fori_loop(0, count, one, 0, unroll=8)
+    lax.fori_loop(0, count, one, 0, unroll=16)
 
 
 def split_rims(split_ref, rim_ref, base):
@@ -213,7 +213,7 @@
             split_store(split_ref, t, e * S, rim_ref[rim_rows_at(base, t * 4 + e)])
         return carry
 
-    lax.fori_loop(0, T, split, 0, unroll=2)
+    lax.fori_loop(0, T, split, 0, unroll=4)
 
 
 def live_lines(dst_ref, dst_first, line_of, tab_ref, tab_first):
@@ -222,7 +222,7 @@
         dst_ref[dst_first + i] = jnp.where(live, line_of(i), jnp.zeros((S, 256), BF16))
         return carry
 
-    lax.fori_loop(0, 64, one, 0, unroll=8)
+    lax.fori_loop(0, 64, one, 0, unroll=16)
 
 
 def line_grads(g_ref, c_ref, mixers_ref):

time: 122 us -> 121 us (level)
  no operation moved by 1% of the time
where the time goes in v7:
time: 121 us
  Pallas kernels  50 us (41%)
  blocking collectives  36.2 us (30%)
  waiting for transfers between devices  19.4 us (16%)
  starting transfers between devices  13.5 us (11%)
    pallas_call x9, Pallas kernels, call(): pl.pallas_call(kernel, out_shape=[pltpu.HBM(o.shape, o.dtype) if m == 'h'...  50 us
    all_to_all x2, blocking collectives, exchange(): return lax.all_to_all(array, TILE, split_axis=0, concat_axis=0, tiled=True)  28 us
    all_to_all x2, waiting for transfers between devices, exchange(): return lax.all_to_all(array, TILE, split_axis=0, concat_axis=0, tiled=True)  19.4 us
    all_to_all x2, starting transfers between devices, exchange(): return lax.all_to_all(array, TILE, split_axis=0, concat_axis=0, tiled=True)  13.5 us
    all_to_all x1, blocking collectives, whole_block(): lax.all_to_all(part, 'batch', split_axis=0, concat_axis=0, tiled=True)  8.16 us
  transfers between devices with their start and end apart: 2, of which 2 were waited for; matrix products, arithmetic and copies ran while one was open for 0% of the time, Pallas kernels for 12%

profile of v7, /device:TPU:1, one launch (start us, length us, event | category | flops | bytes accessed | tf_op | source)
XLA Modules:
  0.0 120.8 jit_solution(2558144768018997595)
XLA Ops:
  0.6 4.4 %shard_map.164 = (s32[8,128]{1,0:T(8,128)}, bf16[64,32,256]{2,1,0:T(8,128)(2,1)}, bf16[64,16,256]{2,1,0:T(8,128)(2,1)}) custom-call(s32[8,256]{1,0:T(8,128)} %bitcast.29, s32[8,256]{1,0:T(8,128)} %bitcast.30, bf16[2048,256]{1,0:T(8,128)(2,1)} %bitcast.22, bf16[2048,256]{1,0:T(8,128)(2,1)} %bitcast.18, bf16[128,256]{1,0:T(8,128)(2,1)} %constant.12.clone.refs_4_.refs_7_), custom_call_target="tpu_custom_call" | custom-call | tf_op jit(solution)/shard_map/pallas_call | solution.py:758
  5.0 0.0 copy-start
  5.0 0.0 copy-start.1
  5.1 0.0 copy-start.2
  5.1 0.0 copy-start.3
  5.1 0.0 copy-start.4
  5.1 0.0 copy-start.5
  5.1 0.0 copy-start.6
  5.1 9.7 %all-to-all-start = ((bf16[32,64,256]{2,1,0:T(8,128)(2,1)}), bf16[32,64,256]{2,1,0:T(8,128)(2,1)S(1)}, u32[]{:S(2)}, u32[]{:S(2)}) async-start(bf16[32,64,256]{2,1,0:T(8,128)(2,1)} %bitcast.28), calls=%async_computation | async-start | bytes 2097152 | tf_op jit(solution)/shard_map/all_to_all | solution.py:771
  14.9 13.1 %shard_map.165 = (f32[1536,256]{1,0:T(8,128)}, bf16[2048,256]{1,0:T(8,128)(2,1)}, bf16[64,16,256]{2,1,0:T(8,128)(2,1)}, bf16[64,16,256]{2,1,0:T(8,128)(2,1)}, bf...) custom-call(s32[8,128]{1,0:T(8,128)} %get-tuple-element.34.refs_0_, ...), custom_call_target="tpu_custom_call" | custom-call | tf_op jit(solution)/shard_map/pallas_call | solution.py:758
  27.9 3.8 %all-to-all-done = bf16[32,64,256]{2,1,0:T(8,128)(2,1)S(1)} async-done(((bf16[32,64,256]{2,1,0:T(8,128)(2,1)}), bf16[32,64,256]{2,1,0:T(8,128)(2,1)S(1)}, u32[]{:S(2)}, u32[]{:S(2)}) %all-to-all-start) | async-done | bytes 1048608 | tf_op jit(solution)/shard_map/all_to_all | solution.py:771
  31.8 0.0 copy-done
  31.8 5.2 %shard_map.166 = (bf16[512,256]{1,0:T(8,128)(2,1)}, bf16[512,256]{1,0:T(8,128)(2,1)}, bf16[512,256]{1,0:T(8,128)(2,1)}, bf16[512,256]{1,0:T(8,128)(2,1)}, bf16[6...) custom-call(s32[8,128]{1,0:T(8,128)S(1)} %copy-done.4, ...), custom_call_target="tpu_custom_call" | custom-call | tf_op jit(solution)/shard_map/pallas_call | solution.py:758
  37.1 12.4 %shard_map.167 = (bf16[32,40,128]{2,1,0:T(8,128)(2,1)}, f32[2048,256]{1,0:T(8,128)}, bf16[2048,256]{1,0:T(8,128)(2,1)}, bf16[64,16,256]{2,1,0:T(8,128)(2,1)}, bf16[128,16,256]{2,1,0:T(8,128)(2,1)}) custom-call(s32[8,128]{1,0:T(8,128)} %get-tuple-element.34.refs_0_, bf16[2048,256]{1,0:T(8,128)(2,1)} %bitcast.24, bf16[2048,256]{1,0:T(8,128)(2,1)} %bitcast.20, ...), custom_call_target="tpu_custom_call" | custom-call | tf_op jit(solution)/shard_map/pallas_call | solution.py:758
  49.5 13.6 %all_to_all.25.refs_0_ = bf16[32,40,128]{2,1,0:T(8,128)(2,1)S(1)} all-to-all(bf16[32,40,128]{2,1,0:T(8,128)(2,1)} %get-tuple-element.59), channel_id=1, replica_groups=mesh['tile_0'=4,'tile_1'=4,'tile_2'=2,'batch'=4] {'tile_0','tile_1','til..., dimensions={0} | all-to-all | bytes 655360 | tf_op jit(solution)/shard_map/all_to_all | solution.py:771
  63.0 0.1 shard_map.170
  63.1 8.2 %all_to_all.26.refs_0_ = bf16[4,40,128]{2,1,0:T(8,128)(2,1)S(1)} all-to-all(bf16[4,40,128]{2,1,0:T(8,128)(2,1)S(1)} %shard_map.170), channel_id=1, replica_groups=mesh['tile_0'=4,'tile_1'=4,'tile_2'=2,'batch'=4] {'batch'}, dimensions={0} | all-to-all | bytes 81920 | tf_op jit(solution)/shard_map/all_to_all | solution.py:867
  71.3 14.5 %all_to_all.27.refs_0_ = bf16[32,40,128]{2,1,0:T(8,128)(2,1)S(1)} all-to-all(bf16[32,40,128]{2,1,0:T(8,128)(2,1)S(1)} %shard_map.171), channel_id=1, replica_groups=mesh['tile_0'=4,'tile_1'=4,'tile_2'=2,'batch'=4] {'tile_0','tile_1','til..., dimensions={0} | all-to-all | bytes 655360 | tf_op jit(solution)/shard_map/all_to_all | solution.py:771
  85.8 3.7 %all-to-all-start.1 = ((bf16[32,64,256]{2,1,0:T(8,128)(2,1)}), bf16[32,64,256]{2,1,0:T(8,128)(2,1)S(1)}, u32[]{:S(2)}, u32[]{:S(2)}) async-start(bf16[32,64,256]{2,1,0:T(8,128)(2,1)} %bitcast.7), calls=%async_computation.1 | async-start | bytes 2097152 | tf_op jit(solution)/shard_map/all_to_all | solution.py:771
  89.5 1.4 %shard_map.172 = (f32[2,256,256]{2,1,0:T(8,128)}, f32[9,2,256]{2,1,0:T(2,128)}, f32[2,256]{1,0:T(2,128)}) custom-call(bf16[32,40,128]{2,1,0:T(8,128)(2,1)S(1)} %all_to_all.27.refs_0_), custom_call_target="tpu_custom_call" | custom-call | tf_op jit(solution)/shard_map/pallas_call | solution.py:758
  91.0 15.5 %all-to-all-done.1 = bf16[32,64,256]{2,1,0:T(8,128)(2,1)S(1)} async-done(((bf16[32,64,256]{2,1,0:T(8,128)(2,1)}), bf16[32,64,256]{2,1,0:T(8,128)(2,1)S(1)}, u32[]{:S(2)}, u32[]{:S(2)}) %all-to-all-start.1) | async-done | bytes 1048608 | tf_op jit(solution)/shard_map/all_to_all | solution.py:771
  106.5 1.0 copy-done.7
  107.5 7.2 %shard_map.168 = (bf16[2048,256]{1,0:T(8,128)(2,1)}, bf16[8,128,256]{2,1,0:T(8,128)(2,1)}) custom-call(s32[8,128]{1,0:T(8,128)} %get-tuple-element.34.refs_0_, bf16[64,32,256]{2,1,0:T(8,128)(2,1)} %bitcast.26, bf16[64,16,256]{2,1,0:T(8,128)(2,1)} %get-tuple-element.53.refs_2_, bf16[128,16,256]{2,1,0:T(8,128)(2,1)} %get-tuple-element.54.refs_3_, ...), custom_call_target="tpu_custom_call" | custom-call | tf_op jit(solution)/shard_map/pallas_call | solution.py:758
  114.7 6.1 %shard_map.169 = bf16[2048,256]{1,0:T(8,128)(2,1)} custom-call(bf16[2048,256]{1,0:T(8,128)(2,1)} %get-tuple-element.57.refs_0_, bf16[8,128,256]{2,1,0:T(8,128)(2,1)} %get-tuple-element.58.refs_1_, bf16[2048,256]{1,0:T(8,128)(2,1)} %bitcast.21, f32[9,2,256]{2,1,0:T(2,128)} %bitcast.16, bf16[512,256]{1,0:T(8,128)(2,1)} %constant.14.clone.refs_6_.refs_18_.refs_4_, ...), custom_call_target="tpu_custom_call" | custom-call | tf_op jit(solution)/shard_map/pallas_call | solution.py:758
  (8 shorter events, 0.1 us)
Async XLA Ops:
  5.0 26.7 %copy-start = (bf16[2,256,256]{2,1,0:T(8,128)(2,1)S(1)}, bf16[2,256,256]{2,1,0:T(8,128)(2,1)}, u32[]{:S(2)}) copy-start(bf16[2,256,256]{2,1,0:T(8,128)(2,1)} %refs_6_.4) | copy-start | bytes 786436
  5.0 26.7 %copy-start.1 = (bf16[64,16,256]{2,1,0:T(8,128)(2,1)S(1)}, bf16[64,16,256]{2,1,0:T(8,128)(2,1)}, u32[]{:S(2)}) copy-start(bf16[64,16,256]{2,1,0:T(8,128)(2,1)} %get-tuple-element.36.refs_2_) | copy-start | bytes 1572868
  5.1 26.7 %copy-start.2 = (f32[2,9,256]{2,0,1:T(2,128)S(1)}, f32[2,9,256]{2,0,1:T(2,128)}, u32[]{:S(2)}) copy-start(f32[2,9,256]{2,0,1:T(2,128)} %param.18) | copy-start | bytes 55300
  5.1 26.7 %copy-start.3 = (bf16[64,64]{1,0:T(8,128)(2,1)S(1)}, bf16[64,64]{1,0:T(8,128)(2,1)}, u32[]{:S(2)}) copy-start(bf16[64,64]{1,0:T(8,128)(2,1)} %constant.15.clone.refs_7_.refs_20_) | copy-start | bytes 24580
  5.1 26.7 %copy-start.4 = (s32[8,128]{1,0:T(8,128)S(1)}, s32[8,128]{1,0:T(8,128)}, u32[]{:S(2)}) copy-start(s32[8,128]{1,0:T(8,128)} %get-tuple-element.34.refs_0_) | copy-start | bytes 12292
  5.1 26.7 %copy-start.5 = (f32[2,256]{1,0:T(2,128)S(1)}, f32[2,256]{1,0:T(2,128)}, u32[]{:S(2)}) copy-start(f32[2,256]{1,0:T(2,128)} %refs_8_.2) | copy-start | bytes 6148
  5.1 26.7 %copy-start.6 = (bf16[64,128]{1,0:T(8,128)(2,1)S(1)}, bf16[64,128]{1,0:T(8,128)(2,1)}, u32[]{:S(2)}) copy-start(bf16[64,128]{1,0:T(8,128)(2,1)} %constant.16.clone.refs_8_) | copy-start | bytes 49156
  5.1 26.7 %all-to-all-start = ((bf16[32,64,256]{2,1,0:T(8,128)(2,1)}), bf16[32,64,256]{2,1,0:T(8,128)(2,1)S(1)}, u32[]{:S(2)}, u32[]{:S(2)}) async-start(bf16[32,64,256]{2,1,0:T(8,128)(2,1)} %bitcast.28), calls=%async_computation | async-start | bytes 2097152 | tf_op jit(solution)/shard_map/all_to_all | solution.py:771
  85.8 20.7 %all-to-all-start.1 = ((bf16[32,64,256]{2,1,0:T(8,128)(2,1)}), bf16[32,64,256]{2,1,0:T(8,128)(2,1)S(1)}, u32[]{:S(2)}, u32[]{:S(2)}) async-start(bf16[32,64,256]{2,1,0:T(8,128)(2,1)} %bitcast.7), calls=%async_computation.1 | async-start | bytes 2097152 | tf_op jit(solution)/shard_map/all_to_all | solution.py:771
  106.5 1.0 copy-start.7
